TPU v7x, 128 devices: a whole 4x4x4 slice. The times are simulated.
128 devices in a mesh: src: 16 (over z, x_hi, core), dst: 8 (over x_lo, y).
Axes of the slice: x: 4 (x_hi: 2, x_lo: 2; x = x_hi * 2 + x_lo), y: 4, z: 4, core: 2. Of those that a mesh axis runs over, the one named last changes fastest.
Arguments:
- adjacency: float32 [20480, 20480], P('dst', 'src'), may hold values from -0.0625 to 0.0625
- features: float32 [20480, 256], P(('src', 'dst')), may hold values from -6 to 6
- layer_weights: float32 [2, 2, 256, 256], replicated, may hold values from -0.375 to 0.375
- layer_biases: float32 [2, 256], replicated, may hold values from -3 to 3
Outputs:
- result: float32 [20480, 256], P(('src', 'dst'))
All inputs are finite; a program needn't handle non-finite values.
Results may differ from a plain program's by a relative error of at most 0.0001.
Values sent between devices are 32-bit elements; how exact they have to be, the bound alone decides.
No kernel may reach another device: no remote copies, remote signals or barrier semaphores. Data moves between devices by JAX's collectives and lax.ppermute only.
A program may use at most 128 MiB of HBM per device.

v0:
```python
import itertools

import jax
import jax.numpy as jnp
from jax import lax
from jax.sharding import Mesh
from jax.sharding import PartitionSpec as P

LAYERS = 2

SRC = ("z", "xh", "core")
DST = ("xl", "y")
SIZE = {"z": 4, "xh": 2, "core": 2, "xl": 2, "y": 4}
PARTS = 8


def column_chip(block, share):
    high, middle, low = (share >> 2) & 1, (share >> 1) & 1, share & 1
    z = ((low ^ (block >> 1)) & 1) * 2 + (middle ^ (block >> 2))
    return z * 2 + (high ^ (block & 1))


def places(short):
    if short == "xl":
        return lax.axis_index("xl"), lambda at: at
    xl, y = lax.axis_index("xl"), lax.axis_index("y")
    return lax.axis_index("xh") ^ (y & 1), lambda at: ((at & 1) ^ xl) * 2 + ((at >> 1) ^ (y >> 1))


def swap(value, axis, step):
    return lax.ppermute(value, axis, [(i, i ^ step) for i in range(SIZE[axis])])


def gather(block, short, ring):
    rows, width = block.shape
    me = lax.axis_index(ring)
    in_pair, place = places(short)
    got = swap(block, short, 1)
    first = in_pair == 0
    both = jnp.stack([jnp.where(first, block, got), jnp.where(first, got, block)])
    whole = jnp.zeros((2, 4, rows, width), block.dtype)
    whole = lax.dynamic_update_slice(whole, both[:, None], (0, place(me), 0, 0))
    for step in (2, 1, 3):
        got = swap(both, ring, step)
        whole = lax.dynamic_update_slice(whole, got[:, None], (0, place(me ^ step), 0, 0))
    return whole.reshape(-1, width)


def reduce(parts, short, ring):
    parts = parts.reshape(2, 4, -1, parts.shape[1])
    me = lax.axis_index(ring)
    in_pair, place = places(short)
    share = lambda at: lax.dynamic_slice_in_dim(parts, place(at), 1, 1)[:, 0]
    got = [swap(share(me ^ step), ring, step) for step in (2, 1, 3)]
    both = share(me) + got[0] + got[1] + got[2]
    first = in_pair == 0
    sent = swap(jnp.where(first, both[1], both[0]), short, 1)
    return jnp.where(first, both[0], both[1]) + sent


def exchange_cores(value):
    return lax.ppermute(value, "core", [(0, 1), (1, 0)])


def turn(value, to_rows):
    pairs = []
    for block, core, share in itertools.product(range(PARTS), range(2), range(PARTS)):
        row = (block * 2 + core) * PARTS + share
        column = (column_chip(block, share) * 2 + core) * PARTS + block
        pairs.append((column, row) if to_rows else (row, column))
    return lax.ppermute(value, SRC + DST, pairs)


def split(value):
    high = lax.reduce_precision(value, 8, 7)
    return high.astype(jnp.bfloat16), (value - high).astype(jnp.bfloat16)


def product(left, right, dims):
    dot = lambda a, b: lax.dot_general(a, b, (dims, ((), ())), preferred_element_type=jnp.float32)
    width = right[0].shape[1]
    wide = dot(left[0], jnp.concatenate(right, axis=1))
    return wide[:, :width] + wide[:, width:] + dot(left[1], right[0])


def mix(forward, reverse, weights, bias):
    both = split(jnp.concatenate([forward, reverse], axis=1))
    stacked = split(weights.reshape(-1, weights.shape[-1]))
    return jax.nn.relu(product(both, stacked, ((1,), (0,))) + bias[None, :])


def body(adjacency, features, layer_weights, layer_biases):
    core = lax.axis_index("core")
    half = adjacency.shape[0] // 2
    row_block = features
    for layer in range(LAYERS):
        if layer == 0:
            column_block = turn(features, False)
            own = split(lax.dynamic_slice_in_dim(adjacency, core * half, half, 0))
            other = split(lax.dynamic_slice_in_dim(adjacency, (1 - core) * half, half, 0))
        source_rows = split(gather(row_block, "xl", "y"))
        own_rows = gather(column_block, "xh", "z")
        other_rows = exchange_cores(own_rows)
        other_rows = split(other_rows)
        own_rows = split(own_rows)
        sent = product(other, source_rows, ((1,), (0,)))
        got = exchange_cores(sent)
        kept = product(own, source_rows, ((1,), (0,)))
        forward = reduce(kept + got, "xh", "z")
        partial = product(own, own_rows, ((0,), (0,)))
        partial = partial + product(other, other_rows, ((0,), (0,)))
        reverse = reduce(partial, "xl", "y")
        weights, bias = layer_weights[layer], layer_biases[layer]
        turned_forward = turn(forward, True)
        row_block = mix(turned_forward, reverse, weights, bias)
        if layer + 1 < LAYERS:
            turned_reverse = turn(reverse, False)
            column_block = mix(forward, turned_reverse, weights, bias)
    return row_block


def solution(mesh):
    fine = Mesh(mesh.devices.reshape([SIZE[a] for a in SRC + DST]), SRC + DST)
    placed = (P(DST, SRC), P(SRC + DST, None), P(), P())
    return jax.shard_map(
        body, mesh=fine, in_specs=placed, out_specs=P(SRC + DST, None), check_vma=False
    )
```

profile of v0, /device:TPU:30, one launch (start us, length us, event | category | flops | bytes accessed | tf_op | source)
XLA Modules:
  0.0 163.0 jit_solution(121014892121856856)
XLA Ops:
  0.0 6.5 %collective-permute-start.10 = (f32[160,256]{1,0:T(8,128)}, f32[160,256]{1,0:T(8,128)}, u32[]{:S(2)}, u32[]{:S(2)}) collective-permute-start(f32[160,256]{1,0:T(8,128)} %param.5), channel_id=1, source_target_pairs={{0,0},{1,64},{2,32},{3,96},{4,16},{5,80},{6,48},{7,112},{8,8},{9,7... | collective-permute-start | bytes 491528 | tf_op jit(solution)/shard_map/ppermute | solution.py:71
  7.5 1.3 fusion.77
  10.5 5.8 %reduce-precision_convert_fusion = (bf16[1280,1280]{1,0:T(8,128)(2,1)S(1)}, bf16[1280,1280]{1,0:T(8,128)(2,1)S(1)}, bf16[1280,1280]{1,0:T(8,128)(2,1)S(1)}, bf16[1280,1280]{1,0:T(8,128)(2,1)S(1)}) fusion(f32[2560,1280]{1,0:T(8,128)} %param.4, s32[]{:T(128)S(6)} %select_n.161, s32[]{:T(128)S(6)} %select_n.153), kind=kLoop, calls=%fused_computation.1 | loop fusion | flops 13107200 | bytes 26214408 | tf_op jit(solution)/shard_map/convert_element_type | solution.py:76
  18.0 1.5 collective-permute-start.1
  20.1 2.0 %collective-permute-start.3 = (f32[2,160,256]{2,1,0:T(8,128)S(1)}, f32[2,160,256]{2,1,0:T(8,128)S(1)}, u32[]{:S(2)}, u32[]{:S(2)}) collective-permute-start(f32[2,160,256]{2,1,0:T(8,128)S(1)} %pad_maximum_fusion.9), channel_id=1, source_target_pairs={{0,3},{1,2},{2,1},{3,0},{4,7},{5,6},{6,5},{7,4},{8,11},{9,10},{10,... | collective-permute-start | bytes 983048 | tf_op jit(solution)/shard_map/ppermute | solution.py:31
  22.3 1.2 collective-permute-done.11
  24.5 1.1 collective-permute-start.12
  25.6 2.2 %collective-permute-start.13 = (f32[2,160,256]{2,1,0:T(8,128)S(1)}, f32[2,160,256]{2,1,0:T(8,128)S(1)}, u32[]{:S(2)}, u32[]{:S(2)}) collective-permute-start(f32[2,160,256]{2,1,0:T(8,128)S(1)} %pad_maximum_fusion.10), channel_id=1, source_target_pairs={{0,32},{32,0},{64,96},{96,64},{1,33},{33,1},{65,97},{97,65},{2,34}... | collective-permute-start | bytes 983048 | tf_op jit(solution)/shard_map/ppermute | solution.py:31
  27.9 2.2 %collective-permute-done.1 = f32[2,160,256]{2,1,0:T(8,128)S(1)} collective-permute-done((f32[2,160,256]{2,1,0:T(8,128)S(1)}, f32[2,160,256]{2,1,0:T(8,128)S(1)}, u32[]{:S(2)}, u32[]{:S(2)}) %collective-permute-start.1) | collective-permute-done | bytes 327712 | tf_op jit(solution)/shard_map/ppermute | solution.py:31
  30.2 3.2 %collective-permute-start.14 = (f32[2,160,256]{2,1,0:T(8,128)S(1)}, f32[2,160,256]{2,1,0:T(8,128)S(1)}, u32[]{:S(2)}, u32[]{:S(2)}) collective-permute-start(f32[2,160,256]{2,1,0:T(8,128)S(1)} %pad_maximum_fusion.10), channel_id=1, source_target_pairs={{0,96},{32,64},{64,32},{96,0},{1,97},{33,65},{65,33},{97,1},{2,98}... | collective-permute-start | bytes 983048 | tf_op jit(solution)/shard_map/ppermute | solution.py:31
  33.5 2.0 %collective-permute-done.3 = f32[2,160,256]{2,1,0:T(8,128)S(1)} collective-permute-done((f32[2,160,256]{2,1,0:T(8,128)S(1)}, f32[2,160,256]{2,1,0:T(8,128)S(1)}, u32[]{:S(2)}, u32[]{:S(2)}) %collective-permute-start.3) | collective-permute-done | bytes 327712 | tf_op jit(solution)/shard_map/ppermute | solution.py:31
  35.7 1.9 %fusion.36 = f32[1280,512]{1,0:T(8,128)S(1)} fusion(bf16[1280,1280]{1,0:T(8,128)(2,1)S(1)} %get-tuple-element.5, bf16[1280,256]{1,0:T(8,128)(2,1)S(1)} %get-tuple-element.24, bf16[1280,256]{1,0:T(8,128)(2,1)S(1)} %get-tuple-element.25), kind=kOutput, calls=%fused_computation.73 | convolution fusion | flops 1680343040 | bytes 7208960 | tf_op jit(solution)/shard_map/dot_general | solution.py:80
  38.7 1.9 %fusion.37 = f32[1280,512]{1,0:T(8,128)S(1)} fusion(bf16[1280,1280]{1,0:T(8,128)(2,1)S(1)} %get-tuple-element.8, bf16[1280,256]{1,0:T(8,128)(2,1)S(1)} %get-tuple-element.24, bf16[1280,256]{1,0:T(8,128)(2,1)S(1)} %get-tuple-element.25), kind=kOutput, calls=%fused_computation.74 | convolution fusion | flops 1680343040 | bytes 7208960 | tf_op jit(solution)/shard_map/dot_general | solution.py:80
  41.7 1.9 %fusion.12 = f32[1280,512]{1,0:T(8,128)S(1)} fusion(bf16[1280,1280]{1,0:T(8,128)(2,1)S(1)} %get-tuple-element.8, bf16[1280,256]{1,0:T(8,128)(2,1)S(1)} %get-tuple-element.31, bf16[1280,256]{1,0:T(8,128)(2,1)S(1)} %get-tuple-element.32), kind=kOutput, calls=%fused_computation.45 | convolution fusion | flops 1680343040 | bytes 7208960 | tf_op jit(solution)/shard_map/dot_general | solution.py:80
  43.6 1.1 convolution_add_fusion.5
  44.7 1.1 fusion.2
  46.0 1.9 %collective-permute-start.7 = (f32[2,160,256]{2,1,0:T(8,128)S(1)}, f32[2,160,256]{2,1,0:T(8,128)S(1)}, u32[]{:S(2)}, u32[]{:S(2)}) collective-permute-start(f32[2,160,256]{2,1,0:T(8,128)S(1)} %get-tuple-element.22), channel_id=1, source_target_pairs={{0,96},{32,64},{64,32},{96,0},{1,97},{33,65},{65,33},{97,1},{2,98}... | collective-permute-start | bytes 983048 | tf_op jit(solution)/shard_map/ppermute | solution.py:31
  48.3 2.4 %collective-permute-start.5 = (f32[2,160,256]{2,1,0:T(8,128)S(1)}, f32[2,160,256]{2,1,0:T(8,128)S(1)}, u32[]{:S(2)}, u32[]{:S(2)}) collective-permute-start(f32[2,160,256]{2,1,0:T(8,128)S(1)} %get-tuple-element.21), channel_id=1, source_target_pairs={{0,64},{32,96},{64,0},{96,32},{1,65},{33,97},{65,1},{97,33},{2,66}... | collective-permute-start | bytes 983048 | tf_op jit(solution)/shard_map/ppermute | solution.py:31
  50.9 1.9 %fusion.16 = f32[1280,512]{1,0:T(8,128)S(1)} fusion(bf16[1280,1280]{1,0:T(8,128)(2,1)S(1)} %get-tuple-element.5, bf16[1280,256]{1,0:T(8,128)(2,1)S(1)} %get-tuple-element.29, bf16[1280,256]{1,0:T(8,128)(2,1)S(1)} %get-tuple-element.30), kind=kOutput, calls=%fused_computation.49 | convolution fusion | flops 1680343040 | bytes 7208960 | tf_op jit(solution)/shard_map/dot_general | solution.py:80
  52.9 1.1 fusion.3
  54.1 1.3 collective-permute-start.18
  55.5 1.9 %collective-permute-done.7 = f32[2,160,256]{2,1,0:T(8,128)S(1)} collective-permute-done((f32[2,160,256]{2,1,0:T(8,128)S(1)}, f32[2,160,256]{2,1,0:T(8,128)S(1)}, u32[]{:S(2)}, u32[]{:S(2)}) %collective-permute-start.7) | collective-permute-done | bytes 327712 | tf_op jit(solution)/shard_map/ppermute | solution.py:31
  57.3 1.6 collective-permute-start.16
  58.9 6.6 %collective-permute-done.5 = f32[2,160,256]{2,1,0:T(8,128)S(1)} collective-permute-done((f32[2,160,256]{2,1,0:T(8,128)S(1)}, f32[2,160,256]{2,1,0:T(8,128)S(1)}, u32[]{:S(2)}, u32[]{:S(2)}) %collective-permute-start.5) | collective-permute-done | bytes 327712 | tf_op jit(solution)/shard_map/ppermute | solution.py:31
  65.7 2.3 %collective-permute-start.8 = (f32[160,256]{1,0:T(8,128)S(1)}, f32[160,256]{1,0:T(8,128)S(1)}, u32[]{:S(2)}, u32[]{:S(2)}) collective-permute-start(f32[160,256]{1,0:T(8,128)S(1)} %select_bitcast_fusion.9), channel_id=1, source_target_pairs={{0,16},{16,0},{1,17},{17,1},{2,18},{18,2},{3,19},{19,3},{4,20},{20... | collective-permute-start | bytes 491528 | tf_op jit(solution)/shard_map/ppermute | solution.py:31
  68.0 4.9 %collective-permute-done.16 = f32[2,160,256]{2,1,0:T(8,128)S(1)} collective-permute-done((f32[2,160,256]{2,1,0:T(8,128)S(1)}, f32[2,160,256]{2,1,0:T(8,128)S(1)}, u32[]{:S(2)}, u32[]{:S(2)}) %collective-permute-start.16) | collective-permute-done | bytes 327712 | tf_op jit(solution)/shard_map/ppermute | solution.py:31
  73.0 1.2 collective-permute-start.19
  74.2 3.6 %collective-permute-start.9 = (f32[160,256]{1,0:T(8,128)S(1)}, f32[160,256]{1,0:T(8,128)S(1)}, u32[]{:S(2)}, u32[]{:S(2)}) collective-permute-start(f32[160,256]{1,0:T(8,128)S(1)} %bitcast_add_fusion.7), channel_id=1, source_target_pairs={{0,0},{64,1},{32,2},{96,3},{16,4},{80,5},{48,6},{112,7},{8,8},{72,... | collective-permute-start | bytes 491528 | tf_op jit(solution)/shard_map/ppermute | solution.py:71
  78.4 7.4 %collective-permute-start.30 = (f32[160,256]{1,0:T(8,128)S(1)}, f32[160,256]{1,0:T(8,128)S(1)}, u32[]{:S(2)}, u32[]{:S(2)}) collective-permute-start(f32[160,256]{1,0:T(8,128)S(1)} %bitcast_add_fusion.6), channel_id=1, source_target_pairs={{0,0},{1,64},{2,32},{3,96},{4,16},{5,80},{6,48},{7,112},{8,8},{9,7... | collective-permute-start | bytes 491528 | tf_op jit(solution)/shard_map/ppermute | solution.py:71
  85.8 6.3 %collective-permute-done.9 = f32[160,256]{1,0:T(8,128)S(1)} collective-permute-done((f32[160,256]{1,0:T(8,128)S(1)}, f32[160,256]{1,0:T(8,128)S(1)}, u32[]{:S(2)}, u32[]{:S(2)}) %collective-permute-start.9) | collective-permute-done | bytes 163872 | tf_op jit(solution)/shard_map/ppermute | solution.py:71
  93.8 4.3 %collective-permute-done.20 = f32[160,256]{1,0:T(8,128)S(1)} collective-permute-done((f32[160,256]{1,0:T(8,128)S(1)}, f32[160,256]{1,0:T(8,128)S(1)}, u32[]{:S(2)}, u32[]{:S(2)}) %collective-permute-start.20) | collective-permute-done | bytes 163872 | tf_op jit(solution)/shard_map/ppermute | solution.py:31
  98.6 3.7 %collective-permute-start.23 = (f32[2,160,256]{2,1,0:T(8,128)S(1)}, f32[2,160,256]{2,1,0:T(8,128)S(1)}, u32[]{:S(2)}, u32[]{:S(2)}) collective-permute-start(f32[2,160,256]{2,1,0:T(8,128)S(1)} %pad_maximum_fusion.12), channel_id=1, source_target_pairs={{0,3},{1,2},{2,1},{3,0},{4,7},{5,6},{6,5},{7,4},{8,11},{9,10},{10,... | collective-permute-start | bytes 983048 | tf_op jit(solution)/shard_map/ppermute | solution.py:31
  103.1 5.2 %collective-permute-done.21 = f32[2,160,256]{2,1,0:T(8,128)S(1)} collective-permute-done((f32[2,160,256]{2,1,0:T(8,128)S(1)}, f32[2,160,256]{2,1,0:T(8,128)S(1)}, u32[]{:S(2)}, u32[]{:S(2)}) %collective-permute-start.21) | collective-permute-done | bytes 327712 | tf_op jit(solution)/shard_map/ppermute | solution.py:31
  109.4 2.4 %collective-permute-done.23 = f32[2,160,256]{2,1,0:T(8,128)S(1)} collective-permute-done((f32[2,160,256]{2,1,0:T(8,128)S(1)}, f32[2,160,256]{2,1,0:T(8,128)S(1)}, u32[]{:S(2)}, u32[]{:S(2)}) %collective-permute-start.23) | collective-permute-done | bytes 327712 | tf_op jit(solution)/shard_map/ppermute | solution.py:31
  112.0 1.9 %fusion.34 = f32[1280,512]{1,0:T(8,128)S(1)} fusion(bf16[1280,1280]{1,0:T(8,128)(2,1)S(1)} %get-tuple-element.5, bf16[1280,256]{1,0:T(8,128)(2,1)S(1)} %get-tuple-element.12, bf16[1280,256]{1,0:T(8,128)(2,1)S(1)} %get-tuple-element.13), kind=kOutput, calls=%fused_computation.71 | convolution fusion | flops 1680343040 | bytes 7208960 | tf_op jit(solution)/shard_map/dot_general | solution.py:80
  113.8 1.9 %fusion.35 = f32[1280,512]{1,0:T(8,128)S(1)} fusion(bf16[1280,1280]{1,0:T(8,128)(2,1)S(1)} %get-tuple-element.8, bf16[1280,256]{1,0:T(8,128)(2,1)S(1)} %get-tuple-element.12, bf16[1280,256]{1,0:T(8,128)(2,1)S(1)} %get-tuple-element.13), kind=kOutput, calls=%fused_computation.72 | convolution fusion | flops 1680343040 | bytes 7208960 | tf_op jit(solution)/shard_map/dot_general | solution.py:80
  117.8 1.9 %fusion.20 = f32[1280,512]{1,0:T(8,128)S(1)} fusion(bf16[1280,1280]{1,0:T(8,128)(2,1)S(1)} %get-tuple-element.8, bf16[1280,256]{1,0:T(8,128)(2,1)S(1)} %get-tuple-element.19, bf16[1280,256]{1,0:T(8,128)(2,1)S(1)} %get-tuple-element.20), kind=kOutput, calls=%fused_computation.54 | convolution fusion | flops 1680343040 | bytes 7208960 | tf_op jit(solution)/shard_map/dot_general | solution.py:80
  122.1 1.3 collective-permute-start.26
  123.4 3.4 %collective-permute-start.25 = (f32[2,160,256]{2,1,0:T(8,128)S(1)}, f32[2,160,256]{2,1,0:T(8,128)S(1)}, u32[]{:S(2)}, u32[]{:S(2)}) collective-permute-start(f32[2,160,256]{2,1,0:T(8,128)S(1)} %get-tuple-element.9), channel_id=1, source_target_pairs={{0,64},{32,96},{64,0},{96,32},{1,65},{33,97},{65,1},{97,33},{2,66}... | collective-permute-start | bytes 983048 | tf_op jit(solution)/shard_map/ppermute | solution.py:31
  127.0 1.9 %fusion.24 = f32[1280,512]{1,0:T(8,128)S(1)} fusion(bf16[1280,1280]{1,0:T(8,128)(2,1)S(1)} %get-tuple-element.5, bf16[1280,256]{1,0:T(8,128)(2,1)S(1)} %get-tuple-element.17, bf16[1280,256]{1,0:T(8,128)(2,1)S(1)} %get-tuple-element.18), kind=kOutput, calls=%fused_computation.58 | convolution fusion | flops 1680343040 | bytes 7208960 | tf_op jit(solution)/shard_map/dot_general | solution.py:80
  131.4 1.5 collective-permute-done.27
  133.0 1.9 %collective-permute-start.36 = (f32[2,160,256]{2,1,0:T(8,128)S(1)}, f32[2,160,256]{2,1,0:T(8,128)S(1)}, u32[]{:S(2)}, u32[]{:S(2)}) collective-permute-start(f32[2,160,256]{2,1,0:T(8,128)S(1)} %get-tuple-element.14), channel_id=1, source_target_pairs={{0,2},{1,3},{2,0},{3,1},{4,6},{5,7},{6,4},{7,5},{8,10},{9,11},{10,... | collective-permute-start | bytes 983048 | tf_op jit(solution)/shard_map/ppermute | solution.py:31
  134.9 6.3 %collective-permute-done.25 = f32[2,160,256]{2,1,0:T(8,128)S(1)} collective-permute-done((f32[2,160,256]{2,1,0:T(8,128)S(1)}, f32[2,160,256]{2,1,0:T(8,128)S(1)}, u32[]{:S(2)}, u32[]{:S(2)}) %collective-permute-start.25) | collective-permute-done | bytes 327712 | tf_op jit(solution)/shard_map/ppermute | solution.py:31
  141.3 1.6 collective-permute-start.28
  142.9 5.5 %collective-permute-done.36 = f32[2,160,256]{2,1,0:T(8,128)S(1)} collective-permute-done((f32[2,160,256]{2,1,0:T(8,128)S(1)}, f32[2,160,256]{2,1,0:T(8,128)S(1)}, u32[]{:S(2)}, u32[]{:S(2)}) %collective-permute-start.36) | collective-permute-done | bytes 327712 | tf_op jit(solution)/shard_map/ppermute | solution.py:31
  148.9 3.5 %collective-permute-start.29 = (f32[160,256]{1,0:T(8,128)S(1)}, f32[160,256]{1,0:T(8,128)S(1)}, u32[]{:S(2)}, u32[]{:S(2)}) collective-permute-start(f32[160,256]{1,0:T(8,128)S(1)} %bitcast_add_fusion.5), channel_id=1, source_target_pairs={{0,0},{64,1},{32,2},{96,3},{16,4},{80,5},{48,6},{112,7},{8,8},{72,... | collective-permute-start | bytes 491528 | tf_op jit(solution)/shard_map/ppermute | solution.py:71
  152.4 1.5 collective-permute-done.39
  154.0 7.9 %collective-permute-done.29 = f32[160,256]{1,0:T(8,128)S(1)} collective-permute-done((f32[160,256]{1,0:T(8,128)S(1)}, f32[160,256]{1,0:T(8,128)S(1)}, u32[]{:S(2)}, u32[]{:S(2)}) %collective-permute-start.29) | collective-permute-done | bytes 163872 | tf_op jit(solution)/shard_map/ppermute | solution.py:71
  (119 shorter events, 23.3 us)
Async XLA Ops:
  0.0 16.3 %collective-permute-start.10 = (f32[160,256]{1,0:T(8,128)}, f32[160,256]{1,0:T(8,128)}, u32[]{:S(2)}, u32[]{:S(2)}) collective-permute-start(f32[160,256]{1,0:T(8,128)} %param.5), channel_id=1, source_target_pairs={{0,0},{1,64},{2,32},{3,96},{4,16},{5,80},{6,48},{7,112},{8,8},{9,7... | collective-permute-start | bytes 491528 | tf_op jit(solution)/shard_map/ppermute | solution.py:71
  6.5 10.4 %collective-permute-start = (f32[160,256]{1,0:T(8,128)}, f32[160,256]{1,0:T(8,128)}, u32[]{:S(2)}, u32[]{:S(2)}) collective-permute-start(f32[160,256]{1,0:T(8,128)} %param.5), channel_id=1, source_target_pairs={{0,4},{4,0},{1,5},{5,1},{2,6},{6,2},{3,7},{7,3},{8,12},{12,8},{9,1... | collective-permute-start | bytes 491528 | tf_op jit(solution)/shard_map/ppermute | solution.py:31
  10.5 5.8 %copy-start.4 = (f32[2,256]{1,0:T(2,128)S(1)}, f32[2,256]{1,0:T(2,128)}, u32[]{:S(2)}) copy-start(f32[2,256]{1,0:T(2,128)} %param.7) | copy-start | bytes 6148
  10.5 6.5 %copy-start.3 = (f32[160,256]{1,0:T(8,128)S(1)}, f32[160,256]{1,0:T(8,128)}, u32[]{:S(2)}) copy-start(f32[160,256]{1,0:T(8,128)} %param.5) | copy-start | bytes 491524
  16.3 7.2 %collective-permute-start.11 = (f32[160,256]{1,0:T(8,128)}, f32[160,256]{1,0:T(8,128)S(1)}, u32[]{:S(2)}, u32[]{:S(2)}) collective-permute-start(f32[160,256]{1,0:T(8,128)} %collective-permute-done.10), channel_id=1, source_target_pairs={{0,16},{16,0},{1,17},{17,1},{2,18},{18,2},{3,19},{19,3},{4,20},{20... | collective-permute-start | bytes 491528 | tf_op jit(solution)/shard_map/ppermute | solution.py:31
  18.0 12.2 %collective-permute-start.1 = (f32[2,160,256]{2,1,0:T(8,128)S(1)}, f32[2,160,256]{2,1,0:T(8,128)S(1)}, u32[]{:S(2)}, u32[]{:S(2)}) collective-permute-start(f32[2,160,256]{2,1,0:T(8,128)S(1)} %pad_maximum_fusion.9), channel_id=1, source_target_pairs={{0,2},{1,3},{2,0},{3,1},{4,6},{5,7},{6,4},{7,5},{8,10},{9,11},{10,... | collective-permute-start | bytes 983048 | tf_op jit(solution)/shard_map/ppermute | solution.py:31
  19.5 14.0 %collective-permute-start.2 = (f32[2,160,256]{2,1,0:T(8,128)S(1)}, f32[2,160,256]{2,1,0:T(8,128)S(1)}, u32[]{:S(2)}, u32[]{:S(2)}) collective-permute-start(f32[2,160,256]{2,1,0:T(8,128)S(1)} %pad_maximum_fusion.9), channel_id=1, source_target_pairs={{0,1},{1,0},{2,3},{3,2},{4,5},{5,4},{6,7},{7,6},{8,9},{9,8},{10,11... | collective-permute-start | bytes 983048 | tf_op jit(solution)/shard_map/ppermute | solution.py:31
  20.1 15.3 %collective-permute-start.3 = (f32[2,160,256]{2,1,0:T(8,128)S(1)}, f32[2,160,256]{2,1,0:T(8,128)S(1)}, u32[]{:S(2)}, u32[]{:S(2)}) collective-permute-start(f32[2,160,256]{2,1,0:T(8,128)S(1)} %pad_maximum_fusion.9), channel_id=1, source_target_pairs={{0,3},{1,2},{2,1},{3,0},{4,7},{5,6},{6,5},{7,4},{8,11},{9,10},{10,... | collective-permute-start | bytes 983048 | tf_op jit(solution)/shard_map/ppermute | solution.py:31
  24.5 16.1 %collective-permute-start.12 = (f32[2,160,256]{2,1,0:T(8,128)S(1)}, f32[2,160,256]{2,1,0:T(8,128)S(1)}, u32[]{:S(2)}, u32[]{:S(2)}) collective-permute-start(f32[2,160,256]{2,1,0:T(8,128)S(1)} %pad_maximum_fusion.10), channel_id=1, source_target_pairs={{0,64},{32,96},{64,0},{96,32},{1,65},{33,97},{65,1},{97,33},{2,66}... | collective-permute-start | bytes 983048 | tf_op jit(solution)/shard_map/ppermute | solution.py:31
  25.6 15.0 %collective-permute-start.13 = (f32[2,160,256]{2,1,0:T(8,128)S(1)}, f32[2,160,256]{2,1,0:T(8,128)S(1)}, u32[]{:S(2)}, u32[]{:S(2)}) collective-permute-start(f32[2,160,256]{2,1,0:T(8,128)S(1)} %pad_maximum_fusion.10), channel_id=1, source_target_pairs={{0,32},{32,0},{64,96},{96,64},{1,33},{33,1},{65,97},{97,65},{2,34}... | collective-permute-start | bytes 983048 | tf_op jit(solution)/shard_map/ppermute | solution.py:31
  30.2 10.9 %collective-permute-start.14 = (f32[2,160,256]{2,1,0:T(8,128)S(1)}, f32[2,160,256]{2,1,0:T(8,128)S(1)}, u32[]{:S(2)}, u32[]{:S(2)}) collective-permute-start(f32[2,160,256]{2,1,0:T(8,128)S(1)} %pad_maximum_fusion.10), channel_id=1, source_target_pairs={{0,96},{32,64},{64,32},{96,0},{1,97},{33,65},{65,33},{97,1},{2,98}... | collective-permute-start | bytes 983048 | tf_op jit(solution)/shard_map/ppermute | solution.py:31
  38.6 6.1 %collective-permute-start.4 = (f32[1280,256]{1,0:T(8,128)S(1)}, f32[1280,256]{1,0:T(8,128)S(1)}, u32[]{:S(2)}, u32[]{:S(2)}) collective-permute-start(f32[1280,256]{1,0:T(8,128)S(1)} %convolution_add_fusion.6), channel_id=1, source_target_pairs={{0,8},{8,0},{1,9},{9,1},{2,10},{10,2},{3,11},{11,3},{4,12},{12,4},... | collective-permute-start | bytes 3932168 | tf_op jit(solution)/shard_map/ppermute | solution.py:62
  41.1 9.6 %collective-permute-start.15 = (f32[1280,256]{1,0:T(8,128)S(1)}, f32[1280,256]{1,0:T(8,128)S(1)}, u32[]{:S(2)}, u32[]{:S(2)}) collective-permute-start(f32[1280,256]{1,0:T(8,128)S(1)} %bitcast.200), channel_id=1, source_target_pairs={{0,8},{8,0},{1,9},{9,1},{2,10},{10,2},{3,11},{11,3},{4,12},{12,4},... | collective-permute-start | bytes 3932168 | tf_op jit(solution)/shard_map/ppermute | solution.py:62
  46.0 11.4 %collective-permute-start.7 = (f32[2,160,256]{2,1,0:T(8,128)S(1)}, f32[2,160,256]{2,1,0:T(8,128)S(1)}, u32[]{:S(2)}, u32[]{:S(2)}) collective-permute-start(f32[2,160,256]{2,1,0:T(8,128)S(1)} %get-tuple-element.22), channel_id=1, source_target_pairs={{0,96},{32,64},{64,32},{96,0},{1,97},{33,65},{65,33},{97,1},{2,98}... | collective-permute-start | bytes 983048 | tf_op jit(solution)/shard_map/ppermute | solution.py:31
  47.8 11.1 %collective-permute-start.6 = (f32[2,160,256]{2,1,0:T(8,128)S(1)}, f32[2,160,256]{2,1,0:T(8,128)S(1)}, u32[]{:S(2)}, u32[]{:S(2)}) collective-permute-start(f32[2,160,256]{2,1,0:T(8,128)S(1)} %get-tuple-element.23), channel_id=1, source_target_pairs={{0,32},{32,0},{64,96},{96,64},{1,33},{33,1},{65,97},{97,65},{2,34}... | collective-permute-start | bytes 983048 | tf_op jit(solution)/shard_map/ppermute | solution.py:31
  48.3 17.2 %collective-permute-start.5 = (f32[2,160,256]{2,1,0:T(8,128)S(1)}, f32[2,160,256]{2,1,0:T(8,128)S(1)}, u32[]{:S(2)}, u32[]{:S(2)}) collective-permute-start(f32[2,160,256]{2,1,0:T(8,128)S(1)} %get-tuple-element.21), channel_id=1, source_target_pairs={{0,64},{32,96},{64,0},{96,32},{1,65},{33,97},{65,1},{97,33},{2,66}... | collective-permute-start | bytes 983048 | tf_op jit(solution)/shard_map/ppermute | solution.py:31
  54.1 13.8 %collective-permute-start.18 = (f32[2,160,256]{2,1,0:T(8,128)S(1)}, f32[2,160,256]{2,1,0:T(8,128)S(1)}, u32[]{:S(2)}, u32[]{:S(2)}) collective-permute-start(f32[2,160,256]{2,1,0:T(8,128)S(1)} %get-tuple-element.27), channel_id=1, source_target_pairs={{0,3},{1,2},{2,1},{3,0},{4,7},{5,6},{6,5},{7,4},{8,11},{9,10},{10,... | collective-permute-start | bytes 983048 | tf_op jit(solution)/shard_map/ppermute | solution.py:31
  55.5 12.5 %collective-permute-start.17 = (f32[2,160,256]{2,1,0:T(8,128)S(1)}, f32[2,160,256]{2,1,0:T(8,128)S(1)}, u32[]{:S(2)}, u32[]{:S(2)}) collective-permute-start(f32[2,160,256]{2,1,0:T(8,128)S(1)} %get-tuple-element.28), channel_id=1, source_target_pairs={{0,1},{1,0},{2,3},{3,2},{4,5},{5,4},{6,7},{7,6},{8,9},{9,8},{10,11... | collective-permute-start | bytes 983048 | tf_op jit(solution)/shard_map/ppermute | solution.py:31
  57.3 15.5 %collective-permute-start.16 = (f32[2,160,256]{2,1,0:T(8,128)S(1)}, f32[2,160,256]{2,1,0:T(8,128)S(1)}, u32[]{:S(2)}, u32[]{:S(2)}) collective-permute-start(f32[2,160,256]{2,1,0:T(8,128)S(1)} %get-tuple-element.26), channel_id=1, source_target_pairs={{0,2},{1,3},{2,0},{3,1},{4,6},{5,7},{6,4},{7,5},{8,10},{9,11},{10,... | collective-permute-start | bytes 983048 | tf_op jit(solution)/shard_map/ppermute | solution.py:31
  65.7 8.5 %collective-permute-start.8 = (f32[160,256]{1,0:T(8,128)S(1)}, f32[160,256]{1,0:T(8,128)S(1)}, u32[]{:S(2)}, u32[]{:S(2)}) collective-permute-start(f32[160,256]{1,0:T(8,128)S(1)} %select_bitcast_fusion.9), channel_id=1, source_target_pairs={{0,16},{16,0},{1,17},{17,1},{2,18},{18,2},{3,19},{19,3},{4,20},{20... | collective-permute-start | bytes 491528 | tf_op jit(solution)/shard_map/ppermute | solution.py:31
  73.0 19.2 %copy-start.2 = (bf16[512,256]{1,0:T(8,128)(2,1)S(1)}, bf16[512,256]{1,0:T(8,128)(2,1)}, u32[]{:S(2)}) copy-start(bf16[512,256]{1,0:T(8,128)(2,1)} %get-tuple-element.37) | copy-start | bytes 786436
  73.0 5.4 %collective-permute-start.19 = (f32[160,256]{1,0:T(8,128)S(1)}, f32[160,256]{1,0:T(8,128)S(1)}, u32[]{:S(2)}, u32[]{:S(2)}) collective-permute-start(f32[160,256]{1,0:T(8,128)S(1)} %select_bitcast_fusion.6), channel_id=1, source_target_pairs={{0,4},{4,0},{1,5},{5,1},{2,6},{6,2},{3,7},{7,3},{8,12},{12,8},{9,1... | collective-permute-start | bytes 491528 | tf_op jit(solution)/shard_map/ppermute | solution.py:31
  74.2 17.9 %collective-permute-start.9 = (f32[160,256]{1,0:T(8,128)S(1)}, f32[160,256]{1,0:T(8,128)S(1)}, u32[]{:S(2)}, u32[]{:S(2)}) collective-permute-start(f32[160,256]{1,0:T(8,128)S(1)} %bitcast_add_fusion.7), channel_id=1, source_target_pairs={{0,0},{64,1},{32,2},{96,3},{16,4},{80,5},{48,6},{112,7},{8,8},{72,... | collective-permute-start | bytes 491528 | tf_op jit(solution)/shard_map/ppermute | solution.py:71
  78.4 14.3 %collective-permute-start.30 = (f32[160,256]{1,0:T(8,128)S(1)}, f32[160,256]{1,0:T(8,128)S(1)}, u32[]{:S(2)}, u32[]{:S(2)}) collective-permute-start(f32[160,256]{1,0:T(8,128)S(1)} %bitcast_add_fusion.6), channel_id=1, source_target_pairs={{0,0},{1,64},{2,32},{3,96},{4,16},{5,80},{6,48},{7,112},{8,8},{9,7... | collective-permute-start | bytes 491528 | tf_op jit(solution)/shard_map/ppermute | solution.py:71
  92.6 5.4 %collective-permute-start.20 = (f32[160,256]{1,0:T(8,128)S(1)}, f32[160,256]{1,0:T(8,128)S(1)}, u32[]{:S(2)}, u32[]{:S(2)}) collective-permute-start(f32[160,256]{1,0:T(8,128)S(1)} %fusion.33), channel_id=1, source_target_pairs={{0,4},{4,0},{1,5},{5,1},{2,6},{6,2},{3,7},{7,3},{8,12},{12,8},{9,1... | collective-permute-start | bytes 491528 | tf_op jit(solution)/shard_map/ppermute | solution.py:31
  93.2 9.2 %collective-permute-start.31 = (f32[160,256]{1,0:T(8,128)S(1)}, f32[160,256]{1,0:T(8,128)S(1)}, u32[]{:S(2)}, u32[]{:S(2)}) collective-permute-start(f32[160,256]{1,0:T(8,128)S(1)} %fusion.31), channel_id=1, source_target_pairs={{0,16},{16,0},{1,17},{17,1},{2,18},{18,2},{3,19},{19,3},{4,20},{20... | collective-permute-start | bytes 491528 | tf_op jit(solution)/shard_map/ppermute | solution.py:31
  98.1 10.3 %collective-permute-start.21 = (f32[2,160,256]{2,1,0:T(8,128)S(1)}, f32[2,160,256]{2,1,0:T(8,128)S(1)}, u32[]{:S(2)}, u32[]{:S(2)}) collective-permute-start(f32[2,160,256]{2,1,0:T(8,128)S(1)} %pad_maximum_fusion.12), channel_id=1, source_target_pairs={{0,2},{1,3},{2,0},{3,1},{4,6},{5,7},{6,4},{7,5},{8,10},{9,11},{10,... | collective-permute-start | bytes 983048 | tf_op jit(solution)/shard_map/ppermute | solution.py:31
  98.6 10.7 %collective-permute-start.22 = (f32[2,160,256]{2,1,0:T(8,128)S(1)}, f32[2,160,256]{2,1,0:T(8,128)S(1)}, u32[]{:S(2)}, u32[]{:S(2)}) collective-permute-start(f32[2,160,256]{2,1,0:T(8,128)S(1)} %pad_maximum_fusion.12), channel_id=1, source_target_pairs={{0,1},{1,0},{2,3},{3,2},{4,5},{5,4},{6,7},{7,6},{8,9},{9,8},{10,11... | collective-permute-start | bytes 983048 | tf_op jit(solution)/shard_map/ppermute | solution.py:31
  98.6 13.1 %collective-permute-start.23 = (f32[2,160,256]{2,1,0:T(8,128)S(1)}, f32[2,160,256]{2,1,0:T(8,128)S(1)}, u32[]{:S(2)}, u32[]{:S(2)}) collective-permute-start(f32[2,160,256]{2,1,0:T(8,128)S(1)} %pad_maximum_fusion.12), channel_id=1, source_target_pairs={{0,3},{1,2},{2,1},{3,0},{4,7},{5,6},{6,5},{7,4},{8,11},{9,10},{10,... | collective-permute-start | bytes 983048 | tf_op jit(solution)/shard_map/ppermute | solution.py:31
  102.5 14.4 %collective-permute-start.32 = (f32[2,160,256]{2,1,0:T(8,128)S(1)}, f32[2,160,256]{2,1,0:T(8,128)S(1)}, u32[]{:S(2)}, u32[]{:S(2)}) collective-permute-start(f32[2,160,256]{2,1,0:T(8,128)S(1)} %pad_maximum_fusion.14), channel_id=1, source_target_pairs={{0,64},{32,96},{64,0},{96,32},{1,65},{33,97},{65,1},{97,33},{2,66}... | collective-permute-start | bytes 983048 | tf_op jit(solution)/shard_map/ppermute | solution.py:31
  102.6 14.4 %collective-permute-start.33 = (f32[2,160,256]{2,1,0:T(8,128)S(1)}, f32[2,160,256]{2,1,0:T(8,128)S(1)}, u32[]{:S(2)}, u32[]{:S(2)}) collective-permute-start(f32[2,160,256]{2,1,0:T(8,128)S(1)} %pad_maximum_fusion.14), channel_id=1, source_target_pairs={{0,32},{32,0},{64,96},{96,64},{1,33},{33,1},{65,97},{97,65},{2,34}... | collective-permute-start | bytes 983048 | tf_op jit(solution)/shard_map/ppermute | solution.py:31
  108.4 8.6 %collective-permute-start.34 = (f32[2,160,256]{2,1,0:T(8,128)S(1)}, f32[2,160,256]{2,1,0:T(8,128)S(1)}, u32[]{:S(2)}, u32[]{:S(2)}) collective-permute-start(f32[2,160,256]{2,1,0:T(8,128)S(1)} %pad_maximum_fusion.14), channel_id=1, source_target_pairs={{0,96},{32,64},{64,32},{96,0},{1,97},{33,65},{65,33},{97,1},{2,98}... | collective-permute-start | bytes 983048 | tf_op jit(solution)/shard_map/ppermute | solution.py:31
  116.8 4.0 %collective-permute-start.24 = (f32[1280,256]{1,0:T(8,128)S(1)}, f32[1280,256]{1,0:T(8,128)S(1)}, u32[]{:S(2)}, u32[]{:S(2)}) collective-permute-start(f32[1280,256]{1,0:T(8,128)S(1)} %convolution_add_fusion.2), channel_id=1, source_target_pairs={{0,8},{8,0},{1,9},{9,1},{2,10},{10,2},{3,11},{11,3},{4,12},{12,4},... | collective-permute-start | bytes 3932168 | tf_op jit(solution)/shard_map/ppermute | solution.py:62
  117.0 9.7 %collective-permute-start.35 = (f32[1280,256]{1,0:T(8,128)S(1)}, f32[1280,256]{1,0:T(8,128)S(1)}, u32[]{:S(2)}, u32[]{:S(2)}) collective-permute-start(f32[1280,256]{1,0:T(8,128)S(1)} %bitcast.199), channel_id=1, source_target_pairs={{0,8},{8,0},{1,9},{9,1},{2,10},{10,2},{3,11},{11,3},{4,12},{12,4},... | collective-permute-start | bytes 3932168 | tf_op jit(solution)/shard_map/ppermute | solution.py:62
  122.0 11.0 %collective-permute-start.27 = (f32[2,160,256]{2,1,0:T(8,128)S(1)}, f32[2,160,256]{2,1,0:T(8,128)S(1)}, u32[]{:S(2)}, u32[]{:S(2)}) collective-permute-start(f32[2,160,256]{2,1,0:T(8,128)S(1)} %get-tuple-element.10), channel_id=1, source_target_pairs={{0,96},{32,64},{64,32},{96,0},{1,97},{33,65},{65,33},{97,1},{2,98}... | collective-permute-start | bytes 983048 | tf_op jit(solution)/shard_map/ppermute | solution.py:31
  122.1 12.8 %collective-permute-start.26 = (f32[2,160,256]{2,1,0:T(8,128)S(1)}, f32[2,160,256]{2,1,0:T(8,128)S(1)}, u32[]{:S(2)}, u32[]{:S(2)}) collective-permute-start(f32[2,160,256]{2,1,0:T(8,128)S(1)} %get-tuple-element.11), channel_id=1, source_target_pairs={{0,32},{32,0},{64,96},{96,64},{1,33},{33,1},{65,97},{97,65},{2,34}... | collective-permute-start | bytes 983048 | tf_op jit(solution)/shard_map/ppermute | solution.py:31
  123.4 17.8 %collective-permute-start.25 = (f32[2,160,256]{2,1,0:T(8,128)S(1)}, f32[2,160,256]{2,1,0:T(8,128)S(1)}, u32[]{:S(2)}, u32[]{:S(2)}) collective-permute-start(f32[2,160,256]{2,1,0:T(8,128)S(1)} %get-tuple-element.9), channel_id=1, source_target_pairs={{0,64},{32,96},{64,0},{96,32},{1,65},{33,97},{65,1},{97,33},{2,66}... | collective-permute-start | bytes 983048 | tf_op jit(solution)/shard_map/ppermute | solution.py:31
  130.1 12.8 %collective-permute-start.38 = (f32[2,160,256]{2,1,0:T(8,128)S(1)}, f32[2,160,256]{2,1,0:T(8,128)S(1)}, u32[]{:S(2)}, u32[]{:S(2)}) collective-permute-start(f32[2,160,256]{2,1,0:T(8,128)S(1)} %get-tuple-element.15), channel_id=1, source_target_pairs={{0,3},{1,2},{2,1},{3,0},{4,7},{5,6},{6,5},{7,4},{8,11},{9,10},{10,... | collective-permute-start | bytes 983048 | tf_op jit(solution)/shard_map/ppermute | solution.py:31
  130.9 12.0 %collective-permute-start.37 = (f32[2,160,256]{2,1,0:T(8,128)S(1)}, f32[2,160,256]{2,1,0:T(8,128)S(1)}, u32[]{:S(2)}, u32[]{:S(2)}) collective-permute-start(f32[2,160,256]{2,1,0:T(8,128)S(1)} %get-tuple-element.16), channel_id=1, source_target_pairs={{0,1},{1,0},{2,3},{3,2},{4,5},{5,4},{6,7},{7,6},{8,9},{9,8},{10,11... | collective-permute-start | bytes 983048 | tf_op jit(solution)/shard_map/ppermute | solution.py:31
  133.0 15.4 %collective-permute-start.36 = (f32[2,160,256]{2,1,0:T(8,128)S(1)}, f32[2,160,256]{2,1,0:T(8,128)S(1)}, u32[]{:S(2)}, u32[]{:S(2)}) collective-permute-start(f32[2,160,256]{2,1,0:T(8,128)S(1)} %get-tuple-element.14), channel_id=1, source_target_pairs={{0,2},{1,3},{2,0},{3,1},{4,6},{5,7},{6,4},{7,5},{8,10},{9,11},{10,... | collective-permute-start | bytes 983048 | tf_op jit(solution)/shard_map/ppermute | solution.py:31
  141.3 7.6 %collective-permute-start.28 = (f32[160,256]{1,0:T(8,128)S(1)}, f32[160,256]{1,0:T(8,128)S(1)}, u32[]{:S(2)}, u32[]{:S(2)}) collective-permute-start(f32[160,256]{1,0:T(8,128)S(1)} %select_bitcast_fusion.3), channel_id=1, source_target_pairs={{0,16},{16,0},{1,17},{17,1},{2,18},{18,2},{3,19},{19,3},{4,20},{20... | collective-permute-start | bytes 491528 | tf_op jit(solution)/shard_map/ppermute | solution.py:31
  148.5 13.4 %copy-start = (bf16[512,256]{1,0:T(8,128)(2,1)S(1)}, bf16[512,256]{1,0:T(8,128)(2,1)}, u32[]{:S(2)}) copy-start(bf16[512,256]{1,0:T(8,128)(2,1)} %get-tuple-element.36) | copy-start | bytes 786436
  148.5 13.4 %copy-start.1 = (bf16[512,256]{1,0:T(8,128)(2,1)S(1)}, bf16[512,256]{1,0:T(8,128)(2,1)}, u32[]{:S(2)}) copy-start(bf16[512,256]{1,0:T(8,128)(2,1)} %get-tuple-element.35) | copy-start | bytes 786436
  148.5 5.4 %collective-permute-start.39 = (f32[160,256]{1,0:T(8,128)S(1)}, f32[160,256]{1,0:T(8,128)S(1)}, u32[]{:S(2)}, u32[]{:S(2)}) collective-permute-start(f32[160,256]{1,0:T(8,128)S(1)} %select_bitcast_fusion), channel_id=1, source_target_pairs={{0,4},{4,0},{1,5},{5,1},{2,6},{6,2},{3,7},{7,3},{8,12},{12,8},{9,1... | collective-permute-start | bytes 491528 | tf_op jit(solution)/shard_map/ppermute | solution.py:31
  148.9 12.9 %collective-permute-start.29 = (f32[160,256]{1,0:T(8,128)S(1)}, f32[160,256]{1,0:T(8,128)S(1)}, u32[]{:S(2)}, u32[]{:S(2)}) collective-permute-start(f32[160,256]{1,0:T(8,128)S(1)} %bitcast_add_fusion.5), channel_id=1, source_target_pairs={{0,0},{64,1},{32,2},{96,3},{16,4},{80,5},{48,6},{112,7},{8,8},{72,... | collective-permute-start | bytes 491528 | tf_op jit(solution)/shard_map/ppermute | solution.py:71
where the time goes:
time: 163 us
  waiting for transfers between devices  61.6 us (38%)
  starting transfers between devices  61 us (37%)
  matrix products  25.8 us (16%)
  other arithmetic  11.4 us (7%)
  local copies, waits for them, and re-layouts  2.45 us (2%)
    ppermute x32, waiting for transfers between devices, swap(): return lax.ppermute(value, axis, [(i, i ^ step) for i in range(SIZE[axis])])  47.4 us
    ppermute x32, starting transfers between devices, swap(): return lax.ppermute(value, axis, [(i, i ^ step) for i in range(SIZE[axis])])  38.9 us
    dot_general x22, matrix products, product(): lax.dot_general(a, b, (dims, ((), ())), preferred_element_type=jnp.float32)  25.8 us
    ppermute x4, starting transfers between devices, turn(): return lax.ppermute(value, SRC + DST, pairs)  21 us
    ppermute x4, waiting for transfers between devices, turn(): return lax.ppermute(value, SRC + DST, pairs)  14.2 us
    convert_element_type x9, other arithmetic, split(): return (high.astype(jnp.bfloat16), (value - high).astype(jnp.bfloat16))  8.68 us
  transfers between devices with their start and end apart: 40, of which 18 were waited for; matrix products, arithmetic and copies ran while one was open for 24% of the time, Pallas kernels for 0%

commit v1 on v0

--- a/solution.py
+++ b/solution.py
@@ -31,11 +31,12 @@
     return lax.ppermute(value, axis, [(i, i ^ step) for i in range(SIZE[axis])])
 
 
-def gather(block, short, ring):
+def gather(block, short, ring, got=None):
     rows, width = block.shape
     me = lax.axis_index(ring)
     in_pair, place = places(short)
-    got = swap(block, short, 1)
+    if got is None:
+        got = swap(block, short, 1)
     first = in_pair == 0
     both = jnp.stack([jnp.where(first, block, got), jnp.where(first, got, block)])
     whole = jnp.zeros((2, 4, rows, width), block.dtype)
@@ -58,15 +59,27 @@
     return jnp.where(first, both[0], both[1]) + sent
 
 
+def reduce_to_rows(parts, ring):
+    parts = parts.reshape(2, 4, -1, parts.shape[1])
+    me = lax.axis_index(ring)
+    in_pair, place = places("xh")
+    share = lambda at: lax.dynamic_slice_in_dim(parts, place(at), 1, 1)[:, 0]
+    got = [swap(share(me ^ step), ring, step) for step in (2, 1, 3)]
+    both = share(me) + got[0] + got[1] + got[2]
+    first = in_pair == 0
+    own = turn(jnp.where(first, both[0], both[1]), True)
+    return own + turn(jnp.where(first, both[1], both[0]), True, 1)
+
+
 def exchange_cores(value):
     return lax.ppermute(value, "core", [(0, 1), (1, 0)])
 
 
-def turn(value, to_rows):
+def turn(value, to_rows, flip=0):
     pairs = []
     for block, core, share in itertools.product(range(PARTS), range(2), range(PARTS)):
         row = (block * 2 + core) * PARTS + share
-        column = (column_chip(block, share) * 2 + core) * PARTS + block
+        column = ((column_chip(block, share) ^ flip) * 2 + core) * PARTS + block
         pairs.append((column, row) if to_rows else (row, column))
     return lax.ppermute(value, SRC + DST, pairs)
 
@@ -106,14 +119,18 @@
         sent = product(other, source_rows, ((1,), (0,)))
         got = exchange_cores(sent)
         kept = product(own, source_rows, ((1,), (0,)))
-        forward = reduce(kept + got, "xh", "z")
+        last = layer + 1 == LAYERS
+        if last:
+            turned_forward = reduce_to_rows(kept + got, "z")
+        else:
+            forward = reduce(kept + got, "xh", "z")
+            turned_forward = turn(forward, True)
         partial = product(own, own_rows, ((0,), (0,)))
         partial = partial + product(other, other_rows, ((0,), (0,)))
         reverse = reduce(partial, "xl", "y")
         weights, bias = layer_weights[layer], layer_biases[layer]
-        turned_forward = turn(forward, True)
         row_block = mix(turned_forward, reverse, weights, bias)
-        if layer + 1 < LAYERS:
+        if not last:
             turned_reverse = turn(reverse, False)
             column_block = mix(forward, turned_reverse, weights, bias)
     return row_block

time: 163 us -> 160 us (0.982)
  the two profiles are of different devices: /device:TPU:30 before, /device:TPU:0 now
where the time goes in v1:
time: 160 us; the launch traced here: 159 us
  starting transfers between devices  85.8 us (54%)
  waiting for transfers between devices  35.7 us (22%)
  matrix products  26.1 us (16%)
  other arithmetic  8.04 us (5%)
  local copies, waits for them, and re-layouts  2.47 us (2%)
    ppermute x31, starting transfers between devices, swap(): return lax.ppermute(value, axis, [(i, i ^ step) for i in range(SIZE[axis])])  76.1 us
    ppermute x31, waiting for transfers between devices, swap(): return lax.ppermute(value, axis, [(i, i ^ step) for i in range(SIZE[axis])])  35.7 us
    dot_general x22, matrix products, product(): lax.dot_general(a, b, (dims, ((), ())), preferred_element_type=jnp.float32)  26.1 us
    ppermute x5, starting transfers between devices, turn(): return lax.ppermute(value, SRC + DST, pairs)  8.2 us
    convert_element_type x9, other arithmetic, split(): return (high.astype(jnp.bfloat16), (value - high).astype(jnp.bfloat16))  7.16 us
  transfers between devices with their start and end apart: 40, of which 14 were waited for; matrix products, arithmetic and copies ran while one was open for 22% of the time, Pallas kernels for 0%

profile of v1, /device:TPU:0, one launch (start us, length us, event | category | flops | bytes accessed | tf_op | source)
XLA Modules:
  0.0 158.9 jit_solution(10679479861786553)
XLA Ops:
  0.0 1.6 collective-permute-start.10
  1.6 3.5 %collective-permute-start = (f32[160,256]{1,0:T(8,128)}, f32[160,256]{1,0:T(8,128)S(1)}, u32[]{:S(2)}, u32[]{:S(2)}) collective-permute-start(f32[160,256]{1,0:T(8,128)} %param.5), channel_id=1, source_target_pairs={{0,4},{4,0},{1,5},{5,1},{2,6},{6,2},{3,7},{7,3},{8,12},{12,8},{9,1... | collective-permute-start | bytes 491528 | tf_op jit(solution)/shard_map/ppermute | solution.py:31
  5.1 1.3 fusion.77
  6.5 5.8 %reduce-precision_convert_fusion = (bf16[1280,1280]{1,0:T(8,128)(2,1)S(1)}, bf16[1280,1280]{1,0:T(8,128)(2,1)S(1)}, bf16[1280,1280]{1,0:T(8,128)(2,1)S(1)}, bf16[1280,1280]{1,0:T(8,128)(2,1)S(1)}) fusion(f32[2560,1280]{1,0:T(8,128)} %param.4, s32[]{:T(128)S(6)} %select_n.161, s32[]{:T(128)S(6)} %select_n.153), kind=kLoop, calls=%fused_computation.1 | loop fusion | flops 13107200 | bytes 26214408 | tf_op jit(solution)/shard_map/convert_element_type | solution.py:89
  12.4 2.8 %collective-permute-start.11 = (f32[160,256]{1,0:T(8,128)S(1)}, f32[160,256]{1,0:T(8,128)S(1)}, u32[]{:S(2)}, u32[]{:S(2)}) collective-permute-start(f32[160,256]{1,0:T(8,128)S(1)} %collective-permute-done.10), channel_id=1, source_target_pairs={{0,16},{16,0},{1,17},{17,1},{2,18},{18,2},{3,19},{19,3},{4,20},{20... | collective-permute-start | bytes 491528 | tf_op jit(solution)/shard_map/ppermute | solution.py:31
  15.3 3.5 %collective-permute-start.1 = (f32[2,160,256]{2,1,0:T(8,128)S(1)}, f32[2,160,256]{2,1,0:T(8,128)S(1)}, u32[]{:S(2)}, u32[]{:S(2)}) collective-permute-start(f32[2,160,256]{2,1,0:T(8,128)S(1)} %pad_maximum_fusion.9), channel_id=1, source_target_pairs={{0,2},{1,3},{2,0},{3,1},{4,6},{5,7},{6,4},{7,5},{8,10},{9,11},{10,... | collective-permute-start | bytes 983048 | tf_op jit(solution)/shard_map/ppermute | solution.py:31
  18.8 3.6 %collective-permute-start.2 = (f32[2,160,256]{2,1,0:T(8,128)S(1)}, f32[2,160,256]{2,1,0:T(8,128)S(1)}, u32[]{:S(2)}, u32[]{:S(2)}) collective-permute-start(f32[2,160,256]{2,1,0:T(8,128)S(1)} %pad_maximum_fusion.9), channel_id=1, source_target_pairs={{0,1},{1,0},{2,3},{3,2},{4,5},{5,4},{6,7},{7,6},{8,9},{9,8},{10,11... | collective-permute-start | bytes 983048 | tf_op jit(solution)/shard_map/ppermute | solution.py:31
  22.6 3.4 %collective-permute-start.12 = (f32[2,160,256]{2,1,0:T(8,128)S(1)}, f32[2,160,256]{2,1,0:T(8,128)S(1)}, u32[]{:S(2)}, u32[]{:S(2)}) collective-permute-start(f32[2,160,256]{2,1,0:T(8,128)S(1)} %pad_maximum_fusion.10), channel_id=1, source_target_pairs={{0,64},{32,96},{64,0},{96,32},{1,65},{33,97},{65,1},{97,33},{2,66}... | collective-permute-start | bytes 983048 | tf_op jit(solution)/shard_map/ppermute | solution.py:31
  26.0 1.7 %collective-permute-start.13 = (f32[2,160,256]{2,1,0:T(8,128)S(1)}, f32[2,160,256]{2,1,0:T(8,128)S(1)}, u32[]{:S(2)}, u32[]{:S(2)}) collective-permute-start(f32[2,160,256]{2,1,0:T(8,128)S(1)} %pad_maximum_fusion.10), channel_id=1, source_target_pairs={{0,32},{32,0},{64,96},{96,64},{1,33},{33,1},{65,97},{97,65},{2,34}... | collective-permute-start | bytes 983048 | tf_op jit(solution)/shard_map/ppermute | solution.py:31
  27.8 6.1 %collective-permute-start.14 = (f32[2,160,256]{2,1,0:T(8,128)S(1)}, f32[2,160,256]{2,1,0:T(8,128)S(1)}, u32[]{:S(2)}, u32[]{:S(2)}) collective-permute-start(f32[2,160,256]{2,1,0:T(8,128)S(1)} %pad_maximum_fusion.10), channel_id=1, source_target_pairs={{0,96},{32,64},{64,32},{96,0},{1,97},{33,65},{65,33},{97,1},{2,98}... | collective-permute-start | bytes 983048 | tf_op jit(solution)/shard_map/ppermute | solution.py:31
  33.9 2.1 %collective-permute-done.2 = f32[2,160,256]{2,1,0:T(8,128)S(1)} collective-permute-done((f32[2,160,256]{2,1,0:T(8,128)S(1)}, f32[2,160,256]{2,1,0:T(8,128)S(1)}, u32[]{:S(2)}, u32[]{:S(2)}) %collective-permute-start.2) | collective-permute-done | bytes 327712 | tf_op jit(solution)/shard_map/ppermute | solution.py:31
  36.3 1.9 %fusion.36 = f32[1280,512]{1,0:T(8,128)S(1)} fusion(bf16[1280,1280]{1,0:T(8,128)(2,1)S(1)} %get-tuple-element.5, bf16[1280,256]{1,0:T(8,128)(2,1)S(1)} %get-tuple-element.24, bf16[1280,256]{1,0:T(8,128)(2,1)S(1)} %get-tuple-element.25), kind=kOutput, calls=%fused_computation.73 | convolution fusion | flops 1680343040 | bytes 7208960 | tf_op jit(solution)/shard_map/dot_general | solution.py:93
  39.3 1.9 %fusion.37 = f32[1280,512]{1,0:T(8,128)S(1)} fusion(bf16[1280,1280]{1,0:T(8,128)(2,1)S(1)} %get-tuple-element.8, bf16[1280,256]{1,0:T(8,128)(2,1)S(1)} %get-tuple-element.24, bf16[1280,256]{1,0:T(8,128)(2,1)S(1)} %get-tuple-element.25), kind=kOutput, calls=%fused_computation.74 | convolution fusion | flops 1680343040 | bytes 7208960 | tf_op jit(solution)/shard_map/dot_general | solution.py:93
  42.3 1.9 %fusion.12 = f32[1280,512]{1,0:T(8,128)S(1)} fusion(bf16[1280,1280]{1,0:T(8,128)(2,1)S(1)} %get-tuple-element.8, bf16[1280,256]{1,0:T(8,128)(2,1)S(1)} %get-tuple-element.31, bf16[1280,256]{1,0:T(8,128)(2,1)S(1)} %get-tuple-element.32), kind=kOutput, calls=%fused_computation.45 | convolution fusion | flops 1680343040 | bytes 7208960 | tf_op jit(solution)/shard_map/dot_general | solution.py:93
  45.3 1.1 fusion.2
  46.6 2.9 %collective-permute-start.7 = (f32[2,160,256]{2,1,0:T(8,128)S(1)}, f32[2,160,256]{2,1,0:T(8,128)S(1)}, u32[]{:S(2)}, u32[]{:S(2)}) collective-permute-start(f32[2,160,256]{2,1,0:T(8,128)S(1)} %get-tuple-element.22), channel_id=1, source_target_pairs={{0,96},{32,64},{64,32},{96,0},{1,97},{33,65},{65,33},{97,1},{2,98}... | collective-permute-start | bytes 983048 | tf_op jit(solution)/shard_map/ppermute | solution.py:31
  49.5 1.9 %collective-permute-start.5 = (f32[2,160,256]{2,1,0:T(8,128)S(1)}, f32[2,160,256]{2,1,0:T(8,128)S(1)}, u32[]{:S(2)}, u32[]{:S(2)}) collective-permute-start(f32[2,160,256]{2,1,0:T(8,128)S(1)} %get-tuple-element.21), channel_id=1, source_target_pairs={{0,64},{32,96},{64,0},{96,32},{1,65},{33,97},{65,1},{97,33},{2,66}... | collective-permute-start | bytes 983048 | tf_op jit(solution)/shard_map/ppermute | solution.py:31
  51.6 1.9 %fusion.16 = f32[1280,512]{1,0:T(8,128)S(1)} fusion(bf16[1280,1280]{1,0:T(8,128)(2,1)S(1)} %get-tuple-element.5, bf16[1280,256]{1,0:T(8,128)(2,1)S(1)} %get-tuple-element.29, bf16[1280,256]{1,0:T(8,128)(2,1)S(1)} %get-tuple-element.30), kind=kOutput, calls=%fused_computation.49 | convolution fusion | flops 1680343040 | bytes 7208960 | tf_op jit(solution)/shard_map/dot_general | solution.py:93
  53.5 1.1 fusion.3
  54.8 2.7 %collective-permute-start.18 = (f32[2,160,256]{2,1,0:T(8,128)S(1)}, f32[2,160,256]{2,1,0:T(8,128)S(1)}, u32[]{:S(2)}, u32[]{:S(2)}) collective-permute-start(f32[2,160,256]{2,1,0:T(8,128)S(1)} %get-tuple-element.27), channel_id=1, source_target_pairs={{0,3},{1,2},{2,1},{3,0},{4,7},{5,6},{6,5},{7,4},{8,11},{9,10},{10,... | collective-permute-start | bytes 983048 | tf_op jit(solution)/shard_map/ppermute | solution.py:31
  57.5 2.0 %collective-permute-start.16 = (f32[2,160,256]{2,1,0:T(8,128)S(1)}, f32[2,160,256]{2,1,0:T(8,128)S(1)}, u32[]{:S(2)}, u32[]{:S(2)}) collective-permute-start(f32[2,160,256]{2,1,0:T(8,128)S(1)} %get-tuple-element.26), channel_id=1, source_target_pairs={{0,2},{1,3},{2,0},{3,1},{4,6},{5,7},{6,4},{7,5},{8,10},{9,11},{10,... | collective-permute-start | bytes 983048 | tf_op jit(solution)/shard_map/ppermute | solution.py:31
  60.1 5.6 %collective-permute-done.5 = f32[2,160,256]{2,1,0:T(8,128)S(1)} collective-permute-done((f32[2,160,256]{2,1,0:T(8,128)S(1)}, f32[2,160,256]{2,1,0:T(8,128)S(1)}, u32[]{:S(2)}, u32[]{:S(2)}) %collective-permute-start.5) | collective-permute-done | bytes 327712 | tf_op jit(solution)/shard_map/ppermute | solution.py:31
  65.8 1.8 %collective-permute-start.8 = (f32[160,256]{1,0:T(8,128)S(1)}, f32[160,256]{1,0:T(8,128)S(1)}, u32[]{:S(2)}, u32[]{:S(2)}) collective-permute-start(f32[160,256]{1,0:T(8,128)S(1)} %select_bitcast_fusion.10), channel_id=1, source_target_pairs={{0,16},{16,0},{1,17},{17,1},{2,18},{18,2},{3,19},{19,3},{4,20},{20... | collective-permute-start | bytes 491528 | tf_op jit(solution)/shard_map/ppermute | solution.py:31
  68.0 5.0 %collective-permute-done.16 = f32[2,160,256]{2,1,0:T(8,128)S(1)} collective-permute-done((f32[2,160,256]{2,1,0:T(8,128)S(1)}, f32[2,160,256]{2,1,0:T(8,128)S(1)}, u32[]{:S(2)}, u32[]{:S(2)}) %collective-permute-start.16) | collective-permute-done | bytes 327712 | tf_op jit(solution)/shard_map/ppermute | solution.py:31
  73.2 1.2 collective-permute-start.19
  75.1 3.7 %collective-permute-done.19 = f32[160,256]{1,0:T(8,128)S(1)} collective-permute-done((f32[160,256]{1,0:T(8,128)S(1)}, f32[160,256]{1,0:T(8,128)S(1)}, u32[]{:S(2)}, u32[]{:S(2)}) %collective-permute-start.19) | collective-permute-done | bytes 163872 | tf_op jit(solution)/shard_map/ppermute | solution.py:31
  80.0 6.6 %collective-permute-start.20 = (f32[160,256]{1,0:T(8,128)S(1)}, f32[160,256]{1,0:T(8,128)S(1)}, u32[]{:S(2)}, u32[]{:S(2)}) collective-permute-start(f32[160,256]{1,0:T(8,128)S(1)} %fusion.33), channel_id=1, source_target_pairs={{0,4},{4,0},{1,5},{5,1},{2,6},{6,2},{3,7},{7,3},{8,12},{12,8},{9,1... | collective-permute-start | bytes 491528 | tf_op jit(solution)/shard_map/ppermute | solution.py:31
  87.1 2.7 %collective-permute-start.31 = (f32[160,256]{1,0:T(8,128)S(1)}, f32[160,256]{1,0:T(8,128)S(1)}, u32[]{:S(2)}, u32[]{:S(2)}) collective-permute-start(f32[160,256]{1,0:T(8,128)S(1)} %fusion.31), channel_id=1, source_target_pairs={{0,16},{16,0},{1,17},{17,1},{2,18},{18,2},{3,19},{19,3},{4,20},{20... | collective-permute-start | bytes 491528 | tf_op jit(solution)/shard_map/ppermute | solution.py:31
  90.4 4.9 %collective-permute-start.21 = (f32[2,160,256]{2,1,0:T(8,128)S(1)}, f32[2,160,256]{2,1,0:T(8,128)S(1)}, u32[]{:S(2)}, u32[]{:S(2)}) collective-permute-start(f32[2,160,256]{2,1,0:T(8,128)S(1)} %pad_maximum_fusion.12), channel_id=1, source_target_pairs={{0,2},{1,3},{2,0},{3,1},{4,6},{5,7},{6,4},{7,5},{8,10},{9,11},{10,... | collective-permute-start | bytes 983048 | tf_op jit(solution)/shard_map/ppermute | solution.py:31
  95.2 3.5 %collective-permute-start.22 = (f32[2,160,256]{2,1,0:T(8,128)S(1)}, f32[2,160,256]{2,1,0:T(8,128)S(1)}, u32[]{:S(2)}, u32[]{:S(2)}) collective-permute-start(f32[2,160,256]{2,1,0:T(8,128)S(1)} %pad_maximum_fusion.12), channel_id=1, source_target_pairs={{0,1},{1,0},{2,3},{3,2},{4,5},{5,4},{6,7},{7,6},{8,9},{9,8},{10,11... | collective-permute-start | bytes 983048 | tf_op jit(solution)/shard_map/ppermute | solution.py:31
  99.0 1.2 collective-permute-start.32
  100.2 2.8 %collective-permute-start.33 = (f32[2,160,256]{2,1,0:T(8,128)S(1)}, f32[2,160,256]{2,1,0:T(8,128)S(1)}, u32[]{:S(2)}, u32[]{:S(2)}) collective-permute-start(f32[2,160,256]{2,1,0:T(8,128)S(1)} %pad_maximum_fusion.14), channel_id=1, source_target_pairs={{0,32},{32,0},{64,96},{96,64},{1,33},{33,1},{65,97},{97,65},{2,34}... | collective-permute-start | bytes 983048 | tf_op jit(solution)/shard_map/ppermute | solution.py:31
  103.5 4.0 %collective-permute-start.34 = (f32[2,160,256]{2,1,0:T(8,128)S(1)}, f32[2,160,256]{2,1,0:T(8,128)S(1)}, u32[]{:S(2)}, u32[]{:S(2)}) collective-permute-start(f32[2,160,256]{2,1,0:T(8,128)S(1)} %pad_maximum_fusion.14), channel_id=1, source_target_pairs={{0,96},{32,64},{64,32},{96,0},{1,97},{33,65},{65,33},{97,1},{2,98}... | collective-permute-start | bytes 983048 | tf_op jit(solution)/shard_map/ppermute | solution.py:31
  107.5 2.3 %collective-permute-done.22 = f32[2,160,256]{2,1,0:T(8,128)S(1)} collective-permute-done((f32[2,160,256]{2,1,0:T(8,128)S(1)}, f32[2,160,256]{2,1,0:T(8,128)S(1)}, u32[]{:S(2)}, u32[]{:S(2)}) %collective-permute-start.22) | collective-permute-done | bytes 327712 | tf_op jit(solution)/shard_map/ppermute | solution.py:31
  110.0 1.9 %fusion.34 = f32[1280,512]{1,0:T(8,128)S(1)} fusion(bf16[1280,1280]{1,0:T(8,128)(2,1)S(1)} %get-tuple-element.5, bf16[1280,256]{1,0:T(8,128)(2,1)S(1)} %get-tuple-element.12, bf16[1280,256]{1,0:T(8,128)(2,1)S(1)} %get-tuple-element.13), kind=kOutput, calls=%fused_computation.71 | convolution fusion | flops 1680343040 | bytes 7208960 | tf_op jit(solution)/shard_map/dot_general | solution.py:93
  112.0 1.9 %fusion.35 = f32[1280,512]{1,0:T(8,128)S(1)} fusion(bf16[1280,1280]{1,0:T(8,128)(2,1)S(1)} %get-tuple-element.8, bf16[1280,256]{1,0:T(8,128)(2,1)S(1)} %get-tuple-element.12, bf16[1280,256]{1,0:T(8,128)(2,1)S(1)} %get-tuple-element.13), kind=kOutput, calls=%fused_computation.72 | convolution fusion | flops 1680343040 | bytes 7208960 | tf_op jit(solution)/shard_map/dot_general | solution.py:93
  115.9 1.9 %fusion.20 = f32[1280,512]{1,0:T(8,128)S(1)} fusion(bf16[1280,1280]{1,0:T(8,128)(2,1)S(1)} %get-tuple-element.8, bf16[1280,256]{1,0:T(8,128)(2,1)S(1)} %get-tuple-element.19, bf16[1280,256]{1,0:T(8,128)(2,1)S(1)} %get-tuple-element.20), kind=kOutput, calls=%fused_computation.54 | convolution fusion | flops 1680343040 | bytes 7208960 | tf_op jit(solution)/shard_map/dot_general | solution.py:93
  121.3 1.2 collective-permute-start.26
  122.5 2.5 %collective-permute-start.25 = (f32[2,160,256]{2,1,0:T(8,128)S(1)}, f32[2,160,256]{2,1,0:T(8,128)S(1)}, u32[]{:S(2)}, u32[]{:S(2)}) collective-permute-start(f32[2,160,256]{2,1,0:T(8,128)S(1)} %get-tuple-element.9), channel_id=1, source_target_pairs={{0,64},{32,96},{64,0},{96,32},{1,65},{33,97},{65,1},{97,33},{2,66}... | collective-permute-start | bytes 983048 | tf_op jit(solution)/shard_map/ppermute | solution.py:31
  125.2 1.9 %fusion.24 = f32[1280,512]{1,0:T(8,128)S(1)} fusion(bf16[1280,1280]{1,0:T(8,128)(2,1)S(1)} %get-tuple-element.5, bf16[1280,256]{1,0:T(8,128)(2,1)S(1)} %get-tuple-element.17, bf16[1280,256]{1,0:T(8,128)(2,1)S(1)} %get-tuple-element.18), kind=kOutput, calls=%fused_computation.58 | convolution fusion | flops 1680343040 | bytes 7208960 | tf_op jit(solution)/shard_map/dot_general | solution.py:93
  127.1 1.1 fusion.5
  128.4 2.6 %collective-permute-start.38 = (f32[2,160,256]{2,1,0:T(8,128)S(1)}, f32[2,160,256]{2,1,0:T(8,128)S(1)}, u32[]{:S(2)}, u32[]{:S(2)}) collective-permute-start(f32[2,160,256]{2,1,0:T(8,128)S(1)} %get-tuple-element.15), channel_id=1, source_target_pairs={{0,3},{1,2},{2,1},{3,0},{4,7},{5,6},{6,5},{7,4},{8,11},{9,10},{10,... | collective-permute-start | bytes 983048 | tf_op jit(solution)/shard_map/ppermute | solution.py:31
  131.2 2.0 %collective-permute-start.36 = (f32[2,160,256]{2,1,0:T(8,128)S(1)}, f32[2,160,256]{2,1,0:T(8,128)S(1)}, u32[]{:S(2)}, u32[]{:S(2)}) collective-permute-start(f32[2,160,256]{2,1,0:T(8,128)S(1)} %get-tuple-element.14), channel_id=1, source_target_pairs={{0,2},{1,3},{2,0},{3,1},{4,6},{5,7},{6,4},{7,5},{8,10},{9,11},{10,... | collective-permute-start | bytes 983048 | tf_op jit(solution)/shard_map/ppermute | solution.py:31
  133.2 6.2 %collective-permute-done.25 = f32[2,160,256]{2,1,0:T(8,128)S(1)} collective-permute-done((f32[2,160,256]{2,1,0:T(8,128)S(1)}, f32[2,160,256]{2,1,0:T(8,128)S(1)}, u32[]{:S(2)}, u32[]{:S(2)}) %collective-permute-start.25) | collective-permute-done | bytes 327712 | tf_op jit(solution)/shard_map/ppermute | solution.py:31
  140.2 4.6 %collective-permute-start.29 = (f32[160,256]{1,0:T(8,128)S(1)}, f32[160,256]{1,0:T(8,128)S(1)}, u32[]{:S(2)}, u32[]{:S(2)}) collective-permute-start(f32[160,256]{1,0:T(8,128)S(1)} %get-tuple-element.39), channel_id=1, source_target_pairs={{16,0},{80,1},{48,2},{112,3},{0,4},{64,5},{32,6},{96,7},{24,8},{88... | collective-permute-start | bytes 491528 | tf_op jit(solution)/shard_map/ppermute | solution.py:84
  144.8 5.5 %collective-permute-done.36 = f32[2,160,256]{2,1,0:T(8,128)S(1)} collective-permute-done((f32[2,160,256]{2,1,0:T(8,128)S(1)}, f32[2,160,256]{2,1,0:T(8,128)S(1)}, u32[]{:S(2)}, u32[]{:S(2)}) %collective-permute-start.36) | collective-permute-done | bytes 327712 | tf_op jit(solution)/shard_map/ppermute | solution.py:31
  150.4 4.1 %collective-permute-start.39 = (f32[160,256]{1,0:T(8,128)S(1)}, f32[160,256]{1,0:T(8,128)S(1)}, u32[]{:S(2)}, u32[]{:S(2)}) collective-permute-start(f32[160,256]{1,0:T(8,128)S(1)} %select_bitcast_fusion), channel_id=1, source_target_pairs={{0,4},{4,0},{1,5},{5,1},{2,6},{6,2},{3,7},{7,3},{8,12},{12,8},{9,1... | collective-permute-start | bytes 491528 | tf_op jit(solution)/shard_map/ppermute | solution.py:31
  154.6 3.2 %collective-permute-done.39 = f32[160,256]{1,0:T(8,128)S(1)} collective-permute-done((f32[160,256]{1,0:T(8,128)S(1)}, f32[160,256]{1,0:T(8,128)S(1)}, u32[]{:S(2)}, u32[]{:S(2)}) %collective-permute-start.39) | collective-permute-done | bytes 163872 | tf_op jit(solution)/shard_map/ppermute | solution.py:31
  (113 shorter events, 17.6 us)
Async XLA Ops:
  0.0 12.4 %collective-permute-start.10 = (f32[160,256]{1,0:T(8,128)}, f32[160,256]{1,0:T(8,128)S(1)}, u32[]{:S(2)}, u32[]{:S(2)}) collective-permute-start(f32[160,256]{1,0:T(8,128)} %param.5), channel_id=1, source_target_pairs={{0,0},{1,64},{2,32},{3,96},{4,16},{5,80},{6,48},{7,112},{8,8},{9,7... | collective-permute-start | bytes 491528 | tf_op jit(solution)/shard_map/ppermute | solution.py:84
  1.6 13.7 %collective-permute-start = (f32[160,256]{1,0:T(8,128)}, f32[160,256]{1,0:T(8,128)S(1)}, u32[]{:S(2)}, u32[]{:S(2)}) collective-permute-start(f32[160,256]{1,0:T(8,128)} %param.5), channel_id=1, source_target_pairs={{0,4},{4,0},{1,5},{5,1},{2,6},{6,2},{3,7},{7,3},{8,12},{12,8},{9,1... | collective-permute-start | bytes 491528 | tf_op jit(solution)/shard_map/ppermute | solution.py:31
  6.5 5.9 %copy-start.1 = (f32[2,256]{1,0:T(2,128)S(1)}, f32[2,256]{1,0:T(2,128)}, u32[]{:S(2)}) copy-start(f32[2,256]{1,0:T(2,128)} %param.7) | copy-start | bytes 6148
  6.5 8.7 %copy-start = (f32[160,256]{1,0:T(8,128)S(1)}, f32[160,256]{1,0:T(8,128)}, u32[]{:S(2)}) copy-start(f32[160,256]{1,0:T(8,128)} %param.5) | copy-start | bytes 491524
  12.4 10.1 %collective-permute-start.11 = (f32[160,256]{1,0:T(8,128)S(1)}, f32[160,256]{1,0:T(8,128)S(1)}, u32[]{:S(2)}, u32[]{:S(2)}) collective-permute-start(f32[160,256]{1,0:T(8,128)S(1)} %collective-permute-done.10), channel_id=1, source_target_pairs={{0,16},{16,0},{1,17},{17,1},{2,18},{18,2},{3,19},{19,3},{4,20},{20... | collective-permute-start | bytes 491528 | tf_op jit(solution)/shard_map/ppermute | solution.py:31
  15.3 12.5 %collective-permute-start.1 = (f32[2,160,256]{2,1,0:T(8,128)S(1)}, f32[2,160,256]{2,1,0:T(8,128)S(1)}, u32[]{:S(2)}, u32[]{:S(2)}) collective-permute-start(f32[2,160,256]{2,1,0:T(8,128)S(1)} %pad_maximum_fusion.9), channel_id=1, source_target_pairs={{0,2},{1,3},{2,0},{3,1},{4,6},{5,7},{6,4},{7,5},{8,10},{9,11},{10,... | collective-permute-start | bytes 983048 | tf_op jit(solution)/shard_map/ppermute | solution.py:31
  18.8 17.2 %collective-permute-start.2 = (f32[2,160,256]{2,1,0:T(8,128)S(1)}, f32[2,160,256]{2,1,0:T(8,128)S(1)}, u32[]{:S(2)}, u32[]{:S(2)}) collective-permute-start(f32[2,160,256]{2,1,0:T(8,128)S(1)} %pad_maximum_fusion.9), channel_id=1, source_target_pairs={{0,1},{1,0},{2,3},{3,2},{4,5},{5,4},{6,7},{7,6},{8,9},{9,8},{10,11... | collective-permute-start | bytes 983048 | tf_op jit(solution)/shard_map/ppermute | solution.py:31
  22.4 13.7 %collective-permute-start.3 = (f32[2,160,256]{2,1,0:T(8,128)S(1)}, f32[2,160,256]{2,1,0:T(8,128)S(1)}, u32[]{:S(2)}, u32[]{:S(2)}) collective-permute-start(f32[2,160,256]{2,1,0:T(8,128)S(1)} %pad_maximum_fusion.9), channel_id=1, source_target_pairs={{0,3},{1,2},{2,1},{3,0},{4,7},{5,6},{6,5},{7,4},{8,11},{9,10},{10,... | collective-permute-start | bytes 983048 | tf_op jit(solution)/shard_map/ppermute | solution.py:31
  22.6 18.6 %collective-permute-start.12 = (f32[2,160,256]{2,1,0:T(8,128)S(1)}, f32[2,160,256]{2,1,0:T(8,128)S(1)}, u32[]{:S(2)}, u32[]{:S(2)}) collective-permute-start(f32[2,160,256]{2,1,0:T(8,128)S(1)} %pad_maximum_fusion.10), channel_id=1, source_target_pairs={{0,64},{32,96},{64,0},{96,32},{1,65},{33,97},{65,1},{97,33},{2,66}... | collective-permute-start | bytes 983048 | tf_op jit(solution)/shard_map/ppermute | solution.py:31
  26.0 15.3 %collective-permute-start.13 = (f32[2,160,256]{2,1,0:T(8,128)S(1)}, f32[2,160,256]{2,1,0:T(8,128)S(1)}, u32[]{:S(2)}, u32[]{:S(2)}) collective-permute-start(f32[2,160,256]{2,1,0:T(8,128)S(1)} %pad_maximum_fusion.10), channel_id=1, source_target_pairs={{0,32},{32,0},{64,96},{96,64},{1,33},{33,1},{65,97},{97,65},{2,34}... | collective-permute-start | bytes 983048 | tf_op jit(solution)/shard_map/ppermute | solution.py:31
  27.8 13.4 %collective-permute-start.14 = (f32[2,160,256]{2,1,0:T(8,128)S(1)}, f32[2,160,256]{2,1,0:T(8,128)S(1)}, u32[]{:S(2)}, u32[]{:S(2)}) collective-permute-start(f32[2,160,256]{2,1,0:T(8,128)S(1)} %pad_maximum_fusion.10), channel_id=1, source_target_pairs={{0,96},{32,64},{64,32},{96,0},{1,97},{33,65},{65,33},{97,1},{2,98}... | collective-permute-start | bytes 983048 | tf_op jit(solution)/shard_map/ppermute | solution.py:31
  39.2 6.1 %collective-permute-start.4 = (f32[1280,256]{1,0:T(8,128)S(1)}, f32[1280,256]{1,0:T(8,128)S(1)}, u32[]{:S(2)}, u32[]{:S(2)}) collective-permute-start(f32[1280,256]{1,0:T(8,128)S(1)} %convolution_add_fusion.6), channel_id=1, source_target_pairs={{0,8},{8,0},{1,9},{9,1},{2,10},{10,2},{3,11},{11,3},{4,12},{12,4},... | collective-permute-start | bytes 3932168 | tf_op jit(solution)/shard_map/ppermute | solution.py:75
  41.3 10.0 %collective-permute-start.15 = (f32[1280,256]{1,0:T(8,128)S(1)}, f32[1280,256]{1,0:T(8,128)S(1)}, u32[]{:S(2)}, u32[]{:S(2)}) collective-permute-start(f32[1280,256]{1,0:T(8,128)S(1)} %bitcast.200), channel_id=1, source_target_pairs={{0,8},{8,0},{1,9},{9,1},{2,10},{10,2},{3,11},{11,3},{4,12},{12,4},... | collective-permute-start | bytes 3932168 | tf_op jit(solution)/shard_map/ppermute | solution.py:75
  46.6 11.0 %collective-permute-start.7 = (f32[2,160,256]{2,1,0:T(8,128)S(1)}, f32[2,160,256]{2,1,0:T(8,128)S(1)}, u32[]{:S(2)}, u32[]{:S(2)}) collective-permute-start(f32[2,160,256]{2,1,0:T(8,128)S(1)} %get-tuple-element.22), channel_id=1, source_target_pairs={{0,96},{32,64},{64,32},{96,0},{1,97},{33,65},{65,33},{97,1},{2,98}... | collective-permute-start | bytes 983048 | tf_op jit(solution)/shard_map/ppermute | solution.py:31
  49.5 10.6 %collective-permute-start.6 = (f32[2,160,256]{2,1,0:T(8,128)S(1)}, f32[2,160,256]{2,1,0:T(8,128)S(1)}, u32[]{:S(2)}, u32[]{:S(2)}) collective-permute-start(f32[2,160,256]{2,1,0:T(8,128)S(1)} %get-tuple-element.23), channel_id=1, source_target_pairs={{0,32},{32,0},{64,96},{96,64},{1,33},{33,1},{65,97},{97,65},{2,34}... | collective-permute-start | bytes 983048 | tf_op jit(solution)/shard_map/ppermute | solution.py:31
  49.5 16.2 %collective-permute-start.5 = (f32[2,160,256]{2,1,0:T(8,128)S(1)}, f32[2,160,256]{2,1,0:T(8,128)S(1)}, u32[]{:S(2)}, u32[]{:S(2)}) collective-permute-start(f32[2,160,256]{2,1,0:T(8,128)S(1)} %get-tuple-element.21), channel_id=1, source_target_pairs={{0,64},{32,96},{64,0},{96,32},{1,65},{33,97},{65,1},{97,33},{2,66}... | collective-permute-start | bytes 983048 | tf_op jit(solution)/shard_map/ppermute | solution.py:31
  54.8 12.8 %collective-permute-start.18 = (f32[2,160,256]{2,1,0:T(8,128)S(1)}, f32[2,160,256]{2,1,0:T(8,128)S(1)}, u32[]{:S(2)}, u32[]{:S(2)}) collective-permute-start(f32[2,160,256]{2,1,0:T(8,128)S(1)} %get-tuple-element.27), channel_id=1, source_target_pairs={{0,3},{1,2},{2,1},{3,0},{4,7},{5,6},{6,5},{7,4},{8,11},{9,10},{10,... | collective-permute-start | bytes 983048 | tf_op jit(solution)/shard_map/ppermute | solution.py:31
  57.4 10.6 %collective-permute-start.17 = (f32[2,160,256]{2,1,0:T(8,128)S(1)}, f32[2,160,256]{2,1,0:T(8,128)S(1)}, u32[]{:S(2)}, u32[]{:S(2)}) collective-permute-start(f32[2,160,256]{2,1,0:T(8,128)S(1)} %get-tuple-element.28), channel_id=1, source_target_pairs={{0,1},{1,0},{2,3},{3,2},{4,5},{5,4},{6,7},{7,6},{8,9},{9,8},{10,11... | collective-permute-start | bytes 983048 | tf_op jit(solution)/shard_map/ppermute | solution.py:31
  57.5 15.5 %collective-permute-start.16 = (f32[2,160,256]{2,1,0:T(8,128)S(1)}, f32[2,160,256]{2,1,0:T(8,128)S(1)}, u32[]{:S(2)}, u32[]{:S(2)}) collective-permute-start(f32[2,160,256]{2,1,0:T(8,128)S(1)} %get-tuple-element.26), channel_id=1, source_target_pairs={{0,2},{1,3},{2,0},{3,1},{4,6},{5,7},{6,4},{7,5},{8,10},{9,11},{10,... | collective-permute-start | bytes 983048 | tf_op jit(solution)/shard_map/ppermute | solution.py:31
  65.8 8.5 %collective-permute-start.8 = (f32[160,256]{1,0:T(8,128)S(1)}, f32[160,256]{1,0:T(8,128)S(1)}, u32[]{:S(2)}, u32[]{:S(2)}) collective-permute-start(f32[160,256]{1,0:T(8,128)S(1)} %select_bitcast_fusion.10), channel_id=1, source_target_pairs={{0,16},{16,0},{1,17},{17,1},{2,18},{18,2},{3,19},{19,3},{4,20},{20... | collective-permute-start | bytes 491528 | tf_op jit(solution)/shard_map/ppermute | solution.py:31
  73.2 5.6 %collective-permute-start.19 = (f32[160,256]{1,0:T(8,128)S(1)}, f32[160,256]{1,0:T(8,128)S(1)}, u32[]{:S(2)}, u32[]{:S(2)}) collective-permute-start(f32[160,256]{1,0:T(8,128)S(1)} %select_bitcast_fusion.7), channel_id=1, source_target_pairs={{0,4},{4,0},{1,5},{5,1},{2,6},{6,2},{3,7},{7,3},{8,12},{12,8},{9,1... | collective-permute-start | bytes 491528 | tf_op jit(solution)/shard_map/ppermute | solution.py:31
  74.4 5.1 %collective-permute-start.9 = (f32[160,256]{1,0:T(8,128)S(1)}, f32[160,256]{1,0:T(8,128)S(1)}, u32[]{:S(2)}, u32[]{:S(2)}) collective-permute-start(f32[160,256]{1,0:T(8,128)S(1)} %bitcast_add_fusion.6), channel_id=1, source_target_pairs={{0,0},{64,1},{32,2},{96,3},{16,4},{80,5},{48,6},{112,7},{8,8},{72,... | collective-permute-start | bytes 491528 | tf_op jit(solution)/shard_map/ppermute | solution.py:84
  78.8 7.8 %collective-permute-start.30 = (f32[160,256]{1,0:T(8,128)S(1)}, f32[160,256]{1,0:T(8,128)S(1)}, u32[]{:S(2)}, u32[]{:S(2)}) collective-permute-start(f32[160,256]{1,0:T(8,128)S(1)} %bitcast_add_fusion.5), channel_id=1, source_target_pairs={{0,0},{1,64},{2,32},{3,96},{4,16},{5,80},{6,48},{7,112},{8,8},{9,7... | collective-permute-start | bytes 491528 | tf_op jit(solution)/shard_map/ppermute | solution.py:84
  80.0 10.3 %collective-permute-start.20 = (f32[160,256]{1,0:T(8,128)S(1)}, f32[160,256]{1,0:T(8,128)S(1)}, u32[]{:S(2)}, u32[]{:S(2)}) collective-permute-start(f32[160,256]{1,0:T(8,128)S(1)} %fusion.33), channel_id=1, source_target_pairs={{0,4},{4,0},{1,5},{5,1},{2,6},{6,2},{3,7},{7,3},{8,12},{12,8},{9,1... | collective-permute-start | bytes 491528 | tf_op jit(solution)/shard_map/ppermute | solution.py:31
  87.1 11.9 %collective-permute-start.31 = (f32[160,256]{1,0:T(8,128)S(1)}, f32[160,256]{1,0:T(8,128)S(1)}, u32[]{:S(2)}, u32[]{:S(2)}) collective-permute-start(f32[160,256]{1,0:T(8,128)S(1)} %fusion.31), channel_id=1, source_target_pairs={{0,16},{16,0},{1,17},{17,1},{2,18},{18,2},{3,19},{19,3},{4,20},{20... | collective-permute-start | bytes 491528 | tf_op jit(solution)/shard_map/ppermute | solution.py:31
  90.4 13.1 %collective-permute-start.21 = (f32[2,160,256]{2,1,0:T(8,128)S(1)}, f32[2,160,256]{2,1,0:T(8,128)S(1)}, u32[]{:S(2)}, u32[]{:S(2)}) collective-permute-start(f32[2,160,256]{2,1,0:T(8,128)S(1)} %pad_maximum_fusion.12), channel_id=1, source_target_pairs={{0,2},{1,3},{2,0},{3,1},{4,6},{5,7},{6,4},{7,5},{8,10},{9,11},{10,... | collective-permute-start | bytes 983048 | tf_op jit(solution)/shard_map/ppermute | solution.py:31
  95.2 14.5 %collective-permute-start.22 = (f32[2,160,256]{2,1,0:T(8,128)S(1)}, f32[2,160,256]{2,1,0:T(8,128)S(1)}, u32[]{:S(2)}, u32[]{:S(2)}) collective-permute-start(f32[2,160,256]{2,1,0:T(8,128)S(1)} %pad_maximum_fusion.12), channel_id=1, source_target_pairs={{0,1},{1,0},{2,3},{3,2},{4,5},{5,4},{6,7},{7,6},{8,9},{9,8},{10,11... | collective-permute-start | bytes 983048 | tf_op jit(solution)/shard_map/ppermute | solution.py:31
  98.8 11.0 %collective-permute-start.23 = (f32[2,160,256]{2,1,0:T(8,128)S(1)}, f32[2,160,256]{2,1,0:T(8,128)S(1)}, u32[]{:S(2)}, u32[]{:S(2)}) collective-permute-start(f32[2,160,256]{2,1,0:T(8,128)S(1)} %pad_maximum_fusion.12), channel_id=1, source_target_pairs={{0,3},{1,2},{2,1},{3,0},{4,7},{5,6},{6,5},{7,4},{8,11},{9,10},{10,... | collective-permute-start | bytes 983048 | tf_op jit(solution)/shard_map/ppermute | solution.py:31
  99.0 16.0 %collective-permute-start.32 = (f32[2,160,256]{2,1,0:T(8,128)S(1)}, f32[2,160,256]{2,1,0:T(8,128)S(1)}, u32[]{:S(2)}, u32[]{:S(2)}) collective-permute-start(f32[2,160,256]{2,1,0:T(8,128)S(1)} %pad_maximum_fusion.14), channel_id=1, source_target_pairs={{0,64},{32,96},{64,0},{96,32},{1,65},{33,97},{65,1},{97,33},{2,66}... | collective-permute-start | bytes 983048 | tf_op jit(solution)/shard_map/ppermute | solution.py:31
  100.2 14.8 %collective-permute-start.33 = (f32[2,160,256]{2,1,0:T(8,128)S(1)}, f32[2,160,256]{2,1,0:T(8,128)S(1)}, u32[]{:S(2)}, u32[]{:S(2)}) collective-permute-start(f32[2,160,256]{2,1,0:T(8,128)S(1)} %pad_maximum_fusion.14), channel_id=1, source_target_pairs={{0,32},{32,0},{64,96},{96,64},{1,33},{33,1},{65,97},{97,65},{2,34}... | collective-permute-start | bytes 983048 | tf_op jit(solution)/shard_map/ppermute | solution.py:31
  103.5 11.7 %collective-permute-start.34 = (f32[2,160,256]{2,1,0:T(8,128)S(1)}, f32[2,160,256]{2,1,0:T(8,128)S(1)}, u32[]{:S(2)}, u32[]{:S(2)}) collective-permute-start(f32[2,160,256]{2,1,0:T(8,128)S(1)} %pad_maximum_fusion.14), channel_id=1, source_target_pairs={{0,96},{32,64},{64,32},{96,0},{1,97},{33,65},{65,33},{97,1},{2,98}... | collective-permute-start | bytes 983048 | tf_op jit(solution)/shard_map/ppermute | solution.py:31
  114.9 4.0 %collective-permute-start.24 = (f32[1280,256]{1,0:T(8,128)S(1)}, f32[1280,256]{1,0:T(8,128)S(1)}, u32[]{:S(2)}, u32[]{:S(2)}) collective-permute-start(f32[1280,256]{1,0:T(8,128)S(1)} %convolution_add_fusion.2), channel_id=1, source_target_pairs={{0,8},{8,0},{1,9},{9,1},{2,10},{10,2},{3,11},{11,3},{4,12},{12,4},... | collective-permute-start | bytes 3932168 | tf_op jit(solution)/shard_map/ppermute | solution.py:75
  115.2 9.9 %collective-permute-start.35 = (f32[1280,256]{1,0:T(8,128)S(1)}, f32[1280,256]{1,0:T(8,128)S(1)}, u32[]{:S(2)}, u32[]{:S(2)}) collective-permute-start(f32[1280,256]{1,0:T(8,128)S(1)} %bitcast.199), channel_id=1, source_target_pairs={{0,8},{8,0},{1,9},{9,1},{2,10},{10,2},{3,11},{11,3},{4,12},{12,4},... | collective-permute-start | bytes 3932168 | tf_op jit(solution)/shard_map/ppermute | solution.py:75
  120.2 11.0 %collective-permute-start.27 = (f32[2,160,256]{2,1,0:T(8,128)S(1)}, f32[2,160,256]{2,1,0:T(8,128)S(1)}, u32[]{:S(2)}, u32[]{:S(2)}) collective-permute-start(f32[2,160,256]{2,1,0:T(8,128)S(1)} %get-tuple-element.10), channel_id=1, source_target_pairs={{0,96},{32,64},{64,32},{96,0},{1,97},{33,65},{65,33},{97,1},{2,98}... | collective-permute-start | bytes 983048 | tf_op jit(solution)/shard_map/ppermute | solution.py:31
  121.3 11.9 %collective-permute-start.26 = (f32[2,160,256]{2,1,0:T(8,128)S(1)}, f32[2,160,256]{2,1,0:T(8,128)S(1)}, u32[]{:S(2)}, u32[]{:S(2)}) collective-permute-start(f32[2,160,256]{2,1,0:T(8,128)S(1)} %get-tuple-element.11), channel_id=1, source_target_pairs={{0,32},{32,0},{64,96},{96,64},{1,33},{33,1},{65,97},{97,65},{2,34}... | collective-permute-start | bytes 983048 | tf_op jit(solution)/shard_map/ppermute | solution.py:31
  122.5 16.9 %collective-permute-start.25 = (f32[2,160,256]{2,1,0:T(8,128)S(1)}, f32[2,160,256]{2,1,0:T(8,128)S(1)}, u32[]{:S(2)}, u32[]{:S(2)}) collective-permute-start(f32[2,160,256]{2,1,0:T(8,128)S(1)} %get-tuple-element.9), channel_id=1, source_target_pairs={{0,64},{32,96},{64,0},{96,32},{1,65},{33,97},{65,1},{97,33},{2,66}... | collective-permute-start | bytes 983048 | tf_op jit(solution)/shard_map/ppermute | solution.py:31
  128.4 16.4 %collective-permute-start.38 = (f32[2,160,256]{2,1,0:T(8,128)S(1)}, f32[2,160,256]{2,1,0:T(8,128)S(1)}, u32[]{:S(2)}, u32[]{:S(2)}) collective-permute-start(f32[2,160,256]{2,1,0:T(8,128)S(1)} %get-tuple-element.15), channel_id=1, source_target_pairs={{0,3},{1,2},{2,1},{3,0},{4,7},{5,6},{6,5},{7,4},{8,11},{9,10},{10,... | collective-permute-start | bytes 983048 | tf_op jit(solution)/shard_map/ppermute | solution.py:31
  131.0 13.8 %collective-permute-start.37 = (f32[2,160,256]{2,1,0:T(8,128)S(1)}, f32[2,160,256]{2,1,0:T(8,128)S(1)}, u32[]{:S(2)}, u32[]{:S(2)}) collective-permute-start(f32[2,160,256]{2,1,0:T(8,128)S(1)} %get-tuple-element.16), channel_id=1, source_target_pairs={{0,1},{1,0},{2,3},{3,2},{4,5},{5,4},{6,7},{7,6},{8,9},{9,8},{10,11... | collective-permute-start | bytes 983048 | tf_op jit(solution)/shard_map/ppermute | solution.py:31
  131.2 19.1 %collective-permute-start.36 = (f32[2,160,256]{2,1,0:T(8,128)S(1)}, f32[2,160,256]{2,1,0:T(8,128)S(1)}, u32[]{:S(2)}, u32[]{:S(2)}) collective-permute-start(f32[2,160,256]{2,1,0:T(8,128)S(1)} %get-tuple-element.14), channel_id=1, source_target_pairs={{0,2},{1,3},{2,0},{3,1},{4,6},{5,7},{6,4},{7,5},{8,10},{9,11},{10,... | collective-permute-start | bytes 983048 | tf_op jit(solution)/shard_map/ppermute | solution.py:31
  139.5 15.0 %collective-permute-start.28 = (f32[160,256]{1,0:T(8,128)S(1)}, f32[160,256]{1,0:T(8,128)S(1)}, u32[]{:S(2)}, u32[]{:S(2)}) collective-permute-start(f32[160,256]{1,0:T(8,128)S(1)} %get-tuple-element.40), channel_id=1, source_target_pairs={{0,0},{64,1},{32,2},{96,3},{16,4},{80,5},{48,6},{112,7},{8,8},{72,... | collective-permute-start | bytes 491528 | tf_op jit(solution)/shard_map/ppermute | solution.py:84
  140.2 14.3 %collective-permute-start.29 = (f32[160,256]{1,0:T(8,128)S(1)}, f32[160,256]{1,0:T(8,128)S(1)}, u32[]{:S(2)}, u32[]{:S(2)}) collective-permute-start(f32[160,256]{1,0:T(8,128)S(1)} %get-tuple-element.39), channel_id=1, source_target_pairs={{16,0},{80,1},{48,2},{112,3},{0,4},{64,5},{32,6},{96,7},{24,8},{88... | collective-permute-start | bytes 491528 | tf_op jit(solution)/shard_map/ppermute | solution.py:84
  150.4 7.4 %collective-permute-start.39 = (f32[160,256]{1,0:T(8,128)S(1)}, f32[160,256]{1,0:T(8,128)S(1)}, u32[]{:S(2)}, u32[]{:S(2)}) collective-permute-start(f32[160,256]{1,0:T(8,128)S(1)} %select_bitcast_fusion), channel_id=1, source_target_pairs={{0,4},{4,0},{1,5},{5,1},{2,6},{6,2},{3,7},{7,3},{8,12},{12,8},{9,1... | collective-permute-start | bytes 491528 | tf_op jit(solution)/shard_map/ppermute | solution.py:31

commit v2 on v1

--- a/solution.py
+++ b/solution.py
@@ -41,7 +41,7 @@
     both = jnp.stack([jnp.where(first, block, got), jnp.where(first, got, block)])
     whole = jnp.zeros((2, 4, rows, width), block.dtype)
     whole = lax.dynamic_update_slice(whole, both[:, None], (0, place(me), 0, 0))
-    for step in (2, 1, 3):
+    for step in (1, 3, 2):
         got = swap(both, ring, step)
         whole = lax.dynamic_update_slice(whole, got[:, None], (0, place(me ^ step), 0, 0))
     return whole.reshape(-1, width)
@@ -98,8 +98,7 @@
 
 def mix(forward, reverse, weights, bias):
     both = split(jnp.concatenate([forward, reverse], axis=1))
-    stacked = split(weights.reshape(-1, weights.shape[-1]))
-    return jax.nn.relu(product(both, stacked, ((1,), (0,))) + bias[None, :])
+    return jax.nn.relu(product(both, weights, ((1,), (0,))) + bias[None, :])
 
 
 def body(adjacency, features, layer_weights, layer_biases):
@@ -109,6 +108,7 @@
     for layer in range(LAYERS):
         if layer == 0:
             column_block = turn(features, False)
+            stacked = split(layer_weights.reshape(LAYERS, -1, layer_weights.shape[-1]))
             own = split(lax.dynamic_slice_in_dim(adjacency, core * half, half, 0))
             other = split(lax.dynamic_slice_in_dim(adjacency, (1 - core) * half, half, 0))
         source_rows = split(gather(row_block, "xl", "y"))
@@ -128,7 +128,7 @@
         partial = product(own, own_rows, ((0,), (0,)))
         partial = partial + product(other, other_rows, ((0,), (0,)))
         reverse = reduce(partial, "xl", "y")
-        weights, bias = layer_weights[layer], layer_biases[layer]
+        weights, bias = [half[layer] for half in stacked], layer_biases[layer]
         row_block = mix(turned_forward, reverse, weights, bias)
         if not last:
             turned_reverse = turn(reverse, False)

time: 160 us -> 159 us (level)
  waiting for transfers between devices: 35.7 us -> 48.7 us
  starting transfers between devices: 85.8 us -> 73 us
    ppermute x31, waiting for transfers between devices: 35.7 us -> 48.7 us  [swap(): return lax.ppermute(value, axis, [(i, i ^ step) for i in range(SIZE[axis])])]
    ppermute x31, starting transfers between devices: 76.1 us -> 64.1 us  [swap(): return lax.ppermute(value, axis, [(i, i ^ step) for i in range(SIZE[axis])])]
    convert_element_type x9 -> x8, other arithmetic: 7.16 us -> 8.41 us  [split(): return (high.astype(jnp.bfloat16), (value - high).astype(jnp.bfloat16))]
  transfers between devices with their start and end apart: 40 -> 40, of which waited for: 14 -> 16; matrix products, arithmetic and copies ran while one was open for 22% -> 22% of each run, Pallas kernels for 0% -> 0%
where the time goes in v2:
time: 159 us
  starting transfers between devices  73 us (46%)
  waiting for transfers between devices  48.7 us (31%)
  matrix products  25.7 us (16%)
  other arithmetic  9.28 us (6%)
    ppermute x31, starting transfers between devices, swap(): return lax.ppermute(value, axis, [(i, i ^ step) for i in range(SIZE[axis])])  64.1 us
    ppermute x31, waiting for transfers between devices, swap(): return lax.ppermute(value, axis, [(i, i ^ step) for i in range(SIZE[axis])])  48.7 us
    dot_general x22, matrix products, product(): lax.dot_general(a, b, (dims, ((), ())), preferred_element_type=jnp.float32)  25.7 us
    convert_element_type x8, other arithmetic, split(): return (high.astype(jnp.bfloat16), (value - high).astype(jnp.bfloat16))  8.41 us
    ppermute x5, starting transfers between devices, turn(): return lax.ppermute(value, SRC + DST, pairs)  7.42 us
  transfers between devices with their start and end apart: 40, of which 16 were waited for; matrix products, arithmetic and copies ran while one was open for 22% of the time, Pallas kernels for 0%

profile of v2, /device:TPU:0, one launch (start us, length us, event | category | flops | bytes accessed | tf_op | source)
XLA Modules:
  0.0 158.8 jit_solution(15758074078733705997)
XLA Ops:
  0.0 1.6 collective-permute-start.10
  1.6 3.5 %collective-permute-start = (f32[160,256]{1,0:T(8,128)}, f32[160,256]{1,0:T(8,128)S(1)}, u32[]{:S(2)}, u32[]{:S(2)}) collective-permute-start(f32[160,256]{1,0:T(8,128)} %param.5), channel_id=1, source_target_pairs={{0,4},{4,0},{1,5},{5,1},{2,6},{6,2},{3,7},{7,3},{8,12},{12,8},{9,1... | collective-permute-start | bytes 491528 | tf_op jit(solution)/shard_map/ppermute | solution.py:31
  5.1 1.4 reduce-precision_convert_fusion.8
  6.6 5.8 %reduce-precision_convert_fusion = (bf16[1280,1280]{1,0:T(8,128)(2,1)S(1)}, bf16[1280,1280]{1,0:T(8,128)(2,1)S(1)}, bf16[1280,1280]{1,0:T(8,128)(2,1)S(1)}, bf16[1280,1280]{1,0:T(8,128)(2,1)S(1)}) fusion(f32[2560,1280]{1,0:T(8,128)} %param.4, s32[]{:T(128)S(6)} %select_n.161, s32[]{:T(128)S(6)} %select_n.153), kind=kLoop, calls=%fused_computation.1 | loop fusion | flops 13107200 | bytes 26214408 | tf_op jit(solution)/shard_map/convert_element_type | solution.py:89
  12.5 2.8 %collective-permute-start.11 = (f32[160,256]{1,0:T(8,128)S(1)}, f32[160,256]{1,0:T(8,128)S(1)}, u32[]{:S(2)}, u32[]{:S(2)}) collective-permute-start(f32[160,256]{1,0:T(8,128)S(1)} %collective-permute-done.10), channel_id=1, source_target_pairs={{0,16},{16,0},{1,17},{17,1},{2,18},{18,2},{3,19},{19,3},{4,20},{20... | collective-permute-start | bytes 491528 | tf_op jit(solution)/shard_map/ppermute | solution.py:31
  15.4 4.0 %collective-permute-start.1 = (f32[2,160,256]{2,1,0:T(8,128)S(1)}, f32[2,160,256]{2,1,0:T(8,128)S(1)}, u32[]{:S(2)}, u32[]{:S(2)}) collective-permute-start(f32[2,160,256]{2,1,0:T(8,128)S(1)} %pad_maximum_fusion.9), channel_id=1, source_target_pairs={{0,1},{1,0},{2,3},{3,2},{4,5},{5,4},{6,7},{7,6},{8,9},{9,8},{10,11... | collective-permute-start | bytes 983048 | tf_op jit(solution)/shard_map/ppermute | solution.py:31
  19.3 2.4 %collective-permute-start.2 = (f32[2,160,256]{2,1,0:T(8,128)S(1)}, f32[2,160,256]{2,1,0:T(8,128)S(1)}, u32[]{:S(2)}, u32[]{:S(2)}) collective-permute-start(f32[2,160,256]{2,1,0:T(8,128)S(1)} %pad_maximum_fusion.9), channel_id=1, source_target_pairs={{0,3},{1,2},{2,1},{3,0},{4,7},{5,6},{6,5},{7,4},{8,11},{9,10},{10,... | collective-permute-start | bytes 983048 | tf_op jit(solution)/shard_map/ppermute | solution.py:31
  21.7 1.4 collective-permute-start.3
  23.3 2.2 %collective-permute-start.12 = (f32[2,160,256]{2,1,0:T(8,128)S(1)}, f32[2,160,256]{2,1,0:T(8,128)S(1)}, u32[]{:S(2)}, u32[]{:S(2)}) collective-permute-start(f32[2,160,256]{2,1,0:T(8,128)S(1)} %pad_maximum_fusion.10), channel_id=1, source_target_pairs={{0,32},{32,0},{64,96},{96,64},{1,33},{33,1},{65,97},{97,65},{2,34}... | collective-permute-start | bytes 983048 | tf_op jit(solution)/shard_map/ppermute | solution.py:31
  25.5 1.5 collective-permute-start.13
  27.9 4.3 %collective-permute-start.14 = (f32[2,160,256]{2,1,0:T(8,128)S(1)}, f32[2,160,256]{2,1,0:T(8,128)S(1)}, u32[]{:S(2)}, u32[]{:S(2)}) collective-permute-start(f32[2,160,256]{2,1,0:T(8,128)S(1)} %pad_maximum_fusion.10), channel_id=1, source_target_pairs={{0,64},{32,96},{64,0},{96,32},{1,65},{33,97},{65,1},{97,33},{2,66}... | collective-permute-start | bytes 983048 | tf_op jit(solution)/shard_map/ppermute | solution.py:31
  32.2 2.7 %collective-permute-done.2 = f32[2,160,256]{2,1,0:T(8,128)S(1)} collective-permute-done((f32[2,160,256]{2,1,0:T(8,128)S(1)}, f32[2,160,256]{2,1,0:T(8,128)S(1)}, u32[]{:S(2)}, u32[]{:S(2)}) %collective-permute-start.2) | collective-permute-done | bytes 327712 | tf_op jit(solution)/shard_map/ppermute | solution.py:31
  34.9 1.8 %collective-permute-done.3 = f32[2,160,256]{2,1,0:T(8,128)S(1)} collective-permute-done((f32[2,160,256]{2,1,0:T(8,128)S(1)}, f32[2,160,256]{2,1,0:T(8,128)S(1)}, u32[]{:S(2)}, u32[]{:S(2)}) %collective-permute-start.3) | collective-permute-done | bytes 327712 | tf_op jit(solution)/shard_map/ppermute | solution.py:31
  36.9 1.9 %fusion.37 = f32[1280,512]{1,0:T(8,128)S(1)} fusion(bf16[1280,1280]{1,0:T(8,128)(2,1)S(1)} %get-tuple-element.5, bf16[1280,256]{1,0:T(8,128)(2,1)S(1)} %get-tuple-element.24, bf16[1280,256]{1,0:T(8,128)(2,1)S(1)} %get-tuple-element.25), kind=kOutput, calls=%fused_computation.76 | convolution fusion | flops 1680343040 | bytes 7208960 | tf_op jit(solution)/shard_map/dot_general | solution.py:93
  39.9 1.9 %fusion.38 = f32[1280,512]{1,0:T(8,128)S(1)} fusion(bf16[1280,1280]{1,0:T(8,128)(2,1)S(1)} %get-tuple-element.8, bf16[1280,256]{1,0:T(8,128)(2,1)S(1)} %get-tuple-element.24, bf16[1280,256]{1,0:T(8,128)(2,1)S(1)} %get-tuple-element.25), kind=kOutput, calls=%fused_computation.77 | convolution fusion | flops 1680343040 | bytes 7208960 | tf_op jit(solution)/shard_map/dot_general | solution.py:93
  42.9 1.9 %fusion.12 = f32[1280,512]{1,0:T(8,128)S(1)} fusion(bf16[1280,1280]{1,0:T(8,128)(2,1)S(1)} %get-tuple-element.8, bf16[1280,256]{1,0:T(8,128)(2,1)S(1)} %get-tuple-element.31, bf16[1280,256]{1,0:T(8,128)(2,1)S(1)} %get-tuple-element.32), kind=kOutput, calls=%fused_computation.47 | convolution fusion | flops 1680343040 | bytes 7208960 | tf_op jit(solution)/shard_map/dot_general | solution.py:93
  45.9 1.1 fusion.2
  47.1 2.7 %collective-permute-start.7 = (f32[2,160,256]{2,1,0:T(8,128)S(1)}, f32[2,160,256]{2,1,0:T(8,128)S(1)}, u32[]{:S(2)}, u32[]{:S(2)}) collective-permute-start(f32[2,160,256]{2,1,0:T(8,128)S(1)} %get-tuple-element.22), channel_id=1, source_target_pairs={{0,96},{32,64},{64,32},{96,0},{1,97},{33,65},{65,33},{97,1},{2,98}... | collective-permute-start | bytes 983048 | tf_op jit(solution)/shard_map/ppermute | solution.py:31
  49.9 2.1 %collective-permute-start.5 = (f32[2,160,256]{2,1,0:T(8,128)S(1)}, f32[2,160,256]{2,1,0:T(8,128)S(1)}, u32[]{:S(2)}, u32[]{:S(2)}) collective-permute-start(f32[2,160,256]{2,1,0:T(8,128)S(1)} %get-tuple-element.21), channel_id=1, source_target_pairs={{0,64},{32,96},{64,0},{96,32},{1,65},{33,97},{65,1},{97,33},{2,66}... | collective-permute-start | bytes 983048 | tf_op jit(solution)/shard_map/ppermute | solution.py:31
  52.1 1.9 %fusion.16 = f32[1280,512]{1,0:T(8,128)S(1)} fusion(bf16[1280,1280]{1,0:T(8,128)(2,1)S(1)} %get-tuple-element.5, bf16[1280,256]{1,0:T(8,128)(2,1)S(1)} %get-tuple-element.29, bf16[1280,256]{1,0:T(8,128)(2,1)S(1)} %get-tuple-element.30), kind=kOutput, calls=%fused_computation.51 | convolution fusion | flops 1680343040 | bytes 7208960 | tf_op jit(solution)/shard_map/dot_general | solution.py:93
  55.2 2.0 %collective-permute-start.18 = (f32[2,160,256]{2,1,0:T(8,128)S(1)}, f32[2,160,256]{2,1,0:T(8,128)S(1)}, u32[]{:S(2)}, u32[]{:S(2)}) collective-permute-start(f32[2,160,256]{2,1,0:T(8,128)S(1)} %get-tuple-element.27), channel_id=1, source_target_pairs={{0,3},{1,2},{2,1},{3,0},{4,7},{5,6},{6,5},{7,4},{8,11},{9,10},{10,... | collective-permute-start | bytes 983048 | tf_op jit(solution)/shard_map/ppermute | solution.py:31
  58.1 1.9 %collective-permute-start.16 = (f32[2,160,256]{2,1,0:T(8,128)S(1)}, f32[2,160,256]{2,1,0:T(8,128)S(1)}, u32[]{:S(2)}, u32[]{:S(2)}) collective-permute-start(f32[2,160,256]{2,1,0:T(8,128)S(1)} %get-tuple-element.26), channel_id=1, source_target_pairs={{0,2},{1,3},{2,0},{3,1},{4,6},{5,7},{6,4},{7,5},{8,10},{9,11},{10,... | collective-permute-start | bytes 983048 | tf_op jit(solution)/shard_map/ppermute | solution.py:31
  60.5 5.8 %collective-permute-done.5 = f32[2,160,256]{2,1,0:T(8,128)S(1)} collective-permute-done((f32[2,160,256]{2,1,0:T(8,128)S(1)}, f32[2,160,256]{2,1,0:T(8,128)S(1)}, u32[]{:S(2)}, u32[]{:S(2)}) %collective-permute-start.5) | collective-permute-done | bytes 327712 | tf_op jit(solution)/shard_map/ppermute | solution.py:31
  66.4 1.4 collective-permute-start.8
  67.8 5.7 %collective-permute-done.16 = f32[2,160,256]{2,1,0:T(8,128)S(1)} collective-permute-done((f32[2,160,256]{2,1,0:T(8,128)S(1)}, f32[2,160,256]{2,1,0:T(8,128)S(1)}, u32[]{:S(2)}, u32[]{:S(2)}) %collective-permute-start.16) | collective-permute-done | bytes 327712 | tf_op jit(solution)/shard_map/ppermute | solution.py:31
  75.0 4.2 %collective-permute-done.19 = f32[160,256]{1,0:T(8,128)S(1)} collective-permute-done((f32[160,256]{1,0:T(8,128)S(1)}, f32[160,256]{1,0:T(8,128)S(1)}, u32[]{:S(2)}, u32[]{:S(2)}) %collective-permute-start.19) | collective-permute-done | bytes 163872 | tf_op jit(solution)/shard_map/ppermute | solution.py:31
  80.4 6.3 %collective-permute-start.20 = (f32[160,256]{1,0:T(8,128)S(1)}, f32[160,256]{1,0:T(8,128)S(1)}, u32[]{:S(2)}, u32[]{:S(2)}) collective-permute-start(f32[160,256]{1,0:T(8,128)S(1)} %fusion.33), channel_id=1, source_target_pairs={{0,4},{4,0},{1,5},{5,1},{2,6},{6,2},{3,7},{7,3},{8,12},{12,8},{9,1... | collective-permute-start | bytes 491528 | tf_op jit(solution)/shard_map/ppermute | solution.py:31
  87.2 2.8 %collective-permute-start.31 = (f32[160,256]{1,0:T(8,128)S(1)}, f32[160,256]{1,0:T(8,128)S(1)}, u32[]{:S(2)}, u32[]{:S(2)}) collective-permute-start(f32[160,256]{1,0:T(8,128)S(1)} %fusion.31), channel_id=1, source_target_pairs={{0,16},{16,0},{1,17},{17,1},{2,18},{18,2},{3,19},{19,3},{4,20},{20... | collective-permute-start | bytes 491528 | tf_op jit(solution)/shard_map/ppermute | solution.py:31
  90.3 5.7 %collective-permute-start.21 = (f32[2,160,256]{2,1,0:T(8,128)S(1)}, f32[2,160,256]{2,1,0:T(8,128)S(1)}, u32[]{:S(2)}, u32[]{:S(2)}) collective-permute-start(f32[2,160,256]{2,1,0:T(8,128)S(1)} %pad_maximum_fusion.12), channel_id=1, source_target_pairs={{0,1},{1,0},{2,3},{3,2},{4,5},{5,4},{6,7},{7,6},{8,9},{9,8},{10,11... | collective-permute-start | bytes 983048 | tf_op jit(solution)/shard_map/ppermute | solution.py:31
  96.0 3.5 %collective-permute-start.22 = (f32[2,160,256]{2,1,0:T(8,128)S(1)}, f32[2,160,256]{2,1,0:T(8,128)S(1)}, u32[]{:S(2)}, u32[]{:S(2)}) collective-permute-start(f32[2,160,256]{2,1,0:T(8,128)S(1)} %pad_maximum_fusion.12), channel_id=1, source_target_pairs={{0,3},{1,2},{2,1},{3,0},{4,7},{5,6},{6,5},{7,4},{8,11},{9,10},{10,... | collective-permute-start | bytes 983048 | tf_op jit(solution)/shard_map/ppermute | solution.py:31
  99.5 1.4 collective-permute-start.23
  101.1 1.9 %collective-permute-start.32 = (f32[2,160,256]{2,1,0:T(8,128)S(1)}, f32[2,160,256]{2,1,0:T(8,128)S(1)}, u32[]{:S(2)}, u32[]{:S(2)}) collective-permute-start(f32[2,160,256]{2,1,0:T(8,128)S(1)} %pad_maximum_fusion.14), channel_id=1, source_target_pairs={{0,32},{32,0},{64,96},{96,64},{1,33},{33,1},{65,97},{97,65},{2,34}... | collective-permute-start | bytes 983048 | tf_op jit(solution)/shard_map/ppermute | solution.py:31
  103.2 1.4 collective-permute-done.21
  104.6 1.2 collective-permute-start.34
  105.8 4.2 %collective-permute-done.22 = f32[2,160,256]{2,1,0:T(8,128)S(1)} collective-permute-done((f32[2,160,256]{2,1,0:T(8,128)S(1)}, f32[2,160,256]{2,1,0:T(8,128)S(1)}, u32[]{:S(2)}, u32[]{:S(2)}) %collective-permute-start.22) | collective-permute-done | bytes 327712 | tf_op jit(solution)/shard_map/ppermute | solution.py:31
  110.0 1.8 %collective-permute-done.23 = f32[2,160,256]{2,1,0:T(8,128)S(1)} collective-permute-done((f32[2,160,256]{2,1,0:T(8,128)S(1)}, f32[2,160,256]{2,1,0:T(8,128)S(1)}, u32[]{:S(2)}, u32[]{:S(2)}) %collective-permute-start.23) | collective-permute-done | bytes 327712 | tf_op jit(solution)/shard_map/ppermute | solution.py:31
  112.1 1.9 %fusion.35 = f32[1280,512]{1,0:T(8,128)S(1)} fusion(bf16[1280,1280]{1,0:T(8,128)(2,1)S(1)} %get-tuple-element.5, bf16[1280,256]{1,0:T(8,128)(2,1)S(1)} %get-tuple-element.12, bf16[1280,256]{1,0:T(8,128)(2,1)S(1)} %get-tuple-element.13), kind=kOutput, calls=%fused_computation.74 | convolution fusion | flops 1680343040 | bytes 7208960 | tf_op jit(solution)/shard_map/dot_general | solution.py:93
  114.0 1.9 %fusion.36 = f32[1280,512]{1,0:T(8,128)S(1)} fusion(bf16[1280,1280]{1,0:T(8,128)(2,1)S(1)} %get-tuple-element.8, bf16[1280,256]{1,0:T(8,128)(2,1)S(1)} %get-tuple-element.12, bf16[1280,256]{1,0:T(8,128)(2,1)S(1)} %get-tuple-element.13), kind=kOutput, calls=%fused_computation.75 | convolution fusion | flops 1680343040 | bytes 7208960 | tf_op jit(solution)/shard_map/dot_general | solution.py:93
  117.9 1.9 %fusion.20 = f32[1280,512]{1,0:T(8,128)S(1)} fusion(bf16[1280,1280]{1,0:T(8,128)(2,1)S(1)} %get-tuple-element.8, bf16[1280,256]{1,0:T(8,128)(2,1)S(1)} %get-tuple-element.19, bf16[1280,256]{1,0:T(8,128)(2,1)S(1)} %get-tuple-element.20), kind=kOutput, calls=%fused_computation.56 | convolution fusion | flops 1680343040 | bytes 7208960 | tf_op jit(solution)/shard_map/dot_general | solution.py:93
  120.9 1.1 fusion.4
  122.4 4.5 %collective-permute-start.25 = (f32[2,160,256]{2,1,0:T(8,128)S(1)}, f32[2,160,256]{2,1,0:T(8,128)S(1)}, u32[]{:S(2)}, u32[]{:S(2)}) collective-permute-start(f32[2,160,256]{2,1,0:T(8,128)S(1)} %get-tuple-element.9), channel_id=1, source_target_pairs={{0,64},{32,96},{64,0},{96,32},{1,65},{33,97},{65,1},{97,33},{2,66}... | collective-permute-start | bytes 983048 | tf_op jit(solution)/shard_map/ppermute | solution.py:31
  127.1 1.9 %fusion.24 = f32[1280,512]{1,0:T(8,128)S(1)} fusion(bf16[1280,1280]{1,0:T(8,128)(2,1)S(1)} %get-tuple-element.5, bf16[1280,256]{1,0:T(8,128)(2,1)S(1)} %get-tuple-element.17, bf16[1280,256]{1,0:T(8,128)(2,1)S(1)} %get-tuple-element.18), kind=kOutput, calls=%fused_computation.60 | convolution fusion | flops 1680343040 | bytes 7208960 | tf_op jit(solution)/shard_map/dot_general | solution.py:93
  130.2 1.9 %collective-permute-start.38 = (f32[2,160,256]{2,1,0:T(8,128)S(1)}, f32[2,160,256]{2,1,0:T(8,128)S(1)}, u32[]{:S(2)}, u32[]{:S(2)}) collective-permute-start(f32[2,160,256]{2,1,0:T(8,128)S(1)} %get-tuple-element.15), channel_id=1, source_target_pairs={{0,3},{1,2},{2,1},{3,0},{4,7},{5,6},{6,5},{7,4},{8,11},{9,10},{10,... | collective-permute-start | bytes 983048 | tf_op jit(solution)/shard_map/ppermute | solution.py:31
  133.1 1.9 %collective-permute-start.36 = (f32[2,160,256]{2,1,0:T(8,128)S(1)}, f32[2,160,256]{2,1,0:T(8,128)S(1)}, u32[]{:S(2)}, u32[]{:S(2)}) collective-permute-start(f32[2,160,256]{2,1,0:T(8,128)S(1)} %get-tuple-element.14), channel_id=1, source_target_pairs={{0,2},{1,3},{2,0},{3,1},{4,6},{5,7},{6,4},{7,5},{8,10},{9,11},{10,... | collective-permute-start | bytes 983048 | tf_op jit(solution)/shard_map/ppermute | solution.py:31
  135.0 6.3 %collective-permute-done.25 = f32[2,160,256]{2,1,0:T(8,128)S(1)} collective-permute-done((f32[2,160,256]{2,1,0:T(8,128)S(1)}, f32[2,160,256]{2,1,0:T(8,128)S(1)}, u32[]{:S(2)}, u32[]{:S(2)}) %collective-permute-start.25) | collective-permute-done | bytes 327712 | tf_op jit(solution)/shard_map/ppermute | solution.py:31
  142.1 3.8 %collective-permute-start.29 = (f32[160,256]{1,0:T(8,128)S(1)}, f32[160,256]{1,0:T(8,128)S(1)}, u32[]{:S(2)}, u32[]{:S(2)}) collective-permute-start(f32[160,256]{1,0:T(8,128)S(1)} %get-tuple-element.39), channel_id=1, source_target_pairs={{16,0},{80,1},{48,2},{112,3},{0,4},{64,5},{32,6},{96,7},{24,8},{88... | collective-permute-start | bytes 491528 | tf_op jit(solution)/shard_map/ppermute | solution.py:84
  145.9 6.2 %collective-permute-done.36 = f32[2,160,256]{2,1,0:T(8,128)S(1)} collective-permute-done((f32[2,160,256]{2,1,0:T(8,128)S(1)}, f32[2,160,256]{2,1,0:T(8,128)S(1)}, u32[]{:S(2)}, u32[]{:S(2)}) %collective-permute-start.36) | collective-permute-done | bytes 327712 | tf_op jit(solution)/shard_map/ppermute | solution.py:31
  152.3 5.3 %collective-permute-done.39 = f32[160,256]{1,0:T(8,128)S(1)} collective-permute-done((f32[160,256]{1,0:T(8,128)S(1)}, f32[160,256]{1,0:T(8,128)S(1)}, u32[]{:S(2)}, u32[]{:S(2)}) %collective-permute-start.39) | collective-permute-done | bytes 163872 | tf_op jit(solution)/shard_map/ppermute | solution.py:31
  (112 shorter events, 19.5 us)
Async XLA Ops:
  0.0 12.5 %collective-permute-start.10 = (f32[160,256]{1,0:T(8,128)}, f32[160,256]{1,0:T(8,128)S(1)}, u32[]{:S(2)}, u32[]{:S(2)}) collective-permute-start(f32[160,256]{1,0:T(8,128)} %param.5), channel_id=1, source_target_pairs={{0,0},{1,64},{2,32},{3,96},{4,16},{5,80},{6,48},{7,112},{8,8},{9,7... | collective-permute-start | bytes 491528 | tf_op jit(solution)/shard_map/ppermute | solution.py:84
  1.6 13.7 %collective-permute-start = (f32[160,256]{1,0:T(8,128)}, f32[160,256]{1,0:T(8,128)S(1)}, u32[]{:S(2)}, u32[]{:S(2)}) collective-permute-start(f32[160,256]{1,0:T(8,128)} %param.5), channel_id=1, source_target_pairs={{0,4},{4,0},{1,5},{5,1},{2,6},{6,2},{3,7},{7,3},{8,12},{12,8},{9,1... | collective-permute-start | bytes 491528 | tf_op jit(solution)/shard_map/ppermute | solution.py:31
  6.6 5.9 %copy-start.1 = (f32[2,256]{1,0:T(2,128)S(1)}, f32[2,256]{1,0:T(2,128)}, u32[]{:S(2)}) copy-start(f32[2,256]{1,0:T(2,128)} %param.7) | copy-start | bytes 6148
  6.6 8.7 %copy-start = (f32[160,256]{1,0:T(8,128)S(1)}, f32[160,256]{1,0:T(8,128)}, u32[]{:S(2)}) copy-start(f32[160,256]{1,0:T(8,128)} %param.5) | copy-start | bytes 491524
  12.5 10.7 %collective-permute-start.11 = (f32[160,256]{1,0:T(8,128)S(1)}, f32[160,256]{1,0:T(8,128)S(1)}, u32[]{:S(2)}, u32[]{:S(2)}) collective-permute-start(f32[160,256]{1,0:T(8,128)S(1)} %collective-permute-done.10), channel_id=1, source_target_pairs={{0,16},{16,0},{1,17},{17,1},{2,18},{18,2},{3,19},{19,3},{4,20},{20... | collective-permute-start | bytes 491528 | tf_op jit(solution)/shard_map/ppermute | solution.py:31
  15.4 12.5 %collective-permute-start.1 = (f32[2,160,256]{2,1,0:T(8,128)S(1)}, f32[2,160,256]{2,1,0:T(8,128)S(1)}, u32[]{:S(2)}, u32[]{:S(2)}) collective-permute-start(f32[2,160,256]{2,1,0:T(8,128)S(1)} %pad_maximum_fusion.9), channel_id=1, source_target_pairs={{0,1},{1,0},{2,3},{3,2},{4,5},{5,4},{6,7},{7,6},{8,9},{9,8},{10,11... | collective-permute-start | bytes 983048 | tf_op jit(solution)/shard_map/ppermute | solution.py:31
  19.3 15.5 %collective-permute-start.2 = (f32[2,160,256]{2,1,0:T(8,128)S(1)}, f32[2,160,256]{2,1,0:T(8,128)S(1)}, u32[]{:S(2)}, u32[]{:S(2)}) collective-permute-start(f32[2,160,256]{2,1,0:T(8,128)S(1)} %pad_maximum_fusion.9), channel_id=1, source_target_pairs={{0,3},{1,2},{2,1},{3,0},{4,7},{5,6},{6,5},{7,4},{8,11},{9,10},{10,... | collective-permute-start | bytes 983048 | tf_op jit(solution)/shard_map/ppermute | solution.py:31
  21.7 15.0 %collective-permute-start.3 = (f32[2,160,256]{2,1,0:T(8,128)S(1)}, f32[2,160,256]{2,1,0:T(8,128)S(1)}, u32[]{:S(2)}, u32[]{:S(2)}) collective-permute-start(f32[2,160,256]{2,1,0:T(8,128)S(1)} %pad_maximum_fusion.9), channel_id=1, source_target_pairs={{0,2},{1,3},{2,0},{3,1},{4,6},{5,7},{6,4},{7,5},{8,10},{9,11},{10,... | collective-permute-start | bytes 983048 | tf_op jit(solution)/shard_map/ppermute | solution.py:31
  23.3 18.5 %collective-permute-start.12 = (f32[2,160,256]{2,1,0:T(8,128)S(1)}, f32[2,160,256]{2,1,0:T(8,128)S(1)}, u32[]{:S(2)}, u32[]{:S(2)}) collective-permute-start(f32[2,160,256]{2,1,0:T(8,128)S(1)} %pad_maximum_fusion.10), channel_id=1, source_target_pairs={{0,32},{32,0},{64,96},{96,64},{1,33},{33,1},{65,97},{97,65},{2,34}... | collective-permute-start | bytes 983048 | tf_op jit(solution)/shard_map/ppermute | solution.py:31
  25.5 16.3 %collective-permute-start.13 = (f32[2,160,256]{2,1,0:T(8,128)S(1)}, f32[2,160,256]{2,1,0:T(8,128)S(1)}, u32[]{:S(2)}, u32[]{:S(2)}) collective-permute-start(f32[2,160,256]{2,1,0:T(8,128)S(1)} %pad_maximum_fusion.10), channel_id=1, source_target_pairs={{0,96},{32,64},{64,32},{96,0},{1,97},{33,65},{65,33},{97,1},{2,98}... | collective-permute-start | bytes 983048 | tf_op jit(solution)/shard_map/ppermute | solution.py:31
  27.9 14.0 %collective-permute-start.14 = (f32[2,160,256]{2,1,0:T(8,128)S(1)}, f32[2,160,256]{2,1,0:T(8,128)S(1)}, u32[]{:S(2)}, u32[]{:S(2)}) collective-permute-start(f32[2,160,256]{2,1,0:T(8,128)S(1)} %pad_maximum_fusion.10), channel_id=1, source_target_pairs={{0,64},{32,96},{64,0},{96,32},{1,65},{33,97},{65,1},{97,33},{2,66}... | collective-permute-start | bytes 983048 | tf_op jit(solution)/shard_map/ppermute | solution.py:31
  39.8 6.1 %collective-permute-start.4 = (f32[1280,256]{1,0:T(8,128)S(1)}, f32[1280,256]{1,0:T(8,128)S(1)}, u32[]{:S(2)}, u32[]{:S(2)}) collective-permute-start(f32[1280,256]{1,0:T(8,128)S(1)} %convolution_add_fusion.6), channel_id=1, source_target_pairs={{0,8},{8,0},{1,9},{9,1},{2,10},{10,2},{3,11},{11,3},{4,12},{12,4},... | collective-permute-start | bytes 3932168 | tf_op jit(solution)/shard_map/ppermute | solution.py:75
  41.9 10.0 %collective-permute-start.15 = (f32[1280,256]{1,0:T(8,128)S(1)}, f32[1280,256]{1,0:T(8,128)S(1)}, u32[]{:S(2)}, u32[]{:S(2)}) collective-permute-start(f32[1280,256]{1,0:T(8,128)S(1)} %bitcast.205), channel_id=1, source_target_pairs={{0,8},{8,0},{1,9},{9,1},{2,10},{10,2},{3,11},{11,3},{4,12},{12,4},... | collective-permute-start | bytes 3932168 | tf_op jit(solution)/shard_map/ppermute | solution.py:75
  47.1 11.0 %collective-permute-start.7 = (f32[2,160,256]{2,1,0:T(8,128)S(1)}, f32[2,160,256]{2,1,0:T(8,128)S(1)}, u32[]{:S(2)}, u32[]{:S(2)}) collective-permute-start(f32[2,160,256]{2,1,0:T(8,128)S(1)} %get-tuple-element.22), channel_id=1, source_target_pairs={{0,96},{32,64},{64,32},{96,0},{1,97},{33,65},{65,33},{97,1},{2,98}... | collective-permute-start | bytes 983048 | tf_op jit(solution)/shard_map/ppermute | solution.py:31
  49.9 10.6 %collective-permute-start.6 = (f32[2,160,256]{2,1,0:T(8,128)S(1)}, f32[2,160,256]{2,1,0:T(8,128)S(1)}, u32[]{:S(2)}, u32[]{:S(2)}) collective-permute-start(f32[2,160,256]{2,1,0:T(8,128)S(1)} %get-tuple-element.23), channel_id=1, source_target_pairs={{0,32},{32,0},{64,96},{96,64},{1,33},{33,1},{65,97},{97,65},{2,34}... | collective-permute-start | bytes 983048 | tf_op jit(solution)/shard_map/ppermute | solution.py:31
  49.9 16.4 %collective-permute-start.5 = (f32[2,160,256]{2,1,0:T(8,128)S(1)}, f32[2,160,256]{2,1,0:T(8,128)S(1)}, u32[]{:S(2)}, u32[]{:S(2)}) collective-permute-start(f32[2,160,256]{2,1,0:T(8,128)S(1)} %get-tuple-element.21), channel_id=1, source_target_pairs={{0,64},{32,96},{64,0},{96,32},{1,65},{33,97},{65,1},{97,33},{2,66}... | collective-permute-start | bytes 983048 | tf_op jit(solution)/shard_map/ppermute | solution.py:31
  55.2 12.6 %collective-permute-start.18 = (f32[2,160,256]{2,1,0:T(8,128)S(1)}, f32[2,160,256]{2,1,0:T(8,128)S(1)}, u32[]{:S(2)}, u32[]{:S(2)}) collective-permute-start(f32[2,160,256]{2,1,0:T(8,128)S(1)} %get-tuple-element.27), channel_id=1, source_target_pairs={{0,3},{1,2},{2,1},{3,0},{4,7},{5,6},{6,5},{7,4},{8,11},{9,10},{10,... | collective-permute-start | bytes 983048 | tf_op jit(solution)/shard_map/ppermute | solution.py:31
  57.2 10.6 %collective-permute-start.17 = (f32[2,160,256]{2,1,0:T(8,128)S(1)}, f32[2,160,256]{2,1,0:T(8,128)S(1)}, u32[]{:S(2)}, u32[]{:S(2)}) collective-permute-start(f32[2,160,256]{2,1,0:T(8,128)S(1)} %get-tuple-element.28), channel_id=1, source_target_pairs={{0,1},{1,0},{2,3},{3,2},{4,5},{5,4},{6,7},{7,6},{8,9},{9,8},{10,11... | collective-permute-start | bytes 983048 | tf_op jit(solution)/shard_map/ppermute | solution.py:31
  58.1 15.4 %collective-permute-start.16 = (f32[2,160,256]{2,1,0:T(8,128)S(1)}, f32[2,160,256]{2,1,0:T(8,128)S(1)}, u32[]{:S(2)}, u32[]{:S(2)}) collective-permute-start(f32[2,160,256]{2,1,0:T(8,128)S(1)} %get-tuple-element.26), channel_id=1, source_target_pairs={{0,2},{1,3},{2,0},{3,1},{4,6},{5,7},{6,4},{7,5},{8,10},{9,11},{10,... | collective-permute-start | bytes 983048 | tf_op jit(solution)/shard_map/ppermute | solution.py:31
  66.4 7.9 %collective-permute-start.8 = (f32[160,256]{1,0:T(8,128)S(1)}, f32[160,256]{1,0:T(8,128)S(1)}, u32[]{:S(2)}, u32[]{:S(2)}) collective-permute-start(f32[160,256]{1,0:T(8,128)S(1)} %select_bitcast_fusion.10), channel_id=1, source_target_pairs={{0,16},{16,0},{1,17},{17,1},{2,18},{18,2},{3,19},{19,3},{4,20},{20... | collective-permute-start | bytes 491528 | tf_op jit(solution)/shard_map/ppermute | solution.py:31
  73.6 5.6 %collective-permute-start.19 = (f32[160,256]{1,0:T(8,128)S(1)}, f32[160,256]{1,0:T(8,128)S(1)}, u32[]{:S(2)}, u32[]{:S(2)}) collective-permute-start(f32[160,256]{1,0:T(8,128)S(1)} %select_bitcast_fusion.7), channel_id=1, source_target_pairs={{0,4},{4,0},{1,5},{5,1},{2,6},{6,2},{3,7},{7,3},{8,12},{12,8},{9,1... | collective-permute-start | bytes 491528 | tf_op jit(solution)/shard_map/ppermute | solution.py:31
  74.3 5.6 %collective-permute-start.9 = (f32[160,256]{1,0:T(8,128)S(1)}, f32[160,256]{1,0:T(8,128)S(1)}, u32[]{:S(2)}, u32[]{:S(2)}) collective-permute-start(f32[160,256]{1,0:T(8,128)S(1)} %bitcast_add_fusion.6), channel_id=1, source_target_pairs={{0,0},{64,1},{32,2},{96,3},{16,4},{80,5},{48,6},{112,7},{8,8},{72,... | collective-permute-start | bytes 491528 | tf_op jit(solution)/shard_map/ppermute | solution.py:84
  79.2 7.4 %collective-permute-start.30 = (f32[160,256]{1,0:T(8,128)S(1)}, f32[160,256]{1,0:T(8,128)S(1)}, u32[]{:S(2)}, u32[]{:S(2)}) collective-permute-start(f32[160,256]{1,0:T(8,128)S(1)} %bitcast_add_fusion.5), channel_id=1, source_target_pairs={{0,0},{1,64},{2,32},{3,96},{4,16},{5,80},{6,48},{7,112},{8,8},{9,7... | collective-permute-start | bytes 491528 | tf_op jit(solution)/shard_map/ppermute | solution.py:84
  80.4 9.8 %collective-permute-start.20 = (f32[160,256]{1,0:T(8,128)S(1)}, f32[160,256]{1,0:T(8,128)S(1)}, u32[]{:S(2)}, u32[]{:S(2)}) collective-permute-start(f32[160,256]{1,0:T(8,128)S(1)} %fusion.33), channel_id=1, source_target_pairs={{0,4},{4,0},{1,5},{5,1},{2,6},{6,2},{3,7},{7,3},{8,12},{12,8},{9,1... | collective-permute-start | bytes 491528 | tf_op jit(solution)/shard_map/ppermute | solution.py:31
  87.2 13.9 %collective-permute-start.31 = (f32[160,256]{1,0:T(8,128)S(1)}, f32[160,256]{1,0:T(8,128)S(1)}, u32[]{:S(2)}, u32[]{:S(2)}) collective-permute-start(f32[160,256]{1,0:T(8,128)S(1)} %fusion.31), channel_id=1, source_target_pairs={{0,16},{16,0},{1,17},{17,1},{2,18},{18,2},{3,19},{19,3},{4,20},{20... | collective-permute-start | bytes 491528 | tf_op jit(solution)/shard_map/ppermute | solution.py:31
  90.3 14.3 %collective-permute-start.21 = (f32[2,160,256]{2,1,0:T(8,128)S(1)}, f32[2,160,256]{2,1,0:T(8,128)S(1)}, u32[]{:S(2)}, u32[]{:S(2)}) collective-permute-start(f32[2,160,256]{2,1,0:T(8,128)S(1)} %pad_maximum_fusion.12), channel_id=1, source_target_pairs={{0,1},{1,0},{2,3},{3,2},{4,5},{5,4},{6,7},{7,6},{8,9},{9,8},{10,11... | collective-permute-start | bytes 983048 | tf_op jit(solution)/shard_map/ppermute | solution.py:31
  96.0 14.0 %collective-permute-start.22 = (f32[2,160,256]{2,1,0:T(8,128)S(1)}, f32[2,160,256]{2,1,0:T(8,128)S(1)}, u32[]{:S(2)}, u32[]{:S(2)}) collective-permute-start(f32[2,160,256]{2,1,0:T(8,128)S(1)} %pad_maximum_fusion.12), channel_id=1, source_target_pairs={{0,3},{1,2},{2,1},{3,0},{4,7},{5,6},{6,5},{7,4},{8,11},{9,10},{10,... | collective-permute-start | bytes 983048 | tf_op jit(solution)/shard_map/ppermute | solution.py:31
  99.5 12.3 %collective-permute-start.23 = (f32[2,160,256]{2,1,0:T(8,128)S(1)}, f32[2,160,256]{2,1,0:T(8,128)S(1)}, u32[]{:S(2)}, u32[]{:S(2)}) collective-permute-start(f32[2,160,256]{2,1,0:T(8,128)S(1)} %pad_maximum_fusion.12), channel_id=1, source_target_pairs={{0,2},{1,3},{2,0},{3,1},{4,6},{5,7},{6,4},{7,5},{8,10},{9,11},{10,... | collective-permute-start | bytes 983048 | tf_op jit(solution)/shard_map/ppermute | solution.py:31
  101.1 15.9 %collective-permute-start.32 = (f32[2,160,256]{2,1,0:T(8,128)S(1)}, f32[2,160,256]{2,1,0:T(8,128)S(1)}, u32[]{:S(2)}, u32[]{:S(2)}) collective-permute-start(f32[2,160,256]{2,1,0:T(8,128)S(1)} %pad_maximum_fusion.14), channel_id=1, source_target_pairs={{0,32},{32,0},{64,96},{96,64},{1,33},{33,1},{65,97},{97,65},{2,34}... | collective-permute-start | bytes 983048 | tf_op jit(solution)/shard_map/ppermute | solution.py:31
  103.0 14.0 %collective-permute-start.33 = (f32[2,160,256]{2,1,0:T(8,128)S(1)}, f32[2,160,256]{2,1,0:T(8,128)S(1)}, u32[]{:S(2)}, u32[]{:S(2)}) collective-permute-start(f32[2,160,256]{2,1,0:T(8,128)S(1)} %pad_maximum_fusion.14), channel_id=1, source_target_pairs={{0,96},{32,64},{64,32},{96,0},{1,97},{33,65},{65,33},{97,1},{2,98}... | collective-permute-start | bytes 983048 | tf_op jit(solution)/shard_map/ppermute | solution.py:31
  104.6 12.5 %collective-permute-start.34 = (f32[2,160,256]{2,1,0:T(8,128)S(1)}, f32[2,160,256]{2,1,0:T(8,128)S(1)}, u32[]{:S(2)}, u32[]{:S(2)}) collective-permute-start(f32[2,160,256]{2,1,0:T(8,128)S(1)} %pad_maximum_fusion.14), channel_id=1, source_target_pairs={{0,64},{32,96},{64,0},{96,32},{1,65},{33,97},{65,1},{97,33},{2,66}... | collective-permute-start | bytes 983048 | tf_op jit(solution)/shard_map/ppermute | solution.py:31
  116.9 4.0 %collective-permute-start.24 = (f32[1280,256]{1,0:T(8,128)S(1)}, f32[1280,256]{1,0:T(8,128)S(1)}, u32[]{:S(2)}, u32[]{:S(2)}) collective-permute-start(f32[1280,256]{1,0:T(8,128)S(1)} %convolution_add_fusion.2), channel_id=1, source_target_pairs={{0,8},{8,0},{1,9},{9,1},{2,10},{10,2},{3,11},{11,3},{4,12},{12,4},... | collective-permute-start | bytes 3932168 | tf_op jit(solution)/shard_map/ppermute | solution.py:75
  117.1 9.8 %collective-permute-start.35 = (f32[1280,256]{1,0:T(8,128)S(1)}, f32[1280,256]{1,0:T(8,128)S(1)}, u32[]{:S(2)}, u32[]{:S(2)}) collective-permute-start(f32[1280,256]{1,0:T(8,128)S(1)} %bitcast.204), channel_id=1, source_target_pairs={{0,8},{8,0},{1,9},{9,1},{2,10},{10,2},{3,11},{11,3},{4,12},{12,4},... | collective-permute-start | bytes 3932168 | tf_op jit(solution)/shard_map/ppermute | solution.py:75
  122.1 11.0 %collective-permute-start.27 = (f32[2,160,256]{2,1,0:T(8,128)S(1)}, f32[2,160,256]{2,1,0:T(8,128)S(1)}, u32[]{:S(2)}, u32[]{:S(2)}) collective-permute-start(f32[2,160,256]{2,1,0:T(8,128)S(1)} %get-tuple-element.10), channel_id=1, source_target_pairs={{0,96},{32,64},{64,32},{96,0},{1,97},{33,65},{65,33},{97,1},{2,98}... | collective-permute-start | bytes 983048 | tf_op jit(solution)/shard_map/ppermute | solution.py:31
  122.2 12.8 %collective-permute-start.26 = (f32[2,160,256]{2,1,0:T(8,128)S(1)}, f32[2,160,256]{2,1,0:T(8,128)S(1)}, u32[]{:S(2)}, u32[]{:S(2)}) collective-permute-start(f32[2,160,256]{2,1,0:T(8,128)S(1)} %get-tuple-element.11), channel_id=1, source_target_pairs={{0,32},{32,0},{64,96},{96,64},{1,33},{33,1},{65,97},{97,65},{2,34}... | collective-permute-start | bytes 983048 | tf_op jit(solution)/shard_map/ppermute | solution.py:31
  122.4 18.9 %collective-permute-start.25 = (f32[2,160,256]{2,1,0:T(8,128)S(1)}, f32[2,160,256]{2,1,0:T(8,128)S(1)}, u32[]{:S(2)}, u32[]{:S(2)}) collective-permute-start(f32[2,160,256]{2,1,0:T(8,128)S(1)} %get-tuple-element.9), channel_id=1, source_target_pairs={{0,64},{32,96},{64,0},{96,32},{1,65},{33,97},{65,1},{97,33},{2,66}... | collective-permute-start | bytes 983048 | tf_op jit(solution)/shard_map/ppermute | solution.py:31
  130.2 15.7 %collective-permute-start.38 = (f32[2,160,256]{2,1,0:T(8,128)S(1)}, f32[2,160,256]{2,1,0:T(8,128)S(1)}, u32[]{:S(2)}, u32[]{:S(2)}) collective-permute-start(f32[2,160,256]{2,1,0:T(8,128)S(1)} %get-tuple-element.15), channel_id=1, source_target_pairs={{0,3},{1,2},{2,1},{3,0},{4,7},{5,6},{6,5},{7,4},{8,11},{9,10},{10,... | collective-permute-start | bytes 983048 | tf_op jit(solution)/shard_map/ppermute | solution.py:31
  132.1 13.8 %collective-permute-start.37 = (f32[2,160,256]{2,1,0:T(8,128)S(1)}, f32[2,160,256]{2,1,0:T(8,128)S(1)}, u32[]{:S(2)}, u32[]{:S(2)}) collective-permute-start(f32[2,160,256]{2,1,0:T(8,128)S(1)} %get-tuple-element.16), channel_id=1, source_target_pairs={{0,1},{1,0},{2,3},{3,2},{4,5},{5,4},{6,7},{7,6},{8,9},{9,8},{10,11... | collective-permute-start | bytes 983048 | tf_op jit(solution)/shard_map/ppermute | solution.py:31
  133.1 19.0 %collective-permute-start.36 = (f32[2,160,256]{2,1,0:T(8,128)S(1)}, f32[2,160,256]{2,1,0:T(8,128)S(1)}, u32[]{:S(2)}, u32[]{:S(2)}) collective-permute-start(f32[2,160,256]{2,1,0:T(8,128)S(1)} %get-tuple-element.14), channel_id=1, source_target_pairs={{0,2},{1,3},{2,0},{3,1},{4,6},{5,7},{6,4},{7,5},{8,10},{9,11},{10,... | collective-permute-start | bytes 983048 | tf_op jit(solution)/shard_map/ppermute | solution.py:31
  141.4 10.9 %collective-permute-start.28 = (f32[160,256]{1,0:T(8,128)S(1)}, f32[160,256]{1,0:T(8,128)S(1)}, u32[]{:S(2)}, u32[]{:S(2)}) collective-permute-start(f32[160,256]{1,0:T(8,128)S(1)} %get-tuple-element.40), channel_id=1, source_target_pairs={{0,0},{64,1},{32,2},{96,3},{16,4},{80,5},{48,6},{112,7},{8,8},{72,... | collective-permute-start | bytes 491528 | tf_op jit(solution)/shard_map/ppermute | solution.py:84
  142.1 10.2 %collective-permute-start.29 = (f32[160,256]{1,0:T(8,128)S(1)}, f32[160,256]{1,0:T(8,128)S(1)}, u32[]{:S(2)}, u32[]{:S(2)}) collective-permute-start(f32[160,256]{1,0:T(8,128)S(1)} %get-tuple-element.39), channel_id=1, source_target_pairs={{16,0},{80,1},{48,2},{112,3},{0,4},{64,5},{32,6},{96,7},{24,8},{88... | collective-permute-start | bytes 491528 | tf_op jit(solution)/shard_map/ppermute | solution.py:84
  152.2 5.4 %collective-permute-start.39 = (f32[160,256]{1,0:T(8,128)S(1)}, f32[160,256]{1,0:T(8,128)S(1)}, u32[]{:S(2)}, u32[]{:S(2)}) collective-permute-start(f32[160,256]{1,0:T(8,128)S(1)} %select_bitcast_fusion), channel_id=1, source_target_pairs={{0,4},{4,0},{1,5},{5,1},{2,6},{6,2},{3,7},{7,3},{8,12},{12,8},{9,1... | collective-permute-start | bytes 491528 | tf_op jit(solution)/shard_map/ppermute | solution.py:31

commit v3 on v2

--- a/solution.py
+++ b/solution.py
@@ -31,7 +31,7 @@
     return lax.ppermute(value, axis, [(i, i ^ step) for i in range(SIZE[axis])])
 
 
-def gather(block, short, ring, got=None):
+def gather(block, short, ring, name, got=None):
     rows, width = block.shape
     me = lax.axis_index(ring)
     in_pair, place = places(short)
@@ -41,7 +41,7 @@
     both = jnp.stack([jnp.where(first, block, got), jnp.where(first, got, block)])
     whole = jnp.zeros((2, 4, rows, width), block.dtype)
     whole = lax.dynamic_update_slice(whole, both[:, None], (0, place(me), 0, 0))
-    for step in (1, 3, 2):
+    for step in ((1, 3, 2) if name == "row" else (2, 1, 3)):
         got = swap(both, ring, step)
         whole = lax.dynamic_update_slice(whole, got[:, None], (0, place(me ^ step), 0, 0))
     return whole.reshape(-1, width)
@@ -111,8 +111,8 @@
             stacked = split(layer_weights.reshape(LAYERS, -1, layer_weights.shape[-1]))
             own = split(lax.dynamic_slice_in_dim(adjacency, core * half, half, 0))
             other = split(lax.dynamic_slice_in_dim(adjacency, (1 - core) * half, half, 0))
-        source_rows = split(gather(row_block, "xl", "y"))
-        own_rows = gather(column_block, "xh", "z")
+        source_rows = split(gather(row_block, "xl", "y", "row"))
+        own_rows = gather(column_block, "xh", "z", "column")
         other_rows = exchange_cores(own_rows)
         other_rows = split(other_rows)
         own_rows = split(own_rows)

time: 159 us -> 158 us (level)
  waiting for transfers between devices: 48.7 us -> 46.5 us
  starting transfers between devices: 73 us -> 74.7 us
    ppermute x31, waiting for transfers between devices: 48.7 us -> 46.4 us  [swap(): return lax.ppermute(value, axis, [(i, i ^ step) for i in range(SIZE[axis])])]
    ppermute x31, starting transfers between devices: 64.1 us -> 66.1 us  [swap(): return lax.ppermute(value, axis, [(i, i ^ step) for i in range(SIZE[axis])])]
where the time goes in v3:
time: 158 us
  starting transfers between devices  74.7 us (47%)
  waiting for transfers between devices  46.5 us (29%)
  matrix products  25.7 us (16%)
  other arithmetic  9.28 us (6%)
    ppermute x31, starting transfers between devices, swap(): return lax.ppermute(value, axis, [(i, i ^ step) for i in range(SIZE[axis])])  66.1 us
    ppermute x31, waiting for transfers between devices, swap(): return lax.ppermute(value, axis, [(i, i ^ step) for i in range(SIZE[axis])])  46.4 us
    dot_general x22, matrix products, product(): lax.dot_general(a, b, (dims, ((), ())), preferred_element_type=jnp.float32)  25.7 us
    convert_element_type x8, other arithmetic, split(): return (high.astype(jnp.bfloat16), (value - high).astype(jnp.bfloat16))  8.41 us
    ppermute x5, starting transfers between devices, turn(): return lax.ppermute(value, SRC + DST, pairs)  7.07 us
  transfers between devices with their start and end apart: 40, of which 16 were waited for; matrix products, arithmetic and copies ran while one was open for 22% of the time, Pallas kernels for 0%

profile of v3, /device:TPU:0, one launch (start us, length us, event | category | flops | bytes accessed | tf_op | source)
XLA Modules:
  0.0 158.1 jit_solution(8013277709073165996)
XLA Ops:
  0.0 1.6 collective-permute-start.10
  1.6 3.5 %collective-permute-start = (f32[160,256]{1,0:T(8,128)}, f32[160,256]{1,0:T(8,128)S(1)}, u32[]{:S(2)}, u32[]{:S(2)}) collective-permute-start(f32[160,256]{1,0:T(8,128)} %param.5), channel_id=1, source_target_pairs={{0,4},{4,0},{1,5},{5,1},{2,6},{6,2},{3,7},{7,3},{8,12},{12,8},{9,1... | collective-permute-start | bytes 491528 | tf_op jit(solution)/shard_map/ppermute | solution.py:31
  5.1 1.4 reduce-precision_convert_fusion.8
  6.6 5.8 %reduce-precision_convert_fusion = (bf16[1280,1280]{1,0:T(8,128)(2,1)S(1)}, bf16[1280,1280]{1,0:T(8,128)(2,1)S(1)}, bf16[1280,1280]{1,0:T(8,128)(2,1)S(1)}, bf16[1280,1280]{1,0:T(8,128)(2,1)S(1)}) fusion(f32[2560,1280]{1,0:T(8,128)} %param.4, s32[]{:T(128)S(6)} %select_n.161, s32[]{:T(128)S(6)} %select_n.153), kind=kLoop, calls=%fused_computation.1 | loop fusion | flops 13107200 | bytes 26214408 | tf_op jit(solution)/shard_map/convert_element_type | solution.py:89
  12.5 2.8 %collective-permute-start.11 = (f32[160,256]{1,0:T(8,128)S(1)}, f32[160,256]{1,0:T(8,128)S(1)}, u32[]{:S(2)}, u32[]{:S(2)}) collective-permute-start(f32[160,256]{1,0:T(8,128)S(1)} %collective-permute-done.10), channel_id=1, source_target_pairs={{0,16},{16,0},{1,17},{17,1},{2,18},{18,2},{3,19},{19,3},{4,20},{20... | collective-permute-start | bytes 491528 | tf_op jit(solution)/shard_map/ppermute | solution.py:31
  15.4 4.0 %collective-permute-start.1 = (f32[2,160,256]{2,1,0:T(8,128)S(1)}, f32[2,160,256]{2,1,0:T(8,128)S(1)}, u32[]{:S(2)}, u32[]{:S(2)}) collective-permute-start(f32[2,160,256]{2,1,0:T(8,128)S(1)} %pad_maximum_fusion.9), channel_id=1, source_target_pairs={{0,1},{1,0},{2,3},{3,2},{4,5},{5,4},{6,7},{7,6},{8,9},{9,8},{10,11... | collective-permute-start | bytes 983048 | tf_op jit(solution)/shard_map/ppermute | solution.py:31
  19.3 2.4 %collective-permute-start.2 = (f32[2,160,256]{2,1,0:T(8,128)S(1)}, f32[2,160,256]{2,1,0:T(8,128)S(1)}, u32[]{:S(2)}, u32[]{:S(2)}) collective-permute-start(f32[2,160,256]{2,1,0:T(8,128)S(1)} %pad_maximum_fusion.9), channel_id=1, source_target_pairs={{0,3},{1,2},{2,1},{3,0},{4,7},{5,6},{6,5},{7,4},{8,11},{9,10},{10,... | collective-permute-start | bytes 983048 | tf_op jit(solution)/shard_map/ppermute | solution.py:31
  21.7 1.4 collective-permute-start.3
  23.3 2.7 %collective-permute-start.12 = (f32[2,160,256]{2,1,0:T(8,128)S(1)}, f32[2,160,256]{2,1,0:T(8,128)S(1)}, u32[]{:S(2)}, u32[]{:S(2)}) collective-permute-start(f32[2,160,256]{2,1,0:T(8,128)S(1)} %pad_maximum_fusion.10), channel_id=1, source_target_pairs={{0,64},{32,96},{64,0},{96,32},{1,65},{33,97},{65,1},{97,33},{2,66}... | collective-permute-start | bytes 983048 | tf_op jit(solution)/shard_map/ppermute | solution.py:31
  26.0 1.8 %collective-permute-start.13 = (f32[2,160,256]{2,1,0:T(8,128)S(1)}, f32[2,160,256]{2,1,0:T(8,128)S(1)}, u32[]{:S(2)}, u32[]{:S(2)}) collective-permute-start(f32[2,160,256]{2,1,0:T(8,128)S(1)} %pad_maximum_fusion.10), channel_id=1, source_target_pairs={{0,32},{32,0},{64,96},{96,64},{1,33},{33,1},{65,97},{97,65},{2,34}... | collective-permute-start | bytes 983048 | tf_op jit(solution)/shard_map/ppermute | solution.py:31
  27.9 4.5 %collective-permute-start.14 = (f32[2,160,256]{2,1,0:T(8,128)S(1)}, f32[2,160,256]{2,1,0:T(8,128)S(1)}, u32[]{:S(2)}, u32[]{:S(2)}) collective-permute-start(f32[2,160,256]{2,1,0:T(8,128)S(1)} %pad_maximum_fusion.10), channel_id=1, source_target_pairs={{0,96},{32,64},{64,32},{96,0},{1,97},{33,65},{65,33},{97,1},{2,98}... | collective-permute-start | bytes 983048 | tf_op jit(solution)/shard_map/ppermute | solution.py:31
  32.5 2.4 %collective-permute-done.2 = f32[2,160,256]{2,1,0:T(8,128)S(1)} collective-permute-done((f32[2,160,256]{2,1,0:T(8,128)S(1)}, f32[2,160,256]{2,1,0:T(8,128)S(1)}, u32[]{:S(2)}, u32[]{:S(2)}) %collective-permute-start.2) | collective-permute-done | bytes 327712 | tf_op jit(solution)/shard_map/ppermute | solution.py:31
  34.9 1.8 %collective-permute-done.3 = f32[2,160,256]{2,1,0:T(8,128)S(1)} collective-permute-done((f32[2,160,256]{2,1,0:T(8,128)S(1)}, f32[2,160,256]{2,1,0:T(8,128)S(1)}, u32[]{:S(2)}, u32[]{:S(2)}) %collective-permute-start.3) | collective-permute-done | bytes 327712 | tf_op jit(solution)/shard_map/ppermute | solution.py:31
  36.9 1.9 %fusion.37 = f32[1280,512]{1,0:T(8,128)S(1)} fusion(bf16[1280,1280]{1,0:T(8,128)(2,1)S(1)} %get-tuple-element.5, bf16[1280,256]{1,0:T(8,128)(2,1)S(1)} %get-tuple-element.24, bf16[1280,256]{1,0:T(8,128)(2,1)S(1)} %get-tuple-element.25), kind=kOutput, calls=%fused_computation.76 | convolution fusion | flops 1680343040 | bytes 7208960 | tf_op jit(solution)/shard_map/dot_general | solution.py:93
  39.9 1.9 %fusion.38 = f32[1280,512]{1,0:T(8,128)S(1)} fusion(bf16[1280,1280]{1,0:T(8,128)(2,1)S(1)} %get-tuple-element.8, bf16[1280,256]{1,0:T(8,128)(2,1)S(1)} %get-tuple-element.24, bf16[1280,256]{1,0:T(8,128)(2,1)S(1)} %get-tuple-element.25), kind=kOutput, calls=%fused_computation.77 | convolution fusion | flops 1680343040 | bytes 7208960 | tf_op jit(solution)/shard_map/dot_general | solution.py:93
  42.9 1.9 %fusion.12 = f32[1280,512]{1,0:T(8,128)S(1)} fusion(bf16[1280,1280]{1,0:T(8,128)(2,1)S(1)} %get-tuple-element.8, bf16[1280,256]{1,0:T(8,128)(2,1)S(1)} %get-tuple-element.31, bf16[1280,256]{1,0:T(8,128)(2,1)S(1)} %get-tuple-element.32), kind=kOutput, calls=%fused_computation.47 | convolution fusion | flops 1680343040 | bytes 7208960 | tf_op jit(solution)/shard_map/dot_general | solution.py:93
  44.8 1.1 convolution_add_fusion.5
  45.9 1.1 fusion.2
  47.1 2.7 %collective-permute-start.7 = (f32[2,160,256]{2,1,0:T(8,128)S(1)}, f32[2,160,256]{2,1,0:T(8,128)S(1)}, u32[]{:S(2)}, u32[]{:S(2)}) collective-permute-start(f32[2,160,256]{2,1,0:T(8,128)S(1)} %get-tuple-element.22), channel_id=1, source_target_pairs={{0,96},{32,64},{64,32},{96,0},{1,97},{33,65},{65,33},{97,1},{2,98}... | collective-permute-start | bytes 983048 | tf_op jit(solution)/shard_map/ppermute | solution.py:31
  49.9 2.1 %collective-permute-start.5 = (f32[2,160,256]{2,1,0:T(8,128)S(1)}, f32[2,160,256]{2,1,0:T(8,128)S(1)}, u32[]{:S(2)}, u32[]{:S(2)}) collective-permute-start(f32[2,160,256]{2,1,0:T(8,128)S(1)} %get-tuple-element.21), channel_id=1, source_target_pairs={{0,64},{32,96},{64,0},{96,32},{1,65},{33,97},{65,1},{97,33},{2,66}... | collective-permute-start | bytes 983048 | tf_op jit(solution)/shard_map/ppermute | solution.py:31
  52.1 1.9 %fusion.16 = f32[1280,512]{1,0:T(8,128)S(1)} fusion(bf16[1280,1280]{1,0:T(8,128)(2,1)S(1)} %get-tuple-element.5, bf16[1280,256]{1,0:T(8,128)(2,1)S(1)} %get-tuple-element.29, bf16[1280,256]{1,0:T(8,128)(2,1)S(1)} %get-tuple-element.30), kind=kOutput, calls=%fused_computation.51 | convolution fusion | flops 1680343040 | bytes 7208960 | tf_op jit(solution)/shard_map/dot_general | solution.py:93
  54.0 1.1 fusion.3
  55.2 2.0 %collective-permute-start.18 = (f32[2,160,256]{2,1,0:T(8,128)S(1)}, f32[2,160,256]{2,1,0:T(8,128)S(1)}, u32[]{:S(2)}, u32[]{:S(2)}) collective-permute-start(f32[2,160,256]{2,1,0:T(8,128)S(1)} %get-tuple-element.27), channel_id=1, source_target_pairs={{0,3},{1,2},{2,1},{3,0},{4,7},{5,6},{6,5},{7,4},{8,11},{9,10},{10,... | collective-permute-start | bytes 983048 | tf_op jit(solution)/shard_map/ppermute | solution.py:31
  58.1 1.9 %collective-permute-start.16 = (f32[2,160,256]{2,1,0:T(8,128)S(1)}, f32[2,160,256]{2,1,0:T(8,128)S(1)}, u32[]{:S(2)}, u32[]{:S(2)}) collective-permute-start(f32[2,160,256]{2,1,0:T(8,128)S(1)} %get-tuple-element.26), channel_id=1, source_target_pairs={{0,2},{1,3},{2,0},{3,1},{4,6},{5,7},{6,4},{7,5},{8,10},{9,11},{10,... | collective-permute-start | bytes 983048 | tf_op jit(solution)/shard_map/ppermute | solution.py:31
  60.5 5.8 %collective-permute-done.5 = f32[2,160,256]{2,1,0:T(8,128)S(1)} collective-permute-done((f32[2,160,256]{2,1,0:T(8,128)S(1)}, f32[2,160,256]{2,1,0:T(8,128)S(1)}, u32[]{:S(2)}, u32[]{:S(2)}) %collective-permute-start.5) | collective-permute-done | bytes 327712 | tf_op jit(solution)/shard_map/ppermute | solution.py:31
  67.8 5.7 %collective-permute-done.16 = f32[2,160,256]{2,1,0:T(8,128)S(1)} collective-permute-done((f32[2,160,256]{2,1,0:T(8,128)S(1)}, f32[2,160,256]{2,1,0:T(8,128)S(1)}, u32[]{:S(2)}, u32[]{:S(2)}) %collective-permute-start.16) | collective-permute-done | bytes 327712 | tf_op jit(solution)/shard_map/ppermute | solution.py:31
  75.0 4.3 %collective-permute-done.19 = f32[160,256]{1,0:T(8,128)S(1)} collective-permute-done((f32[160,256]{1,0:T(8,128)S(1)}, f32[160,256]{1,0:T(8,128)S(1)}, u32[]{:S(2)}, u32[]{:S(2)}) %collective-permute-start.19) | collective-permute-done | bytes 163872 | tf_op jit(solution)/shard_map/ppermute | solution.py:31
  80.4 6.3 %collective-permute-start.20 = (f32[160,256]{1,0:T(8,128)S(1)}, f32[160,256]{1,0:T(8,128)S(1)}, u32[]{:S(2)}, u32[]{:S(2)}) collective-permute-start(f32[160,256]{1,0:T(8,128)S(1)} %fusion.33), channel_id=1, source_target_pairs={{0,4},{4,0},{1,5},{5,1},{2,6},{6,2},{3,7},{7,3},{8,12},{12,8},{9,1... | collective-permute-start | bytes 491528 | tf_op jit(solution)/shard_map/ppermute | solution.py:31
  87.2 2.6 %collective-permute-start.31 = (f32[160,256]{1,0:T(8,128)S(1)}, f32[160,256]{1,0:T(8,128)S(1)}, u32[]{:S(2)}, u32[]{:S(2)}) collective-permute-start(f32[160,256]{1,0:T(8,128)S(1)} %fusion.31), channel_id=1, source_target_pairs={{0,16},{16,0},{1,17},{17,1},{2,18},{18,2},{3,19},{19,3},{4,20},{20... | collective-permute-start | bytes 491528 | tf_op jit(solution)/shard_map/ppermute | solution.py:31
  90.4 5.1 %collective-permute-start.21 = (f32[2,160,256]{2,1,0:T(8,128)S(1)}, f32[2,160,256]{2,1,0:T(8,128)S(1)}, u32[]{:S(2)}, u32[]{:S(2)}) collective-permute-start(f32[2,160,256]{2,1,0:T(8,128)S(1)} %pad_maximum_fusion.12), channel_id=1, source_target_pairs={{0,1},{1,0},{2,3},{3,2},{4,5},{5,4},{6,7},{7,6},{8,9},{9,8},{10,11... | collective-permute-start | bytes 983048 | tf_op jit(solution)/shard_map/ppermute | solution.py:31
  95.5 3.4 %collective-permute-start.22 = (f32[2,160,256]{2,1,0:T(8,128)S(1)}, f32[2,160,256]{2,1,0:T(8,128)S(1)}, u32[]{:S(2)}, u32[]{:S(2)}) collective-permute-start(f32[2,160,256]{2,1,0:T(8,128)S(1)} %pad_maximum_fusion.12), channel_id=1, source_target_pairs={{0,3},{1,2},{2,1},{3,0},{4,7},{5,6},{6,5},{7,4},{8,11},{9,10},{10,... | collective-permute-start | bytes 983048 | tf_op jit(solution)/shard_map/ppermute | solution.py:31
  98.9 1.4 collective-permute-start.23
  100.6 2.5 %collective-permute-start.33 = (f32[2,160,256]{2,1,0:T(8,128)S(1)}, f32[2,160,256]{2,1,0:T(8,128)S(1)}, u32[]{:S(2)}, u32[]{:S(2)}) collective-permute-start(f32[2,160,256]{2,1,0:T(8,128)S(1)} %pad_maximum_fusion.14), channel_id=1, source_target_pairs={{0,32},{32,0},{64,96},{96,64},{1,33},{33,1},{65,97},{97,65},{2,34}... | collective-permute-start | bytes 983048 | tf_op jit(solution)/shard_map/ppermute | solution.py:31
  103.9 2.3 %collective-permute-start.34 = (f32[2,160,256]{2,1,0:T(8,128)S(1)}, f32[2,160,256]{2,1,0:T(8,128)S(1)}, u32[]{:S(2)}, u32[]{:S(2)}) collective-permute-start(f32[2,160,256]{2,1,0:T(8,128)S(1)} %pad_maximum_fusion.14), channel_id=1, source_target_pairs={{0,96},{32,64},{64,32},{96,0},{1,97},{33,65},{65,33},{97,1},{2,98}... | collective-permute-start | bytes 983048 | tf_op jit(solution)/shard_map/ppermute | solution.py:31
  106.2 3.2 %collective-permute-done.22 = f32[2,160,256]{2,1,0:T(8,128)S(1)} collective-permute-done((f32[2,160,256]{2,1,0:T(8,128)S(1)}, f32[2,160,256]{2,1,0:T(8,128)S(1)}, u32[]{:S(2)}, u32[]{:S(2)}) %collective-permute-start.22) | collective-permute-done | bytes 327712 | tf_op jit(solution)/shard_map/ppermute | solution.py:31
  109.4 1.8 %collective-permute-done.23 = f32[2,160,256]{2,1,0:T(8,128)S(1)} collective-permute-done((f32[2,160,256]{2,1,0:T(8,128)S(1)}, f32[2,160,256]{2,1,0:T(8,128)S(1)}, u32[]{:S(2)}, u32[]{:S(2)}) %collective-permute-start.23) | collective-permute-done | bytes 327712 | tf_op jit(solution)/shard_map/ppermute | solution.py:31
  111.5 1.9 %fusion.35 = f32[1280,512]{1,0:T(8,128)S(1)} fusion(bf16[1280,1280]{1,0:T(8,128)(2,1)S(1)} %get-tuple-element.5, bf16[1280,256]{1,0:T(8,128)(2,1)S(1)} %get-tuple-element.12, bf16[1280,256]{1,0:T(8,128)(2,1)S(1)} %get-tuple-element.13), kind=kOutput, calls=%fused_computation.74 | convolution fusion | flops 1680343040 | bytes 7208960 | tf_op jit(solution)/shard_map/dot_general | solution.py:93
  113.4 1.9 %fusion.36 = f32[1280,512]{1,0:T(8,128)S(1)} fusion(bf16[1280,1280]{1,0:T(8,128)(2,1)S(1)} %get-tuple-element.8, bf16[1280,256]{1,0:T(8,128)(2,1)S(1)} %get-tuple-element.12, bf16[1280,256]{1,0:T(8,128)(2,1)S(1)} %get-tuple-element.13), kind=kOutput, calls=%fused_computation.75 | convolution fusion | flops 1680343040 | bytes 7208960 | tf_op jit(solution)/shard_map/dot_general | solution.py:93
  117.3 1.9 %fusion.20 = f32[1280,512]{1,0:T(8,128)S(1)} fusion(bf16[1280,1280]{1,0:T(8,128)(2,1)S(1)} %get-tuple-element.8, bf16[1280,256]{1,0:T(8,128)(2,1)S(1)} %get-tuple-element.19, bf16[1280,256]{1,0:T(8,128)(2,1)S(1)} %get-tuple-element.20), kind=kOutput, calls=%fused_computation.56 | convolution fusion | flops 1680343040 | bytes 7208960 | tf_op jit(solution)/shard_map/dot_general | solution.py:93
  120.3 1.1 fusion.4
  122.9 3.4 %collective-permute-start.25 = (f32[2,160,256]{2,1,0:T(8,128)S(1)}, f32[2,160,256]{2,1,0:T(8,128)S(1)}, u32[]{:S(2)}, u32[]{:S(2)}) collective-permute-start(f32[2,160,256]{2,1,0:T(8,128)S(1)} %get-tuple-element.9), channel_id=1, source_target_pairs={{0,64},{32,96},{64,0},{96,32},{1,65},{33,97},{65,1},{97,33},{2,66}... | collective-permute-start | bytes 983048 | tf_op jit(solution)/shard_map/ppermute | solution.py:31
  126.5 1.9 %fusion.24 = f32[1280,512]{1,0:T(8,128)S(1)} fusion(bf16[1280,1280]{1,0:T(8,128)(2,1)S(1)} %get-tuple-element.5, bf16[1280,256]{1,0:T(8,128)(2,1)S(1)} %get-tuple-element.17, bf16[1280,256]{1,0:T(8,128)(2,1)S(1)} %get-tuple-element.18), kind=kOutput, calls=%fused_computation.60 | convolution fusion | flops 1680343040 | bytes 7208960 | tf_op jit(solution)/shard_map/dot_general | solution.py:93
  129.6 1.9 %collective-permute-start.38 = (f32[2,160,256]{2,1,0:T(8,128)S(1)}, f32[2,160,256]{2,1,0:T(8,128)S(1)}, u32[]{:S(2)}, u32[]{:S(2)}) collective-permute-start(f32[2,160,256]{2,1,0:T(8,128)S(1)} %get-tuple-element.15), channel_id=1, source_target_pairs={{0,3},{1,2},{2,1},{3,0},{4,7},{5,6},{6,5},{7,4},{8,11},{9,10},{10,... | collective-permute-start | bytes 983048 | tf_op jit(solution)/shard_map/ppermute | solution.py:31
  132.5 1.9 %collective-permute-start.36 = (f32[2,160,256]{2,1,0:T(8,128)S(1)}, f32[2,160,256]{2,1,0:T(8,128)S(1)}, u32[]{:S(2)}, u32[]{:S(2)}) collective-permute-start(f32[2,160,256]{2,1,0:T(8,128)S(1)} %get-tuple-element.14), channel_id=1, source_target_pairs={{0,2},{1,3},{2,0},{3,1},{4,6},{5,7},{6,4},{7,5},{8,10},{9,11},{10,... | collective-permute-start | bytes 983048 | tf_op jit(solution)/shard_map/ppermute | solution.py:31
  134.4 6.3 %collective-permute-done.25 = f32[2,160,256]{2,1,0:T(8,128)S(1)} collective-permute-done((f32[2,160,256]{2,1,0:T(8,128)S(1)}, f32[2,160,256]{2,1,0:T(8,128)S(1)}, u32[]{:S(2)}, u32[]{:S(2)}) %collective-permute-start.25) | collective-permute-done | bytes 327712 | tf_op jit(solution)/shard_map/ppermute | solution.py:31
  141.5 3.5 %collective-permute-start.29 = (f32[160,256]{1,0:T(8,128)S(1)}, f32[160,256]{1,0:T(8,128)S(1)}, u32[]{:S(2)}, u32[]{:S(2)}) collective-permute-start(f32[160,256]{1,0:T(8,128)S(1)} %get-tuple-element.39), channel_id=1, source_target_pairs={{16,0},{80,1},{48,2},{112,3},{0,4},{64,5},{32,6},{96,7},{24,8},{88... | collective-permute-start | bytes 491528 | tf_op jit(solution)/shard_map/ppermute | solution.py:84
  145.0 6.5 %collective-permute-done.36 = f32[2,160,256]{2,1,0:T(8,128)S(1)} collective-permute-done((f32[2,160,256]{2,1,0:T(8,128)S(1)}, f32[2,160,256]{2,1,0:T(8,128)S(1)}, u32[]{:S(2)}, u32[]{:S(2)}) %collective-permute-start.36) | collective-permute-done | bytes 327712 | tf_op jit(solution)/shard_map/ppermute | solution.py:31
  152.1 4.9 %collective-permute-done.39 = f32[160,256]{1,0:T(8,128)S(1)} collective-permute-done((f32[160,256]{1,0:T(8,128)S(1)}, f32[160,256]{1,0:T(8,128)S(1)}, u32[]{:S(2)}, u32[]{:S(2)}) %collective-permute-start.39) | collective-permute-done | bytes 163872 | tf_op jit(solution)/shard_map/ppermute | solution.py:31
  (112 shorter events, 20.5 us)
Async XLA Ops:
  0.0 12.5 %collective-permute-start.10 = (f32[160,256]{1,0:T(8,128)}, f32[160,256]{1,0:T(8,128)S(1)}, u32[]{:S(2)}, u32[]{:S(2)}) collective-permute-start(f32[160,256]{1,0:T(8,128)} %param.5), channel_id=1, source_target_pairs={{0,0},{1,64},{2,32},{3,96},{4,16},{5,80},{6,48},{7,112},{8,8},{9,7... | collective-permute-start | bytes 491528 | tf_op jit(solution)/shard_map/ppermute | solution.py:84
  1.6 13.7 %collective-permute-start = (f32[160,256]{1,0:T(8,128)}, f32[160,256]{1,0:T(8,128)S(1)}, u32[]{:S(2)}, u32[]{:S(2)}) collective-permute-start(f32[160,256]{1,0:T(8,128)} %param.5), channel_id=1, source_target_pairs={{0,4},{4,0},{1,5},{5,1},{2,6},{6,2},{3,7},{7,3},{8,12},{12,8},{9,1... | collective-permute-start | bytes 491528 | tf_op jit(solution)/shard_map/ppermute | solution.py:31
  6.6 5.9 %copy-start.1 = (f32[2,256]{1,0:T(2,128)S(1)}, f32[2,256]{1,0:T(2,128)}, u32[]{:S(2)}) copy-start(f32[2,256]{1,0:T(2,128)} %param.7) | copy-start | bytes 6148
  6.6 8.7 %copy-start = (f32[160,256]{1,0:T(8,128)S(1)}, f32[160,256]{1,0:T(8,128)}, u32[]{:S(2)}) copy-start(f32[160,256]{1,0:T(8,128)} %param.5) | copy-start | bytes 491524
  12.5 10.7 %collective-permute-start.11 = (f32[160,256]{1,0:T(8,128)S(1)}, f32[160,256]{1,0:T(8,128)S(1)}, u32[]{:S(2)}, u32[]{:S(2)}) collective-permute-start(f32[160,256]{1,0:T(8,128)S(1)} %collective-permute-done.10), channel_id=1, source_target_pairs={{0,16},{16,0},{1,17},{17,1},{2,18},{18,2},{3,19},{19,3},{4,20},{20... | collective-permute-start | bytes 491528 | tf_op jit(solution)/shard_map/ppermute | solution.py:31
  15.4 12.5 %collective-permute-start.1 = (f32[2,160,256]{2,1,0:T(8,128)S(1)}, f32[2,160,256]{2,1,0:T(8,128)S(1)}, u32[]{:S(2)}, u32[]{:S(2)}) collective-permute-start(f32[2,160,256]{2,1,0:T(8,128)S(1)} %pad_maximum_fusion.9), channel_id=1, source_target_pairs={{0,1},{1,0},{2,3},{3,2},{4,5},{5,4},{6,7},{7,6},{8,9},{9,8},{10,11... | collective-permute-start | bytes 983048 | tf_op jit(solution)/shard_map/ppermute | solution.py:31
  19.3 15.5 %collective-permute-start.2 = (f32[2,160,256]{2,1,0:T(8,128)S(1)}, f32[2,160,256]{2,1,0:T(8,128)S(1)}, u32[]{:S(2)}, u32[]{:S(2)}) collective-permute-start(f32[2,160,256]{2,1,0:T(8,128)S(1)} %pad_maximum_fusion.9), channel_id=1, source_target_pairs={{0,3},{1,2},{2,1},{3,0},{4,7},{5,6},{6,5},{7,4},{8,11},{9,10},{10,... | collective-permute-start | bytes 983048 | tf_op jit(solution)/shard_map/ppermute | solution.py:31
  21.7 15.0 %collective-permute-start.3 = (f32[2,160,256]{2,1,0:T(8,128)S(1)}, f32[2,160,256]{2,1,0:T(8,128)S(1)}, u32[]{:S(2)}, u32[]{:S(2)}) collective-permute-start(f32[2,160,256]{2,1,0:T(8,128)S(1)} %pad_maximum_fusion.9), channel_id=1, source_target_pairs={{0,2},{1,3},{2,0},{3,1},{4,6},{5,7},{6,4},{7,5},{8,10},{9,11},{10,... | collective-permute-start | bytes 983048 | tf_op jit(solution)/shard_map/ppermute | solution.py:31
  23.3 18.5 %collective-permute-start.12 = (f32[2,160,256]{2,1,0:T(8,128)S(1)}, f32[2,160,256]{2,1,0:T(8,128)S(1)}, u32[]{:S(2)}, u32[]{:S(2)}) collective-permute-start(f32[2,160,256]{2,1,0:T(8,128)S(1)} %pad_maximum_fusion.10), channel_id=1, source_target_pairs={{0,64},{32,96},{64,0},{96,32},{1,65},{33,97},{65,1},{97,33},{2,66}... | collective-permute-start | bytes 983048 | tf_op jit(solution)/shard_map/ppermute | solution.py:31
  26.0 15.9 %collective-permute-start.13 = (f32[2,160,256]{2,1,0:T(8,128)S(1)}, f32[2,160,256]{2,1,0:T(8,128)S(1)}, u32[]{:S(2)}, u32[]{:S(2)}) collective-permute-start(f32[2,160,256]{2,1,0:T(8,128)S(1)} %pad_maximum_fusion.10), channel_id=1, source_target_pairs={{0,32},{32,0},{64,96},{96,64},{1,33},{33,1},{65,97},{97,65},{2,34}... | collective-permute-start | bytes 983048 | tf_op jit(solution)/shard_map/ppermute | solution.py:31
  27.9 14.0 %collective-permute-start.14 = (f32[2,160,256]{2,1,0:T(8,128)S(1)}, f32[2,160,256]{2,1,0:T(8,128)S(1)}, u32[]{:S(2)}, u32[]{:S(2)}) collective-permute-start(f32[2,160,256]{2,1,0:T(8,128)S(1)} %pad_maximum_fusion.10), channel_id=1, source_target_pairs={{0,96},{32,64},{64,32},{96,0},{1,97},{33,65},{65,33},{97,1},{2,98}... | collective-permute-start | bytes 983048 | tf_op jit(solution)/shard_map/ppermute | solution.py:31
  39.8 6.1 %collective-permute-start.4 = (f32[1280,256]{1,0:T(8,128)S(1)}, f32[1280,256]{1,0:T(8,128)S(1)}, u32[]{:S(2)}, u32[]{:S(2)}) collective-permute-start(f32[1280,256]{1,0:T(8,128)S(1)} %convolution_add_fusion.6), channel_id=1, source_target_pairs={{0,8},{8,0},{1,9},{9,1},{2,10},{10,2},{3,11},{11,3},{4,12},{12,4},... | collective-permute-start | bytes 3932168 | tf_op jit(solution)/shard_map/ppermute | solution.py:75
  41.9 10.0 %collective-permute-start.15 = (f32[1280,256]{1,0:T(8,128)S(1)}, f32[1280,256]{1,0:T(8,128)S(1)}, u32[]{:S(2)}, u32[]{:S(2)}) collective-permute-start(f32[1280,256]{1,0:T(8,128)S(1)} %bitcast.205), channel_id=1, source_target_pairs={{0,8},{8,0},{1,9},{9,1},{2,10},{10,2},{3,11},{11,3},{4,12},{12,4},... | collective-permute-start | bytes 3932168 | tf_op jit(solution)/shard_map/ppermute | solution.py:75
  47.1 11.0 %collective-permute-start.7 = (f32[2,160,256]{2,1,0:T(8,128)S(1)}, f32[2,160,256]{2,1,0:T(8,128)S(1)}, u32[]{:S(2)}, u32[]{:S(2)}) collective-permute-start(f32[2,160,256]{2,1,0:T(8,128)S(1)} %get-tuple-element.22), channel_id=1, source_target_pairs={{0,96},{32,64},{64,32},{96,0},{1,97},{33,65},{65,33},{97,1},{2,98}... | collective-permute-start | bytes 983048 | tf_op jit(solution)/shard_map/ppermute | solution.py:31
  49.9 10.6 %collective-permute-start.6 = (f32[2,160,256]{2,1,0:T(8,128)S(1)}, f32[2,160,256]{2,1,0:T(8,128)S(1)}, u32[]{:S(2)}, u32[]{:S(2)}) collective-permute-start(f32[2,160,256]{2,1,0:T(8,128)S(1)} %get-tuple-element.23), channel_id=1, source_target_pairs={{0,32},{32,0},{64,96},{96,64},{1,33},{33,1},{65,97},{97,65},{2,34}... | collective-permute-start | bytes 983048 | tf_op jit(solution)/shard_map/ppermute | solution.py:31
  49.9 16.4 %collective-permute-start.5 = (f32[2,160,256]{2,1,0:T(8,128)S(1)}, f32[2,160,256]{2,1,0:T(8,128)S(1)}, u32[]{:S(2)}, u32[]{:S(2)}) collective-permute-start(f32[2,160,256]{2,1,0:T(8,128)S(1)} %get-tuple-element.21), channel_id=1, source_target_pairs={{0,64},{32,96},{64,0},{96,32},{1,65},{33,97},{65,1},{97,33},{2,66}... | collective-permute-start | bytes 983048 | tf_op jit(solution)/shard_map/ppermute | solution.py:31
  55.2 12.3 %collective-permute-start.18 = (f32[2,160,256]{2,1,0:T(8,128)S(1)}, f32[2,160,256]{2,1,0:T(8,128)S(1)}, u32[]{:S(2)}, u32[]{:S(2)}) collective-permute-start(f32[2,160,256]{2,1,0:T(8,128)S(1)} %get-tuple-element.27), channel_id=1, source_target_pairs={{0,3},{1,2},{2,1},{3,0},{4,7},{5,6},{6,5},{7,4},{8,11},{9,10},{10,... | collective-permute-start | bytes 983048 | tf_op jit(solution)/shard_map/ppermute | solution.py:31
  57.2 10.6 %collective-permute-start.17 = (f32[2,160,256]{2,1,0:T(8,128)S(1)}, f32[2,160,256]{2,1,0:T(8,128)S(1)}, u32[]{:S(2)}, u32[]{:S(2)}) collective-permute-start(f32[2,160,256]{2,1,0:T(8,128)S(1)} %get-tuple-element.28), channel_id=1, source_target_pairs={{0,1},{1,0},{2,3},{3,2},{4,5},{5,4},{6,7},{7,6},{8,9},{9,8},{10,11... | collective-permute-start | bytes 983048 | tf_op jit(solution)/shard_map/ppermute | solution.py:31
  58.1 15.4 %collective-permute-start.16 = (f32[2,160,256]{2,1,0:T(8,128)S(1)}, f32[2,160,256]{2,1,0:T(8,128)S(1)}, u32[]{:S(2)}, u32[]{:S(2)}) collective-permute-start(f32[2,160,256]{2,1,0:T(8,128)S(1)} %get-tuple-element.26), channel_id=1, source_target_pairs={{0,2},{1,3},{2,0},{3,1},{4,6},{5,7},{6,4},{7,5},{8,10},{9,11},{10,... | collective-permute-start | bytes 983048 | tf_op jit(solution)/shard_map/ppermute | solution.py:31
  66.4 7.8 %collective-permute-start.8 = (f32[160,256]{1,0:T(8,128)S(1)}, f32[160,256]{1,0:T(8,128)S(1)}, u32[]{:S(2)}, u32[]{:S(2)}) collective-permute-start(f32[160,256]{1,0:T(8,128)S(1)} %select_bitcast_fusion.10), channel_id=1, source_target_pairs={{0,16},{16,0},{1,17},{17,1},{2,18},{18,2},{3,19},{19,3},{4,20},{20... | collective-permute-start | bytes 491528 | tf_op jit(solution)/shard_map/ppermute | solution.py:31
  73.6 5.6 %collective-permute-start.19 = (f32[160,256]{1,0:T(8,128)S(1)}, f32[160,256]{1,0:T(8,128)S(1)}, u32[]{:S(2)}, u32[]{:S(2)}) collective-permute-start(f32[160,256]{1,0:T(8,128)S(1)} %select_bitcast_fusion.7), channel_id=1, source_target_pairs={{0,4},{4,0},{1,5},{5,1},{2,6},{6,2},{3,7},{7,3},{8,12},{12,8},{9,1... | collective-permute-start | bytes 491528 | tf_op jit(solution)/shard_map/ppermute | solution.py:31
  74.3 5.7 %collective-permute-start.9 = (f32[160,256]{1,0:T(8,128)S(1)}, f32[160,256]{1,0:T(8,128)S(1)}, u32[]{:S(2)}, u32[]{:S(2)}) collective-permute-start(f32[160,256]{1,0:T(8,128)S(1)} %bitcast_add_fusion.6), channel_id=1, source_target_pairs={{0,0},{64,1},{32,2},{96,3},{16,4},{80,5},{48,6},{112,7},{8,8},{72,... | collective-permute-start | bytes 491528 | tf_op jit(solution)/shard_map/ppermute | solution.py:84
  79.2 7.4 %collective-permute-start.30 = (f32[160,256]{1,0:T(8,128)S(1)}, f32[160,256]{1,0:T(8,128)S(1)}, u32[]{:S(2)}, u32[]{:S(2)}) collective-permute-start(f32[160,256]{1,0:T(8,128)S(1)} %bitcast_add_fusion.5), channel_id=1, source_target_pairs={{0,0},{1,64},{2,32},{3,96},{4,16},{5,80},{6,48},{7,112},{8,8},{9,7... | collective-permute-start | bytes 491528 | tf_op jit(solution)/shard_map/ppermute | solution.py:84
  80.4 9.9 %collective-permute-start.20 = (f32[160,256]{1,0:T(8,128)S(1)}, f32[160,256]{1,0:T(8,128)S(1)}, u32[]{:S(2)}, u32[]{:S(2)}) collective-permute-start(f32[160,256]{1,0:T(8,128)S(1)} %fusion.33), channel_id=1, source_target_pairs={{0,4},{4,0},{1,5},{5,1},{2,6},{6,2},{3,7},{7,3},{8,12},{12,8},{9,1... | collective-permute-start | bytes 491528 | tf_op jit(solution)/shard_map/ppermute | solution.py:31
  87.2 13.3 %collective-permute-start.31 = (f32[160,256]{1,0:T(8,128)S(1)}, f32[160,256]{1,0:T(8,128)S(1)}, u32[]{:S(2)}, u32[]{:S(2)}) collective-permute-start(f32[160,256]{1,0:T(8,128)S(1)} %fusion.31), channel_id=1, source_target_pairs={{0,16},{16,0},{1,17},{17,1},{2,18},{18,2},{3,19},{19,3},{4,20},{20... | collective-permute-start | bytes 491528 | tf_op jit(solution)/shard_map/ppermute | solution.py:31
  90.4 13.5 %collective-permute-start.21 = (f32[2,160,256]{2,1,0:T(8,128)S(1)}, f32[2,160,256]{2,1,0:T(8,128)S(1)}, u32[]{:S(2)}, u32[]{:S(2)}) collective-permute-start(f32[2,160,256]{2,1,0:T(8,128)S(1)} %pad_maximum_fusion.12), channel_id=1, source_target_pairs={{0,1},{1,0},{2,3},{3,2},{4,5},{5,4},{6,7},{7,6},{8,9},{9,8},{10,11... | collective-permute-start | bytes 983048 | tf_op jit(solution)/shard_map/ppermute | solution.py:31
  95.5 13.9 %collective-permute-start.22 = (f32[2,160,256]{2,1,0:T(8,128)S(1)}, f32[2,160,256]{2,1,0:T(8,128)S(1)}, u32[]{:S(2)}, u32[]{:S(2)}) collective-permute-start(f32[2,160,256]{2,1,0:T(8,128)S(1)} %pad_maximum_fusion.12), channel_id=1, source_target_pairs={{0,3},{1,2},{2,1},{3,0},{4,7},{5,6},{6,5},{7,4},{8,11},{9,10},{10,... | collective-permute-start | bytes 983048 | tf_op jit(solution)/shard_map/ppermute | solution.py:31
  98.9 12.3 %collective-permute-start.23 = (f32[2,160,256]{2,1,0:T(8,128)S(1)}, f32[2,160,256]{2,1,0:T(8,128)S(1)}, u32[]{:S(2)}, u32[]{:S(2)}) collective-permute-start(f32[2,160,256]{2,1,0:T(8,128)S(1)} %pad_maximum_fusion.12), channel_id=1, source_target_pairs={{0,2},{1,3},{2,0},{3,1},{4,6},{5,7},{6,4},{7,5},{8,10},{9,11},{10,... | collective-permute-start | bytes 983048 | tf_op jit(solution)/shard_map/ppermute | solution.py:31
  100.5 15.9 %collective-permute-start.32 = (f32[2,160,256]{2,1,0:T(8,128)S(1)}, f32[2,160,256]{2,1,0:T(8,128)S(1)}, u32[]{:S(2)}, u32[]{:S(2)}) collective-permute-start(f32[2,160,256]{2,1,0:T(8,128)S(1)} %pad_maximum_fusion.14), channel_id=1, source_target_pairs={{0,64},{32,96},{64,0},{96,32},{1,65},{33,97},{65,1},{97,33},{2,66}... | collective-permute-start | bytes 983048 | tf_op jit(solution)/shard_map/ppermute | solution.py:31
  100.6 15.8 %collective-permute-start.33 = (f32[2,160,256]{2,1,0:T(8,128)S(1)}, f32[2,160,256]{2,1,0:T(8,128)S(1)}, u32[]{:S(2)}, u32[]{:S(2)}) collective-permute-start(f32[2,160,256]{2,1,0:T(8,128)S(1)} %pad_maximum_fusion.14), channel_id=1, source_target_pairs={{0,32},{32,0},{64,96},{96,64},{1,33},{33,1},{65,97},{97,65},{2,34}... | collective-permute-start | bytes 983048 | tf_op jit(solution)/shard_map/ppermute | solution.py:31
  103.9 12.6 %collective-permute-start.34 = (f32[2,160,256]{2,1,0:T(8,128)S(1)}, f32[2,160,256]{2,1,0:T(8,128)S(1)}, u32[]{:S(2)}, u32[]{:S(2)}) collective-permute-start(f32[2,160,256]{2,1,0:T(8,128)S(1)} %pad_maximum_fusion.14), channel_id=1, source_target_pairs={{0,96},{32,64},{64,32},{96,0},{1,97},{33,65},{65,33},{97,1},{2,98}... | collective-permute-start | bytes 983048 | tf_op jit(solution)/shard_map/ppermute | solution.py:31
  116.3 4.0 %collective-permute-start.24 = (f32[1280,256]{1,0:T(8,128)S(1)}, f32[1280,256]{1,0:T(8,128)S(1)}, u32[]{:S(2)}, u32[]{:S(2)}) collective-permute-start(f32[1280,256]{1,0:T(8,128)S(1)} %convolution_add_fusion.2), channel_id=1, source_target_pairs={{0,8},{8,0},{1,9},{9,1},{2,10},{10,2},{3,11},{11,3},{4,12},{12,4},... | collective-permute-start | bytes 3932168 | tf_op jit(solution)/shard_map/ppermute | solution.py:75
  116.5 9.8 %collective-permute-start.35 = (f32[1280,256]{1,0:T(8,128)S(1)}, f32[1280,256]{1,0:T(8,128)S(1)}, u32[]{:S(2)}, u32[]{:S(2)}) collective-permute-start(f32[1280,256]{1,0:T(8,128)S(1)} %bitcast.204), channel_id=1, source_target_pairs={{0,8},{8,0},{1,9},{9,1},{2,10},{10,2},{3,11},{11,3},{4,12},{12,4},... | collective-permute-start | bytes 3932168 | tf_op jit(solution)/shard_map/ppermute | solution.py:75
  121.5 11.0 %collective-permute-start.27 = (f32[2,160,256]{2,1,0:T(8,128)S(1)}, f32[2,160,256]{2,1,0:T(8,128)S(1)}, u32[]{:S(2)}, u32[]{:S(2)}) collective-permute-start(f32[2,160,256]{2,1,0:T(8,128)S(1)} %get-tuple-element.10), channel_id=1, source_target_pairs={{0,96},{32,64},{64,32},{96,0},{1,97},{33,65},{65,33},{97,1},{2,98}... | collective-permute-start | bytes 983048 | tf_op jit(solution)/shard_map/ppermute | solution.py:31
  122.0 12.4 %collective-permute-start.26 = (f32[2,160,256]{2,1,0:T(8,128)S(1)}, f32[2,160,256]{2,1,0:T(8,128)S(1)}, u32[]{:S(2)}, u32[]{:S(2)}) collective-permute-start(f32[2,160,256]{2,1,0:T(8,128)S(1)} %get-tuple-element.11), channel_id=1, source_target_pairs={{0,32},{32,0},{64,96},{96,64},{1,33},{33,1},{65,97},{97,65},{2,34}... | collective-permute-start | bytes 983048 | tf_op jit(solution)/shard_map/ppermute | solution.py:31
  122.9 17.8 %collective-permute-start.25 = (f32[2,160,256]{2,1,0:T(8,128)S(1)}, f32[2,160,256]{2,1,0:T(8,128)S(1)}, u32[]{:S(2)}, u32[]{:S(2)}) collective-permute-start(f32[2,160,256]{2,1,0:T(8,128)S(1)} %get-tuple-element.9), channel_id=1, source_target_pairs={{0,64},{32,96},{64,0},{96,32},{1,65},{33,97},{65,1},{97,33},{2,66}... | collective-permute-start | bytes 983048 | tf_op jit(solution)/shard_map/ppermute | solution.py:31
  129.6 15.4 %collective-permute-start.38 = (f32[2,160,256]{2,1,0:T(8,128)S(1)}, f32[2,160,256]{2,1,0:T(8,128)S(1)}, u32[]{:S(2)}, u32[]{:S(2)}) collective-permute-start(f32[2,160,256]{2,1,0:T(8,128)S(1)} %get-tuple-element.15), channel_id=1, source_target_pairs={{0,3},{1,2},{2,1},{3,0},{4,7},{5,6},{6,5},{7,4},{8,11},{9,10},{10,... | collective-permute-start | bytes 983048 | tf_op jit(solution)/shard_map/ppermute | solution.py:31
  131.5 13.4 %collective-permute-start.37 = (f32[2,160,256]{2,1,0:T(8,128)S(1)}, f32[2,160,256]{2,1,0:T(8,128)S(1)}, u32[]{:S(2)}, u32[]{:S(2)}) collective-permute-start(f32[2,160,256]{2,1,0:T(8,128)S(1)} %get-tuple-element.16), channel_id=1, source_target_pairs={{0,1},{1,0},{2,3},{3,2},{4,5},{5,4},{6,7},{7,6},{8,9},{9,8},{10,11... | collective-permute-start | bytes 983048 | tf_op jit(solution)/shard_map/ppermute | solution.py:31
  132.5 19.0 %collective-permute-start.36 = (f32[2,160,256]{2,1,0:T(8,128)S(1)}, f32[2,160,256]{2,1,0:T(8,128)S(1)}, u32[]{:S(2)}, u32[]{:S(2)}) collective-permute-start(f32[2,160,256]{2,1,0:T(8,128)S(1)} %get-tuple-element.14), channel_id=1, source_target_pairs={{0,2},{1,3},{2,0},{3,1},{4,6},{5,7},{6,4},{7,5},{8,10},{9,11},{10,... | collective-permute-start | bytes 983048 | tf_op jit(solution)/shard_map/ppermute | solution.py:31
  140.8 11.3 %collective-permute-start.28 = (f32[160,256]{1,0:T(8,128)S(1)}, f32[160,256]{1,0:T(8,128)S(1)}, u32[]{:S(2)}, u32[]{:S(2)}) collective-permute-start(f32[160,256]{1,0:T(8,128)S(1)} %get-tuple-element.40), channel_id=1, source_target_pairs={{0,0},{64,1},{32,2},{96,3},{16,4},{80,5},{48,6},{112,7},{8,8},{72,... | collective-permute-start | bytes 491528 | tf_op jit(solution)/shard_map/ppermute | solution.py:84
  141.5 10.6 %collective-permute-start.29 = (f32[160,256]{1,0:T(8,128)S(1)}, f32[160,256]{1,0:T(8,128)S(1)}, u32[]{:S(2)}, u32[]{:S(2)}) collective-permute-start(f32[160,256]{1,0:T(8,128)S(1)} %get-tuple-element.39), channel_id=1, source_target_pairs={{16,0},{80,1},{48,2},{112,3},{0,4},{64,5},{32,6},{96,7},{24,8},{88... | collective-permute-start | bytes 491528 | tf_op jit(solution)/shard_map/ppermute | solution.py:84
  151.6 5.4 %collective-permute-start.39 = (f32[160,256]{1,0:T(8,128)S(1)}, f32[160,256]{1,0:T(8,128)S(1)}, u32[]{:S(2)}, u32[]{:S(2)}) collective-permute-start(f32[160,256]{1,0:T(8,128)S(1)} %select_bitcast_fusion), channel_id=1, source_target_pairs={{0,4},{4,0},{1,5},{5,1},{2,6},{6,2},{3,7},{7,3},{8,12},{12,8},{9,1... | collective-permute-start | bytes 491528 | tf_op jit(solution)/shard_map/ppermute | solution.py:31
